TPU v7x, 256 devices: a whole 4x4x8 slice. The times are simulated.
256 devices in a mesh: gx: 8 (over y, core), pa: 32 (over x, z).
Axes of the slice: x: 4, y: 4, z: 8, core: 2. Of those that a mesh axis runs over, the one named last changes fastest.
Arguments:
- u_factor: float32 [64, 65536], P(None, 'gx'), may hold values from -160 to 160, as said below
- v_factor: float32 [64, 262144], P(None, 'pa'), may hold values from -160 to 160, as said below
- mass_table: float32 [4, 16], replicated, may hold values from -2 to 2
- diffusivity_table: float32 [4, 16], replicated, may hold values from 0.2 to 1
- material_index: int32 [4, 65536], P(None, 'gx'), may hold values from 0 to 15
- band_weights: float32 [4, 3, 262144], P(None, None, 'pa'), may hold values from -5 to 5
- band_offsets: int32 [4, 3], replicated, may hold values from -4 to 4, as said below
- core_matrix: float32 [64, 64], replicated, may hold values from -4 to 4
- sketch_seed: int32 [1], replicated, may hold values from 0 to 65520
Outputs:
- u_next: float32 [64, 65536], P(None, 'gx')
- v_next: float32 [64, 262144], P(None, 'pa')
- core_next: float32 [64, 64], replicated
Inputs may be any that keep to these rules, and one draw needn't show every extreme that they name: `u_factor`: each factor is finite and its rows are of mixed scales. `v_factor`: each factor is finite and its rows are of mixed scales. `band_offsets`: some tap reaches each end of the band.
All inputs are finite; a program needn't handle non-finite values.
Results may differ from a plain program's by a relative error of at most 0.0003.
Values sent between devices are 32-bit elements; how exact they have to be, the bound alone decides.
No kernel may reach another device: no remote copies, remote signals or barrier semaphores. Data moves between devices by JAX's collectives and lax.ppermute only.
A program may use at most 128 MiB of HBM per device.

v0:
```python
import functools

import jax
import jax.numpy as jnp
from jax import lax
from jax.experimental import pallas as pl
from jax.experimental.pallas import tpu as pltpu
from jax.sharding import PartitionSpec as P

BAND = 4
LANES = 128
RANK = 64
STENCILS = 4
TAPS = 3
WIDE = 256
F32 = jnp.float32
BF16 = jnp.bfloat16
NT = (((1,), (1,)), ((), ()))
NN = (((1,), (0,)), ((), ()))
VMEM_LIMIT = 56 * 1024 * 1024


def smem():
    return pl.BlockSpec(memory_space=pltpu.SMEM)


def vmem():
    return pl.BlockSpec(memory_space=pltpu.VMEM)


def split(x):
    hi = x.astype(BF16)
    lo = (x - hi.astype(F32)).astype(BF16)
    return hi, lo


def fast_dot(a, b, dims):
    return lax.dot_general(a, b, dims, preferred_element_type=F32)


def full_dot(a, b, dims=NN):
    return lax.dot_general(a, b, dims, precision=lax.Precision.HIGHEST, preferred_element_type=F32)


def lane_iota(shape):
    return lax.broadcasted_iota(jnp.int32, shape, len(shape) - 1)


def shift_left(here, after, by):
    mask = lane_iota(here.shape) < LANES - by
    return jnp.where(mask, pltpu.roll(here, LANES - by, 1), pltpu.roll(after, LANES - by, 1))


def shift_right(before, here, by):
    mask = lane_iota(here.shape) >= by
    return jnp.where(mask, pltpu.roll(here, by, 1), pltpu.roll(before, by, 1))


def pack_gram(gram_ref, rows):
    rows[0:128, :] = gram_ref[0:128, 0:128]
    rows[128:256, :] = gram_ref[128:256, 0:128]
    rows[256:384, :] = gram_ref[128:256, 128:256]


def finish_gram(hh_ref, hl_ref, pack_ref, scale, core, mine_ref, other_ref):
    for row, col, at in ((0, 0, 0), (128, 0, 128), (128, 128, 256)):
        part = hl_ref[row:row + 128, col:col + 128] + hl_ref[col:col + 128, row:row + 128].T
        pack_ref[at:at + 128, :] = (hh_ref[row:row + 128, col:col + 128] + part) * scale
    half = 192
    mine_ref[...] = pack_ref[pl.ds(pl.multiple_of(core * half, half), half), :]
    other_ref[...] = pack_ref[pl.ds(pl.multiple_of((1 - core) * half, half), half), :]


def add_gram(hi_ref, lo_ref, hh_ref, hl_ref, first):
    hi = hi_ref[...]
    hh = fast_dot(hi, hi, NT)
    hl = fast_dot(hi, lo_ref[...], NT)

    @pl.when(first)
    def _():
        hh_ref[...] = hh
        hl_ref[...] = hl

    @pl.when(jnp.logical_not(first))
    def _():
        hh_ref[...] += hh
        hl_ref[...] += hl


def gram_scratch(tile):
    return [
        pltpu.VMEM((WIDE, tile), BF16),
        pltpu.VMEM((WIDE, tile), BF16),
        pltpu.VMEM((WIDE, WIDE), F32),
        pltpu.VMEM((WIDE, WIDE), F32),
        pltpu.VMEM((384, LANES), F32),
    ]


def gram_v_kernel(steps, scale, core_ref, off_ref, v_ref, before_ref, after_ref, halo_ref, w_ref, mine_ref, other_ref,
                  moved, hi_ref, lo_ref, hh_ref, hl_ref, pack_ref):
    step = pl.program_id(0)
    core = core_ref[0]
    tile = v_ref.shape[1]
    chunks = tile // LANES
    at_left = jnp.logical_and(step == 0, core == 0)
    at_right = jnp.logical_and(step == steps - 1, core == 1)
    before = jnp.where(at_left, halo_ref[...], before_ref[...])
    after = jnp.where(at_right, halo_ref[...], after_ref[...])
    cells = [before] + [v_ref[:, c * LANES:(c + 1) * LANES] for c in range(chunks)] + [after]
    for c in range(chunks):
        lanes = slice(c * LANES, (c + 1) * LANES)
        for by in range(1, BAND + 1):
            moved[BAND + by, :, lanes] = shift_left(cells[c + 1], cells[c + 2], by)
            moved[BAND - by, :, lanes] = shift_right(cells[c], cells[c + 1], by)
        moved[BAND, :, lanes] = cells[c + 1]
    for k in range(STENCILS):
        rows = slice(k * RANK, (k + 1) * RANK)
        for c in range(chunks):
            lanes = slice(c * LANES, (c + 1) * LANES)
            total = w_ref[k, 0:1, lanes] * moved[off_ref[k, 0] + BAND, :, lanes]
            for t in range(1, TAPS):
                total = total + w_ref[k, t:t + 1, lanes] * moved[off_ref[k, t] + BAND, :, lanes]
            hi, lo = split(total)
            hi_ref[rows, lanes] = hi
            lo_ref[rows, lanes] = lo
    add_gram(hi_ref, lo_ref, hh_ref, hl_ref, step == 0)

    @pl.when(step == steps - 1)
    def _():
        finish_gram(hh_ref, hl_ref, pack_ref, scale, core, mine_ref, other_ref)


def gram_v(core, offsets, v, halo, weights, scale):
    cells = v.shape[1]
    half = cells // 2
    tile = min(1024, half)
    steps = half // tile
    ratio = tile // LANES
    last = cells // LANES - 1
    spec = pltpu.PrefetchScalarGridSpec(
        num_scalar_prefetch=2,
        grid=(steps,),
        in_specs=[
            pl.BlockSpec((RANK, tile), lambda i, c, o: (0, c[0] * steps + i)),
            pl.BlockSpec((RANK, LANES), lambda i, c, o: (0, jnp.maximum((c[0] * steps + i) * ratio - 1, 0))),
            pl.BlockSpec((RANK, LANES), lambda i, c, o: (0, jnp.minimum((c[0] * steps + i + 1) * ratio, last))),
            pl.BlockSpec((RANK, LANES), lambda i, c, o: (0, 0)),
            pl.BlockSpec((STENCILS, TAPS, tile), lambda i, c, o: (0, 0, c[0] * steps + i)),
        ],
        out_specs=[pl.BlockSpec((192, LANES), lambda i, c, o: (0, 0))] * 2,
        scratch_shapes=[pltpu.VMEM((2 * BAND + 1, RANK, tile), F32)] + gram_scratch(tile),
    )
    return pl.pallas_call(
        functools.partial(gram_v_kernel, steps, scale),
        grid_spec=spec,
        out_shape=[jax.ShapeDtypeStruct((192, LANES), F32)] * 2,
        compiler_params=pltpu.CompilerParams(vmem_limit_bytes=VMEM_LIMIT),
        name="gram_v",
    )(core, offsets, v, v, v, halo, weights)


def ends(left_ref, before_ref, after_ref, right_ref, step, steps):
    before = jnp.where(step == 0, left_ref[...], before_ref[...])
    after = jnp.where(step == steps - 1, right_ref[...], after_ref[...])
    return before, after


def laplace_chunks(cells):
    out = []
    for c in range(1, len(cells) - 1):
        up = shift_left(cells[c], cells[c + 1], 1)
        down = shift_right(cells[c - 1], cells[c], 1)
        out.append(up - 2.0 * cells[c] + down)
    return out


def gram_u_kernel(steps, scale, core_ref, u_ref, before_ref, after_ref, left_ref, right_ref, m_ref, d_ref, mine_ref, other_ref,
                  hi_ref, lo_ref, hh_ref, hl_ref, pack_ref):
    step = pl.program_id(0)
    chunks = u_ref.shape[1] // LANES
    before, after = ends(left_ref, before_ref, after_ref, right_ref, step, steps)
    cells = [before] + [u_ref[:, c * LANES:(c + 1) * LANES] for c in range(chunks)] + [after]
    laps = laplace_chunks(cells)
    for c in range(chunks):
        lanes = slice(c * LANES, (c + 1) * LANES)
        for k in range(STENCILS):
            rows = slice(k * RANK, (k + 1) * RANK)
            total = m_ref[k:k + 1, lanes] * cells[c + 1] + d_ref[k:k + 1, lanes] * laps[c]
            hi, lo = split(total)
            hi_ref[rows, lanes] = hi
            lo_ref[rows, lanes] = lo
    add_gram(hi_ref, lo_ref, hh_ref, hl_ref, step == 0)

    @pl.when(step == steps - 1)
    def _():
        finish_gram(hh_ref, hl_ref, pack_ref, scale, core_ref[0], mine_ref, other_ref)


def tile_specs(tile, cells):
    ratio = tile // LANES
    last = cells // LANES - 1
    return [
        pl.BlockSpec((RANK, tile), lambda i, *_: (0, i)),
        pl.BlockSpec((RANK, LANES), lambda i, *_: (0, jnp.maximum(i * ratio - 1, 0))),
        pl.BlockSpec((RANK, LANES), lambda i, *_: (0, jnp.minimum((i + 1) * ratio, last))),
        pl.BlockSpec((RANK, LANES), lambda i, *_: (0, 0)),
        pl.BlockSpec((RANK, LANES), lambda i, *_: (0, 0)),
    ]


def gram_u(core, u, left, right, mass, diffusion, scale):
    cells = u.shape[1]
    tile = min(1024, cells)
    steps = cells // tile
    table = pl.BlockSpec((STENCILS, tile), lambda i, *_: (0, i))
    spec = pltpu.PrefetchScalarGridSpec(
        num_scalar_prefetch=1,
        grid=(steps,),
        in_specs=tile_specs(tile, cells) + [table, table],
        out_specs=[pl.BlockSpec((192, LANES), lambda i, *_: (0, 0))] * 2,
        scratch_shapes=gram_scratch(tile),
    )
    return pl.pallas_call(
        functools.partial(gram_u_kernel, steps, scale),
        grid_spec=spec,
        out_shape=[jax.ShapeDtypeStruct((192, LANES), F32)] * 2,
        compiler_params=pltpu.CompilerParams(vmem_limit_bytes=VMEM_LIMIT),
        name="gram_u",
    )(core, u, u, u, left, right, mass, diffusion)


def lower_inverse(square):
    size = RANK
    groups = size // 8
    rows_idx = lax.broadcasted_iota(jnp.int32, (size, size), 0)
    cols_idx = lax.broadcasted_iota(jnp.int32, (size, size), 1)
    unit = jnp.where(rows_idx == cols_idx, 1.0, 0.0).astype(F32)
    both = jnp.concatenate([square, unit], axis=1)
    work = [both[8 * q:8 * q + 8, :] for q in range(groups)]
    shape = (8, 2 * size)
    sub = lax.broadcasted_iota(jnp.int32, shape, 0)
    done = []
    for p in range(groups):
        cols = [[jnp.broadcast_to(work[q][:, 8 * p + j:8 * p + j + 1], shape) for q in range(p, groups)] for j in range(8)]
        rows = [jnp.broadcast_to(work[p][j:j + 1, :], shape) for j in range(8)]
        scaled = []
        kept = None
        for j in range(8):
            pivot = jnp.broadcast_to(cols[j][0][j:j + 1, :], shape)
            inv = 1.0 / pivot
            for k in range(j + 1, 8):
                factor = jnp.broadcast_to(cols[j][0][k:k + 1, :], shape) * inv
                for q in range(groups - p):
                    cols[k][q] = cols[k][q] - cols[j][q] * factor
                rows[k] = rows[k] - rows[j] * factor
            scaled.append(rows[j] * inv)
            unit_row = rows[j] * lax.rsqrt(pivot)
            kept = unit_row if j == 0 else jnp.where(sub == j, unit_row, kept)
        for q in range(p + 1, groups):
            for j in range(8):
                work[q] = work[q] - cols[j][q - p] * scaled[j]
        done.append(kept)
    return jnp.concatenate(done, axis=0)[:, size:]


def unpack(core, mine_ref, other_ref, full_ref):
    first = core == 0
    low = jnp.where(first, mine_ref[...], other_ref[...])
    high = jnp.where(first, other_ref[...], mine_ref[...])
    g10 = jnp.concatenate([low[128:192], high[0:64]], axis=0)
    full_ref[0:128, 0:128] = low[0:128]
    full_ref[128:256, 0:128] = g10
    full_ref[0:128, 128:256] = g10.T
    full_ref[128:256, 128:256] = high[64:192]


def three(x):
    hi, lo = split(x)
    return jnp.concatenate([hi, hi, lo], axis=1)


def chain_kernel(core_ref, gv_mine, gv_other, gu_mine, gu_other, sketch_ref, c_ref, mu_ref, mv_ref, next_ref,
                 gv_ref, gu_ref, panel_ref, block_ref):
    core = core_ref[0]
    unpack(core, gv_mine, gv_other, gv_ref)
    unpack(core, gu_mine, gu_other, gu_ref)
    block_ref[...] = jnp.zeros_like(block_ref)
    for k in range(STENCILS):
        at = slice(k * RANK, (k + 1) * RANK)
        block_ref[at, at] = c_ref[...]
        panel_ref[k] = gv_ref[:, at]
    parts = [None] * STENCILS
    for p in range(STENCILS):
        at = slice(p * RANK, (p + 1) * RANK)
        inverse = lower_inverse(panel_ref[p, at, :])
        below = full_dot(panel_ref[p, p * RANK:, :], inverse, NT)
        for q in range(p + 1, STENCILS):
            head = (q - p) * RANK
            panel_ref[q, q * RANK:, :] -= full_dot(below[head:], below[head:head + RANK], NT)
        for q in range(p, STENCILS):
            head = (q - p) * RANK
            block = below[head:head + RANK]
            if q == p:
                block = jnp.where(
                    lax.broadcasted_iota(jnp.int32, block.shape, 0) >= lane_iota(block.shape), block, 0.0)
            term = full_dot(sketch_ref[p], block, NT)
            parts[q] = term if parts[q] is None else parts[q] + term
    base = jnp.concatenate(parts, axis=1)
    w_t = full_dot(base, block_ref[...], NT)
    k_t = full_dot(w_t, gu_ref[...])
    inverse_y = lower_inverse(full_dot(w_t, k_t, NT))
    x_t = full_dot(inverse_y, full_dot(k_t, block_ref[...]))
    map_u = full_dot(inverse_y, w_t)
    inner = full_dot(x_t, full_dot(x_t, gv_ref[...]), NT)
    inverse_c = lower_inverse(inner)
    map_v = full_dot(inverse_c, x_t)
    lower = full_dot(inner, inverse_c, NT)
    keep = lax.broadcasted_iota(jnp.int32, lower.shape, 0) >= lane_iota(lower.shape)
    next_ref[...] = jnp.where(keep, lower, 0.0)
    for k in range(STENCILS):
        at = slice(k * RANK, (k + 1) * RANK)
        mu_ref[at, :] = three(map_u[:, at])
        mv_ref[at, :] = three(map_v[:, at])


def chain(core, gv_mine, gv_other, gu_mine, gu_other, sketch_t, core_matrix):
    return pl.pallas_call(
        chain_kernel,
        in_specs=[smem()] + [vmem()] * 6,
        out_specs=[vmem()] * 3,
        out_shape=[
            jax.ShapeDtypeStruct((WIDE, 3 * RANK), BF16),
            jax.ShapeDtypeStruct((WIDE, 3 * RANK), BF16),
            jax.ShapeDtypeStruct((RANK, RANK), F32),
        ],
        scratch_shapes=[
            pltpu.VMEM((WIDE, WIDE), F32),
            pltpu.VMEM((WIDE, WIDE), F32),
            pltpu.VMEM((STENCILS, WIDE, RANK), F32),
            pltpu.VMEM((WIDE, WIDE), F32),
        ],
        compiler_params=pltpu.CompilerParams(vmem_limit_bytes=VMEM_LIMIT),
        name="chain",
    )(core, gv_mine, gv_other, gu_mine, gu_other, sketch_t, core_matrix)


def put_three(ref, at, x):
    hi, lo = split(x)
    ref[0:RANK, at] = hi
    ref[RANK:2 * RANK, at] = lo
    ref[2 * RANK:3 * RANK, at] = hi


def next_u_kernel(steps, u_ref, before_ref, after_ref, left_ref, right_ref, m_ref, d_ref, map_ref, out_ref, plain, laps, p_ref, q_ref):
    step = pl.program_id(0)
    chunks = u_ref.shape[1] // LANES
    before, after = ends(left_ref, before_ref, after_ref, right_ref, step, steps)
    cells = [before] + [u_ref[:, c * LANES:(c + 1) * LANES] for c in range(chunks)] + [after]
    second = laplace_chunks(cells)
    for c in range(chunks):
        at = slice(c * LANES, (c + 1) * LANES)
        put_three(plain, at, cells[c + 1])
        put_three(laps, at, second[c])
    p_ref[...] = fast_dot(map_ref[...], plain[...], NN)
    q_ref[...] = fast_dot(map_ref[...], laps[...], NN)
    for c in range(chunks):
        at = slice(c * LANES, (c + 1) * LANES)
        total = None
        for k in range(STENCILS):
            rows = slice(k * RANK, (k + 1) * RANK)
            term = m_ref[k:k + 1, at] * p_ref[rows, at] + d_ref[k:k + 1, at] * q_ref[rows, at]
            total = term if total is None else total + term
        out_ref[:, at] = total


def next_u(u, left, right, mass, diffusion, map_u):
    cells = u.shape[1]
    tile = min(1024, cells)
    steps = cells // tile
    table = pl.BlockSpec((STENCILS, tile), lambda i: (0, i))
    return pl.pallas_call(
        functools.partial(next_u_kernel, steps),
        grid=(steps,),
        in_specs=tile_specs(tile, cells) + [table, table, pl.BlockSpec((WIDE, 3 * RANK), lambda i: (0, 0))],
        out_specs=pl.BlockSpec((RANK, tile), lambda i: (0, i)),
        out_shape=jax.ShapeDtypeStruct((RANK, cells), F32),
        scratch_shapes=[pltpu.VMEM((3 * RANK, tile), BF16)] * 2 + [pltpu.VMEM((WIDE, tile), F32)] * 2,
        compiler_params=pltpu.CompilerParams(vmem_limit_bytes=VMEM_LIMIT),
        name="next_u",
    )(u, u, u, left, right, mass, diffusion, map_u)


def next_v_kernel(steps, off_ref, v_ref, before_ref, after_ref, left_ref, right_ref, w_ref, map_ref, out_ref, plain, p_ref):
    step = pl.program_id(0)
    chunks = v_ref.shape[1] // LANES
    before, after = ends(left_ref, before_ref, after_ref, right_ref, step, steps)
    cells = [before] + [v_ref[:, c * LANES:(c + 1) * LANES] for c in range(chunks)] + [after]
    for c in range(chunks + 2):
        put_three(plain, slice(c * LANES, (c + 1) * LANES), cells[c])
    p_ref[...] = fast_dot(map_ref[...], plain[...], NN)
    lane = lane_iota((RANK, LANES))
    for k in range(STENCILS):
        rows = slice(k * RANK, (k + 1) * RANK)
        for t in range(TAPS):
            by = off_ref[k, t]
            turn = lax.rem(LANES - by, LANES)
            near = jnp.where(by >= 0, 1, -1)
            inside = jnp.logical_and(lane + by >= 0, lane + by < LANES)
            for c in range(chunks):
                at = slice(c * LANES, (c + 1) * LANES)
                here = p_ref[rows, (c + 1) * LANES:(c + 2) * LANES]
                there = p_ref[rows, pl.ds(pl.multiple_of((c + 1 + near) * LANES, LANES), LANES)]
                mixed = jnp.where(inside, pltpu.roll(here, turn, 1), pltpu.roll(there, turn, 1))
                term = w_ref[k, t:t + 1, at] * mixed
                if k == 0 and t == 0:
                    out_ref[:, at] = term
                else:
                    out_ref[:, at] += term


def next_v(offsets, v, left, right, weights, map_v):
    cells = v.shape[1]
    tile = min(1024, cells)
    steps = cells // tile
    spec = pltpu.PrefetchScalarGridSpec(
        num_scalar_prefetch=1,
        grid=(steps,),
        in_specs=tile_specs(tile, cells) + [
            pl.BlockSpec((STENCILS, TAPS, tile), lambda i, *_: (0, 0, i)),
            pl.BlockSpec((WIDE, 3 * RANK), lambda i, *_: (0, 0)),
        ],
        out_specs=pl.BlockSpec((RANK, tile), lambda i, *_: (0, i)),
        scratch_shapes=[pltpu.VMEM((3 * RANK, tile + 2 * LANES), BF16), pltpu.VMEM((WIDE, tile + 2 * LANES), F32)],
    )
    return pl.pallas_call(
        functools.partial(next_v_kernel, steps),
        grid_spec=spec,
        out_shape=jax.ShapeDtypeStruct((RANK, cells), F32),
        compiler_params=pltpu.CompilerParams(vmem_limit_bytes=VMEM_LIMIT),
        name="next_v",
    )(offsets, v, v, v, left, right, weights, map_v)


def make_sketch_t(sketch_seed, wide, rank):
    shape = (wide // rank, rank, rank)
    rows_idx = lax.broadcasted_iota(jnp.int32, shape, 0) * rank + lax.broadcasted_iota(jnp.int32, shape, 2)
    cols_idx = lax.broadcasted_iota(jnp.int32, shape, 1)
    first = (rows_idx * 131 + cols_idx * 977 + sketch_seed[0]) % 65521
    second = first * 7919 % 65521
    upper = second // 256
    lower = second % 256
    third = (upper * upper * 15 + 512 * upper * lower + lower * lower) % 65521
    fourth = (third * 30011 + rows_idx * 17 + cols_idx) % 65521
    return ((fourth.astype(F32) + 0.5) / 65521.0 - 0.5) * 3.4641


def swap(x, axis, bit):
    return lax.ppermute(x, axis, [(i, i ^ bit) for i in range(lax.axis_size(axis))])


def local(u, v, mass_table, diffusivity_table, material_index, weights, offsets, core_matrix, sketch_seed):
    gx, pa = lax.axis_size("gx"), lax.axis_size("pa")
    at_gx = lax.axis_index("gx")
    core = (at_gx % 2).astype(jnp.int32).reshape(1)
    even = core[0] == 0
    head, tail = v[:, :LANES], v[:, -LANES:]
    send = jnp.where(even, tail, head)
    pairs = []
    for g in range(gx):
        for p in range(pa):
            q = p + 1 if g % 2 == 0 else p - 1
            if 0 <= q < pa:
                pairs.append((g * pa + p, g * pa + q))
    halo = lax.ppermute(send, ("gx", "pa"), pairs)
    gv_mine, gv_other = gram_v(core, offsets, v, halo, weights, 1.0 / (v.shape[1] * pa))

    halo_other = swap(halo, "gx", 1)
    left_v = jnp.where(even, halo, halo_other)
    right_v = jnp.where(even, halo_other, halo)
    left_u = lax.ppermute(u[:, -LANES:], "gx", [(i, i + 1) for i in range(gx - 1)])
    right_u = lax.ppermute(u[:, :LANES], "gx", [(i + 1, i) for i in range(gx - 1)])
    onehot = (material_index[:, None, :] == jnp.arange(mass_table.shape[1], dtype=jnp.int32)[None, :, None]).astype(F32)
    mass = jnp.sum(mass_table[:, :, None] * onehot, axis=1)
    diffusion = jnp.sum(diffusivity_table[:, :, None] * onehot, axis=1)
    gu_mine, gu_other = gram_u(core, u, left_u, right_u, mass, diffusion, 1.0 / (u.shape[1] * gx))

    gv = gv_mine + swap(gv_other, "gx", 1)
    bit = 1
    while bit < pa:
        gv = gv + swap(gv, "pa", bit)
        bit *= 2
    gu = gu_mine + swap(gu_other, "gx", 1)
    bit = 2
    while bit < gx:
        gu = gu + swap(gu, "gx", bit)
        bit *= 2
    gv_far = swap(gv, "gx", 1)
    gu_far = swap(gu, "gx", 1)
    sketch_t = make_sketch_t(sketch_seed, WIDE, RANK)
    map_u, map_v, core_next = chain(core, gv, gv_far, gu, gu_far, sketch_t, core_matrix)
    u_next = next_u(u, left_u, right_u, mass, diffusion, map_u)
    v_next = next_v(offsets, v, left_v, right_v, weights, map_v)
    return (u_next, v_next, core_next)


def solution(mesh):
    return jax.shard_map(
        local,
        mesh=mesh,
        in_specs=(
            P(None, "gx"),
            P(None, "pa"),
            P(),
            P(),
            P(None, "gx"),
            P(None, None, "pa"),
            P(),
            P(),
            P(),
        ),
        out_specs=(P(None, "gx"), P(None, "pa"), P()),
        check_vma=False,
    )
```

profile of v0, /device:TPU:1, one launch (start us, length us, event | category | flops | bytes accessed | tf_op | source)
XLA Modules:
  0.0 111.6 jit_solution(15275451388893060667)
XLA Ops:
  0.6 0.8 slice_select_fusion
  1.4 1.3 %collective-permute-start.2 = (f32[64,128]{1,0:T(8,128)S(1)}, f32[64,128]{1,0:T(8,128)S(1)}, u32[]{:S(2)}, u32[]{:S(2)}) collective-permute-start(f32[64,128]{1,0:T(8,128)S(1)} %slice_select_fusion), channel_id=1, source_target_pairs={{0,1},{1,2},{2,3},{3,4},{4,5},{5,6},{6,7},{7,8},{8,9},{9,10},{10,1... | collective-permute-start | bytes 98312 | tf_op jit(solution)/shard_map/ppermute | solution.py:475
  2.7 2.1 %copy.14.w_ref = f32[4,3,8192]{2,1,0:T(4,128)} copy(f32[4,3,8192]{2,0,1:T(4,128)} %param.14) | data formatting | bytes 786432 | tf_op args[5]
  4.8 2.3 %collective-permute-done.2.halo_ref = f32[64,128]{1,0:T(8,128)S(1)} collective-permute-done((f32[64,128]{1,0:T(8,128)S(1)}, f32[64,128]{1,0:T(8,128)S(1)}, u32[]{:S(2)}, u32[]{:S(2)}) %collective-permute-start.2) | collective-permute-done | bytes 32800 | tf_op jit(solution)/shard_map/ppermute | solution.py:475
  7.1 0.6 copy-done.4
  7.7 0.0 copy-start.6
  7.7 0.0 copy-start.9
  7.7 0.0 copy-start.10
  7.7 8.7 %gram_v.1 = (f32[192,128]{1,0:T(8,128)}, f32[192,128]{1,0:T(8,128)}) custom-call(s32[1]{0:T(128)} %bitcast.core_ref, s32[4,3]{1,0:T(4,128)} %off_ref.3, f32[64,8192]{1,0:T(8,128)} %after_ref.7, f32[64,8192]{1,0:T(8,128)} %after_ref.7, f32[64,8192]{1,0:T(8,128)} %after_ref.7, f32[64,128]{1,0:T(8,128)} %copy-done.4, f32[4,3,8192]{2,1,0:T(4,128)} %copy.14.w_ref), custom_call_target="tpu_custom_call" | custom-call | tf_op jit(solution)/shard_map/gram_v/pallas_call | solution.py:154
  16.4 1.8 %collective-permute-start.3 = (f32[192,128]{1,0:T(8,128)}, f32[192,128]{1,0:T(8,128)S(1)}, u32[]{:S(2)}, u32[]{:S(2)}) collective-permute-start(f32[192,128]{1,0:T(8,128)} %get-tuple-element.11), channel_id=1, source_target_pairs={{0,32},{32,0},{64,96},{96,64},{128,160},{160,128},{192,224},{224,1... | collective-permute-start | bytes 294920 | tf_op jit(solution)/shard_map/ppermute | solution.py:459
  18.2 1.2 %collective-permute-done.3 = f32[192,128]{1,0:T(8,128)S(1)} collective-permute-done((f32[192,128]{1,0:T(8,128)}, f32[192,128]{1,0:T(8,128)S(1)}, u32[]{:S(2)}, u32[]{:S(2)}) %collective-permute-start.3) | collective-permute-done | bytes 98336 | tf_op jit(solution)/shard_map/ppermute | solution.py:459
  19.3 0.9 add.85
  20.2 1.7 %collective-permute-start.4 = (f32[192,128]{1,0:T(8,128)S(1)}, f32[192,128]{1,0:T(8,128)S(1)}, u32[]{:S(2)}, u32[]{:S(2)}) collective-permute-start(f32[192,128]{1,0:T(8,128)S(1)} %add.85), channel_id=1, source_target_pairs={{0,1},{1,0},{2,3},{3,2},{4,5},{5,4},{6,7},{7,6},{8,9},{9,8},{10,11... | collective-permute-start | bytes 294920 | tf_op jit(solution)/shard_map/ppermute | solution.py:459
  21.9 0.8 fusion.18
  22.7 2.5 %collective-permute-start.1 = (f32[64,128]{1,0:T(8,128)S(1)}, f32[64,128]{1,0:T(8,128)S(1)}, u32[]{:S(2)}, u32[]{:S(2)}) collective-permute-start(f32[64,128]{1,0:T(8,128)S(1)} %get-tuple-element.19), channel_id=1, source_target_pairs={{32,0},{64,32},{96,64},{128,96},{160,128},{192,160},{224,192},{33,... | collective-permute-start | bytes 98312 | tf_op jit(solution)/shard_map/ppermute | solution.py:482
  25.3 3.1 %collective-permute-start = (f32[64,128]{1,0:T(8,128)S(1)}, f32[64,128]{1,0:T(8,128)S(1)}, u32[]{:S(2)}, u32[]{:S(2)}) collective-permute-start(f32[64,128]{1,0:T(8,128)S(1)} %get-tuple-element.20), channel_id=1, source_target_pairs={{0,32},{32,64},{64,96},{96,128},{128,160},{160,192},{192,224},{1,3... | collective-permute-start | bytes 98312 | tf_op jit(solution)/shard_map/ppermute | solution.py:481
  28.4 0.0 collective-permute-done.4
  28.4 4.3 %collective-permute-start.5 = (f32[192,128]{1,0:T(8,128)S(1)}, f32[192,128]{1,0:T(8,128)S(1)}, u32[]{:S(2)}, u32[]{:S(2)}) collective-permute-start(f32[192,128]{1,0:T(8,128)S(1)} %add.86), channel_id=1, source_target_pairs={{0,2},{1,3},{2,0},{3,1},{4,6},{5,7},{6,4},{7,5},{8,10},{9,11},{10,... | collective-permute-start | bytes 294920 | tf_op jit(solution)/shard_map/ppermute | solution.py:459
  32.7 0.0 copy-done.6
  32.7 0.0 copy-done.9
  32.7 0.0 copy-done.10
  32.7 1.6 %select_reduce_fusion = (f32[4,8192]{1,0:T(4,128)}, f32[4,8192]{1,0:T(4,128)}) fusion(f32[4,16]{1,0:T(4,128)S(1)} %copy-done.9, s32[4,8192]{1,0:T(4,128)S(1)} %copy-done.6, f32[4,16]{1,0:T(4,128)S(1)} %copy-done.10), kind=kLoop, calls=%fused_computation | loop fusion | flops 2555904 | bytes 393728 | tf_op jit(solution)/shard_map/reduce_sum | solution.py:485
  34.9 0.0 collective-permute-done.1.right_ref
  34.9 0.0 copy-start.2
  35.0 0.0 collective-permute-done.left_ref
  35.0 0.0 copy-start.3
  35.0 0.6 copy-done.2
  35.6 0.0 copy-done.3
  35.6 0.0 copy-start.5
  35.6 9.3 %gram_u.1 = (f32[192,128]{1,0:T(8,128)}, f32[192,128]{1,0:T(8,128)}) custom-call(s32[1]{0:T(128)} %bitcast.core_ref, f32[64,8192]{1,0:T(8,128)} %after_ref.6, f32[64,8192]{1,0:T(8,128)} %after_ref.6, f32[64,8192]{1,0:T(8,128)} %after_ref.6, f32[64,128]{1,0:T(8,128)} %copy-done.3, f32[64,128]{1,0:T(8,128)} %copy-done.2, f32[4,8192]{1,0:T(4,128)} %get-tuple-element.18.m_ref, ...), custom_call_target="tpu_custom_call" | custom-call | tf_op jit(solution)/shard_map/gram_u/pallas_call | solution.py:224
  44.9 0.0 collective-permute-start.10
  44.9 0.0 collective-permute-done.5
  44.9 3.5 %collective-permute-start.6 = (f32[192,128]{1,0:T(8,128)S(1)}, f32[192,128]{1,0:T(8,128)S(1)}, u32[]{:S(2)}, u32[]{:S(2)}) collective-permute-start(f32[192,128]{1,0:T(8,128)S(1)} %add.87), channel_id=1, source_target_pairs={{0,4},{1,5},{2,6},{3,7},{4,0},{5,1},{6,2},{7,3},{8,12},{9,13},{10,... | collective-permute-start | bytes 294920 | tf_op jit(solution)/shard_map/ppermute | solution.py:459
  48.4 0.0 collective-permute-done.10
  48.4 0.9 add.91
  49.3 1.4 %collective-permute-start.11 = (f32[192,128]{1,0:T(8,128)S(1)}, f32[192,128]{1,0:T(8,128)S(1)}, u32[]{:S(2)}, u32[]{:S(2)}) collective-permute-start(f32[192,128]{1,0:T(8,128)S(1)} %add.91), channel_id=1, source_target_pairs={{0,64},{32,96},{64,0},{96,32},{128,192},{160,224},{192,128},{224,1... | collective-permute-start | bytes 294920 | tf_op jit(solution)/shard_map/ppermute | solution.py:459
  50.7 2.1 %collective-permute-done.6 = f32[192,128]{1,0:T(8,128)S(1)} collective-permute-done((f32[192,128]{1,0:T(8,128)S(1)}, f32[192,128]{1,0:T(8,128)S(1)}, u32[]{:S(2)}, u32[]{:S(2)}) %collective-permute-start.6) | collective-permute-done | bytes 98336 | tf_op jit(solution)/shard_map/ppermute | solution.py:459
  52.8 1.3 %collective-permute-start.7 = (f32[192,128]{1,0:T(8,128)S(1)}, f32[192,128]{1,0:T(8,128)S(1)}, u32[]{:S(2)}, u32[]{:S(2)}) collective-permute-start(f32[192,128]{1,0:T(8,128)S(1)} %add.88), channel_id=1, source_target_pairs={{0,8},{1,9},{2,10},{3,11},{4,12},{5,13},{6,14},{7,15},{8,0},{9,1},... | collective-permute-start | bytes 294920 | tf_op jit(solution)/shard_map/ppermute | solution.py:459
  54.1 0.0 copy-done.5
  54.1 1.7 %collective-permute-start.14 = (f32[64,128]{1,0:T(8,128)S(1)}, f32[64,128]{1,0:T(8,128)S(1)}, u32[]{:S(2)}, u32[]{:S(2)}) collective-permute-start(f32[64,128]{1,0:T(8,128)S(1)} %copy-done.5), channel_id=1, source_target_pairs={{0,32},{32,0},{64,96},{96,64},{128,160},{160,128},{192,224},{224,1... | collective-permute-start | bytes 98312 | tf_op jit(solution)/shard_map/ppermute | solution.py:459
  55.8 0.0 collective-permute-done.11
  55.8 2.9 %collective-permute-start.12 = (f32[192,128]{1,0:T(8,128)S(1)}, f32[192,128]{1,0:T(8,128)S(1)}, u32[]{:S(2)}, u32[]{:S(2)}) collective-permute-start(f32[192,128]{1,0:T(8,128)S(1)} %add.92), channel_id=1, source_target_pairs={{0,128},{32,160},{64,192},{96,224},{128,0},{160,32},{192,64},{224,... | collective-permute-start | bytes 294920 | tf_op jit(solution)/shard_map/ppermute | solution.py:459
  58.7 0.0 collective-permute-done.7
  58.7 2.5 %collective-permute-start.8 = (f32[192,128]{1,0:T(8,128)S(1)}, f32[192,128]{1,0:T(8,128)S(1)}, u32[]{:S(2)}, u32[]{:S(2)}) collective-permute-start(f32[192,128]{1,0:T(8,128)S(1)} %add.89), channel_id=1, source_target_pairs={{0,16},{1,17},{2,18},{3,19},{4,20},{5,21},{6,22},{7,23},{8,24},{9,... | collective-permute-start | bytes 294920 | tf_op jit(solution)/shard_map/ppermute | solution.py:459
  61.3 1.2 %fusion.10.sketch_ref = f32[4,64,64]{2,1,0:T(8,128)} fusion(s32[]{:T(128)} %bitcast.2, s32[64]{0:T(128)S(1)} %iota_multiply_fusion, s32[4]{0:T(128)S(1)} %iota_multiply_fusion.1), kind=kLoop, calls=%fused_computation.22 | loop fusion | flops 1048576 | bytes 65812 | tf_op jit(solution)/shard_map/mul | solution.py:455
  62.5 0.0 collective-permute-done.12
  62.5 0.0 copy-start
  62.5 0.8 collective-permute-start.13
  63.3 1.0 collective-permute-done.8
  64.4 0.0 copy-start.1
  64.4 1.4 %collective-permute-start.9 = (f32[192,128]{1,0:T(8,128)S(1)}, f32[192,128]{1,0:T(8,128)S(1)}, u32[]{:S(2)}, u32[]{:S(2)}) collective-permute-start(f32[192,128]{1,0:T(8,128)S(1)} %add.90.gv_mine), channel_id=1, source_target_pairs={{0,32},{32,0},{64,96},{96,64},{128,160},{160,128},{192,224},{224,1... | collective-permute-start | bytes 294920 | tf_op jit(solution)/shard_map/ppermute | solution.py:459
  65.8 0.0 collective-permute-done.14
  65.8 0.6 broadcast_select_fusion
  66.5 0.0 collective-permute-done.13.gu_other
  66.5 0.0 copy-start.7
  66.5 0.3 collective-permute-done.9.gv_other
  66.8 0.0 copy-done
  66.8 0.0 copy-done.1
  66.8 0.3 copy-done.7
  67.1 0.0 copy-start.8
  67.1 0.6 copy-done.8
  67.7 16.7 %chain.1 = (bf16[256,192]{1,0:T(8,128)(2,1)}, bf16[256,192]{1,0:T(8,128)(2,1)}, f32[64,64]{1,0:T(8,128)}) custom-call(s32[1]{0:T(128)} %bitcast.core_ref, f32[192,128]{1,0:T(8,128)} %copy-done.1, f32[192,128]{1,0:T(8,128)} %copy-done.8, f32[192,128]{1,0:T(8,128)} %copy-done, f32[192,128]{1,0:T(8,128)} %copy-done.7, f32[4,64,64]{2,1,0:T(8,128)} %fusion.10.sketch_ref, ...), custom_call_target="tpu_custom_call" | custom-call | tf_op jit(solution)/shard_map/chain/pallas_call | solution.py:328
  84.4 19.4 %next_v.1 = f32[64,8192]{1,0:T(8,128)} custom-call(s32[4,3]{1,0:T(4,128)} %off_ref.3, f32[64,8192]{1,0:T(8,128)} %after_ref.7, f32[64,8192]{1,0:T(8,128)} %after_ref.7, f32[64,8192]{1,0:T(8,128)} %after_ref.7, f32[64,128]{1,0:T(8,128)} %get-tuple-element.22.left_ref, f32[64,128]{1,0:T(8,128)} %get-tuple-element.21.right_ref, f32[4,3,8192]{2,1,0:T(4,128)} %copy.14.w_ref, ...), custom_call_target="tpu_custom_call" | custom-call | tf_op jit(solution)/shard_map/next_v/pallas_call | solution.py:436
  103.8 7.8 %next_u.1 = f32[64,8192]{1,0:T(8,128)} custom-call(f32[64,8192]{1,0:T(8,128)} %after_ref.6, f32[64,8192]{1,0:T(8,128)} %after_ref.6, f32[64,8192]{1,0:T(8,128)} %after_ref.6, f32[64,128]{1,0:T(8,128)} %copy-done.3, f32[64,128]{1,0:T(8,128)} %copy-done.2, f32[4,8192]{1,0:T(4,128)} %get-tuple-element.18.m_ref, f32[4,8192]{1,0:T(4,128)} %get-tuple-element.17.d_ref, ...), custom_call_target="tpu_custom_call" | custom-call | tf_op jit(solution)/shard_map/next_u/pallas_call | solution.py:382
  (10 shorter events, 0.1 us)
Async XLA Ops:
  1.4 5.6 %collective-permute-start.2 = (f32[64,128]{1,0:T(8,128)S(1)}, f32[64,128]{1,0:T(8,128)S(1)}, u32[]{:S(2)}, u32[]{:S(2)}) collective-permute-start(f32[64,128]{1,0:T(8,128)S(1)} %slice_select_fusion), channel_id=1, source_target_pairs={{0,1},{1,2},{2,3},{3,4},{4,5},{5,6},{6,7},{7,8},{8,9},{9,10},{10,1... | collective-permute-start | bytes 98312 | tf_op jit(solution)/shard_map/ppermute | solution.py:475
  7.1 0.6 copy-start.4
  7.7 25.0 %copy-start.6 = (s32[4,8192]{1,0:T(4,128)S(1)}, s32[4,8192]{1,0:T(4,128)}, u32[]{:S(2)}) copy-start(s32[4,8192]{1,0:T(4,128)} %param.13) | copy-start | bytes 393220
  7.7 25.0 %copy-start.9 = (f32[4,16]{1,0:T(4,128)S(1)}, f32[4,16]{1,0:T(4,128)}, u32[]{:S(2)}) copy-start(f32[4,16]{1,0:T(4,128)} %param.12) | copy-start | bytes 772
  7.7 25.0 %copy-start.10 = (f32[4,16]{1,0:T(4,128)S(1)}, f32[4,16]{1,0:T(4,128)}, u32[]{:S(2)}) copy-start(f32[4,16]{1,0:T(4,128)} %param.11) | copy-start | bytes 772
  16.4 2.9 %collective-permute-start.3 = (f32[192,128]{1,0:T(8,128)}, f32[192,128]{1,0:T(8,128)S(1)}, u32[]{:S(2)}, u32[]{:S(2)}) collective-permute-start(f32[192,128]{1,0:T(8,128)} %get-tuple-element.11), channel_id=1, source_target_pairs={{0,32},{32,0},{64,96},{96,64},{128,160},{160,128},{192,224},{224,1... | collective-permute-start | bytes 294920 | tf_op jit(solution)/shard_map/ppermute | solution.py:459
  20.2 8.2 %collective-permute-start.4 = (f32[192,128]{1,0:T(8,128)S(1)}, f32[192,128]{1,0:T(8,128)S(1)}, u32[]{:S(2)}, u32[]{:S(2)}) collective-permute-start(f32[192,128]{1,0:T(8,128)S(1)} %add.85), channel_id=1, source_target_pairs={{0,1},{1,0},{2,3},{3,2},{4,5},{5,4},{6,7},{7,6},{8,9},{9,8},{10,11... | collective-permute-start | bytes 294920 | tf_op jit(solution)/shard_map/ppermute | solution.py:459
  22.7 12.2 %collective-permute-start.1 = (f32[64,128]{1,0:T(8,128)S(1)}, f32[64,128]{1,0:T(8,128)S(1)}, u32[]{:S(2)}, u32[]{:S(2)}) collective-permute-start(f32[64,128]{1,0:T(8,128)S(1)} %get-tuple-element.19), channel_id=1, source_target_pairs={{32,0},{64,32},{96,64},{128,96},{160,128},{192,160},{224,192},{33,... | collective-permute-start | bytes 98312 | tf_op jit(solution)/shard_map/ppermute | solution.py:482
  25.3 9.7 %collective-permute-start = (f32[64,128]{1,0:T(8,128)S(1)}, f32[64,128]{1,0:T(8,128)S(1)}, u32[]{:S(2)}, u32[]{:S(2)}) collective-permute-start(f32[64,128]{1,0:T(8,128)S(1)} %get-tuple-element.20), channel_id=1, source_target_pairs={{0,32},{32,64},{64,96},{96,128},{128,160},{160,192},{192,224},{1,3... | collective-permute-start | bytes 98312 | tf_op jit(solution)/shard_map/ppermute | solution.py:481
  28.4 16.5 %collective-permute-start.5 = (f32[192,128]{1,0:T(8,128)S(1)}, f32[192,128]{1,0:T(8,128)S(1)}, u32[]{:S(2)}, u32[]{:S(2)}) collective-permute-start(f32[192,128]{1,0:T(8,128)S(1)} %add.86), channel_id=1, source_target_pairs={{0,2},{1,3},{2,0},{3,1},{4,6},{5,7},{6,4},{7,5},{8,10},{9,11},{10,... | collective-permute-start | bytes 294920 | tf_op jit(solution)/shard_map/ppermute | solution.py:459
  34.9 0.6 copy-start.2
  35.0 0.6 copy-start.3
  35.6 18.5 %copy-start.5 = (f32[64,128]{1,0:T(8,128)S(1)}, f32[64,128]{1,0:T(8,128)}, u32[]{:S(2)}) copy-start(f32[64,128]{1,0:T(8,128)} %copy-done.4) | copy-start | bytes 98308
  44.9 3.5 %collective-permute-start.10 = (f32[192,128]{1,0:T(8,128)}, f32[192,128]{1,0:T(8,128)S(1)}, u32[]{:S(2)}, u32[]{:S(2)}) collective-permute-start(f32[192,128]{1,0:T(8,128)} %get-tuple-element.13), channel_id=1, source_target_pairs={{0,32},{32,0},{64,96},{96,64},{128,160},{160,128},{192,224},{224,1... | collective-permute-start | bytes 294920 | tf_op jit(solution)/shard_map/ppermute | solution.py:459
  44.9 7.8 %collective-permute-start.6 = (f32[192,128]{1,0:T(8,128)S(1)}, f32[192,128]{1,0:T(8,128)S(1)}, u32[]{:S(2)}, u32[]{:S(2)}) collective-permute-start(f32[192,128]{1,0:T(8,128)S(1)} %add.87), channel_id=1, source_target_pairs={{0,4},{1,5},{2,6},{3,7},{4,0},{5,1},{6,2},{7,3},{8,12},{9,13},{10,... | collective-permute-start | bytes 294920 | tf_op jit(solution)/shard_map/ppermute | solution.py:459
  49.3 6.5 %collective-permute-start.11 = (f32[192,128]{1,0:T(8,128)S(1)}, f32[192,128]{1,0:T(8,128)S(1)}, u32[]{:S(2)}, u32[]{:S(2)}) collective-permute-start(f32[192,128]{1,0:T(8,128)S(1)} %add.91), channel_id=1, source_target_pairs={{0,64},{32,96},{64,0},{96,32},{128,192},{160,224},{192,128},{224,1... | collective-permute-start | bytes 294920 | tf_op jit(solution)/shard_map/ppermute | solution.py:459
  52.8 6.0 %collective-permute-start.7 = (f32[192,128]{1,0:T(8,128)S(1)}, f32[192,128]{1,0:T(8,128)S(1)}, u32[]{:S(2)}, u32[]{:S(2)}) collective-permute-start(f32[192,128]{1,0:T(8,128)S(1)} %add.88), channel_id=1, source_target_pairs={{0,8},{1,9},{2,10},{3,11},{4,12},{5,13},{6,14},{7,15},{8,0},{9,1},... | collective-permute-start | bytes 294920 | tf_op jit(solution)/shard_map/ppermute | solution.py:459
  54.1 11.8 %collective-permute-start.14 = (f32[64,128]{1,0:T(8,128)S(1)}, f32[64,128]{1,0:T(8,128)S(1)}, u32[]{:S(2)}, u32[]{:S(2)}) collective-permute-start(f32[64,128]{1,0:T(8,128)S(1)} %copy-done.5), channel_id=1, source_target_pairs={{0,32},{32,0},{64,96},{96,64},{128,160},{160,128},{192,224},{224,1... | collective-permute-start | bytes 98312 | tf_op jit(solution)/shard_map/ppermute | solution.py:459
  55.8 6.7 %collective-permute-start.12 = (f32[192,128]{1,0:T(8,128)S(1)}, f32[192,128]{1,0:T(8,128)S(1)}, u32[]{:S(2)}, u32[]{:S(2)}) collective-permute-start(f32[192,128]{1,0:T(8,128)S(1)} %add.92), channel_id=1, source_target_pairs={{0,128},{32,160},{64,192},{96,224},{128,0},{160,32},{192,64},{224,... | collective-permute-start | bytes 294920 | tf_op jit(solution)/shard_map/ppermute | solution.py:459
  58.7 5.6 %collective-permute-start.8 = (f32[192,128]{1,0:T(8,128)S(1)}, f32[192,128]{1,0:T(8,128)S(1)}, u32[]{:S(2)}, u32[]{:S(2)}) collective-permute-start(f32[192,128]{1,0:T(8,128)S(1)} %add.89), channel_id=1, source_target_pairs={{0,16},{1,17},{2,18},{3,19},{4,20},{5,21},{6,22},{7,23},{8,24},{9,... | collective-permute-start | bytes 294920 | tf_op jit(solution)/shard_map/ppermute | solution.py:459
  62.5 4.3 %copy-start = (f32[192,128]{1,0:T(8,128)}, f32[192,128]{1,0:T(8,128)S(1)}, u32[]{:S(2)}) copy-start(f32[192,128]{1,0:T(8,128)S(1)} %add.93.gu_mine) | copy-start | bytes 294916
  62.5 4.0 %collective-permute-start.13 = (f32[192,128]{1,0:T(8,128)S(1)}, f32[192,128]{1,0:T(8,128)S(1)}, u32[]{:S(2)}, u32[]{:S(2)}) collective-permute-start(f32[192,128]{1,0:T(8,128)S(1)} %add.93.gu_mine), channel_id=1, source_target_pairs={{0,32},{32,0},{64,96},{96,64},{128,160},{160,128},{192,224},{224,1... | collective-permute-start | bytes 294920 | tf_op jit(solution)/shard_map/ppermute | solution.py:459
  64.4 2.4 %copy-start.1 = (f32[192,128]{1,0:T(8,128)}, f32[192,128]{1,0:T(8,128)S(1)}, u32[]{:S(2)}) copy-start(f32[192,128]{1,0:T(8,128)S(1)} %add.90.gv_mine) | copy-start | bytes 294916
  64.4 2.4 %collective-permute-start.9 = (f32[192,128]{1,0:T(8,128)S(1)}, f32[192,128]{1,0:T(8,128)S(1)}, u32[]{:S(2)}, u32[]{:S(2)}) collective-permute-start(f32[192,128]{1,0:T(8,128)S(1)} %add.90.gv_mine), channel_id=1, source_target_pairs={{0,32},{32,0},{64,96},{96,64},{128,160},{160,128},{192,224},{224,1... | collective-permute-start | bytes 294920 | tf_op jit(solution)/shard_map/ppermute | solution.py:459
  66.5 0.6 copy-start.7
  67.1 0.6 copy-start.8
where the time goes:
time: 112 us
  Pallas kernels  61.8 us (55%)
  starting transfers between devices  30.3 us (27%)
  waiting for transfers between devices  6.89 us (6%)
  other arithmetic  6.09 us (5%)
  local copies, waits for them, and re-layouts  5.05 us (5%)
  between operations  1.44 us (1%)
    ppermute x12, starting transfers between devices, swap(): lax.ppermute(x, axis, [(i, i ^ bit) for i in range(lax.axis_size(axis))])  23.4 us
    pallas_call x1, Pallas kernels, next_v(): pl.pallas_call(functools.partial(next_v_kernel, steps), grid_spec=spec, o...  19.4 us
    pallas_call x1, Pallas kernels, chain(): pl.pallas_call(chain_kernel, in_specs=[smem()] + [vmem()] * 6, out_specs=...  16.7 us
    pallas_call x1, Pallas kernels, gram_u(): pl.pallas_call(functools.partial(gram_u_kernel, steps, scale), grid_spec=...  9.27 us
    pallas_call x1, Pallas kernels, gram_v(): pl.pallas_call(functools.partial(gram_v_kernel, steps, scale), grid_spec=...  8.66 us
    pallas_call x1, Pallas kernels, next_u(): pl.pallas_call(functools.partial(next_u_kernel, steps), grid=(steps,), in...  7.84 us
    ppermute x12, waiting for transfers between devices, swap(): lax.ppermute(x, axis, [(i, i ^ bit) for i in range(lax.axis_size(axis))])  4.58 us
    unnamed x23, local copies, waits for them, and re-layouts  4.27 us
  transfers between devices with their start and end apart: 15, of which 5 were waited for; matrix products, arithmetic and copies ran while one was open for 6% of the time, Pallas kernels for 8%

commit v1 on v0

v1 whole, which is shorter than its diff:
```python
import functools

import jax
import jax.numpy as jnp
from jax import lax
from jax.experimental import pallas as pl
from jax.experimental.pallas import tpu as pltpu
from jax.sharding import PartitionSpec as P

BAND = 4
LANES = 128
RANK = 64
STENCILS = 4
TAPS = 3
WIDE = 256
F32 = jnp.float32
BF16 = jnp.bfloat16
NT = (((1,), (1,)), ((), ()))
NN = (((1,), (0,)), ((), ()))
VMEM_LIMIT = 56 * 1024 * 1024


def smem():
    return pl.BlockSpec(memory_space=pltpu.SMEM)


def vmem():
    return pl.BlockSpec(memory_space=pltpu.VMEM)


def split(x):
    hi = x.astype(BF16)
    lo = (x - hi.astype(F32)).astype(BF16)
    return hi, lo


def fast_dot(a, b, dims):
    return lax.dot_general(a, b, dims, preferred_element_type=F32)


def full_dot(a, b, dims=NN):
    return lax.dot_general(a, b, dims, precision=lax.Precision.HIGHEST, preferred_element_type=F32)


def lane_iota(shape):
    return lax.broadcasted_iota(jnp.int32, shape, len(shape) - 1)


def shift_left(here, after, by):
    mask = lane_iota(here.shape) < LANES - by
    return jnp.where(mask, pltpu.roll(here, LANES - by, 1), pltpu.roll(after, LANES - by, 1))


def shift_right(before, here, by):
    mask = lane_iota(here.shape) >= by
    return jnp.where(mask, pltpu.roll(here, by, 1), pltpu.roll(before, by, 1))


def finish_gram(hh_ref, hl_ref, pack_ref, scale, core, mine_ref, other_ref):
    for row, col, at in ((0, 0, 0), (128, 0, 128), (128, 128, 256)):
        part = hl_ref[row:row + 128, col:col + 128] + hl_ref[col:col + 128, row:row + 128].T
        pack_ref[at:at + 128, :] = (hh_ref[row:row + 128, col:col + 128] + part) * scale
    half = 192
    mine_ref[...] = pack_ref[pl.ds(pl.multiple_of(core * half, half), half), :]
    other_ref[...] = pack_ref[pl.ds(pl.multiple_of((1 - core) * half, half), half), :]


def add_gram(hi_ref, lo_ref, hh_ref, hl_ref):
    hi = hi_ref[...]
    hh_ref[...] += fast_dot(hi, hi, NT)
    hl_ref[...] += fast_dot(hi, lo_ref[...], NT)


def keep_wide(total, k, near, at, hi_ref, lo_ref, wide_hi, wide_lo):
    rows = slice(k * RANK, (k + 1) * RANK)
    hi, lo = split(total)
    hi_ref[rows, near] = hi
    lo_ref[rows, near] = lo
    wide_hi[rows, at] = hi
    wide_lo[rows, at] = lo


def gram_scratch(part):
    return [pltpu.VMEM((WIDE, part), BF16)] * 4 + [pltpu.VMEM((WIDE, WIDE), F32)] * 2 + [pltpu.VMEM((384, LANES), F32)]


def start_gram(hi_ref, lo_ref, hh_ref, hl_ref):
    hi_ref[...] = jnp.zeros_like(hi_ref)
    lo_ref[...] = jnp.zeros_like(lo_ref)
    hh_ref[...] = jnp.zeros_like(hh_ref)
    hl_ref[...] = jnp.zeros_like(hl_ref)


def shift_all(cells, first, count, moved):
    for i in range(count):
        c = first + i
        lanes = slice(i * LANES, (i + 1) * LANES)
        for by in range(1, BAND + 1):
            moved[BAND + by, :, lanes] = shift_left(cells[c + 1], cells[c + 2], by)
            moved[BAND - by, :, lanes] = shift_right(cells[c], cells[c + 1], by)
        moved[BAND, :, lanes] = cells[c + 1]


def gram_v_kernel(steps, scale, core_ref, off_ref, v_ref, before_ref, after_ref, halo_ref, w_ref,
                  mine_ref, other_ref, wide_hi, wide_lo,
                  moved_a, moved_b, hi_a, lo_a, hi_b, lo_b, hh_ref, hl_ref, pack_ref):
    step = pl.program_id(0)
    core = core_ref[0]
    tile = v_ref.shape[1]
    chunks = tile // LANES
    part = chunks // 2

    @pl.when(step == 0)
    def _():
        start_gram(hi_b, lo_b, hh_ref, hl_ref)

    at_left = jnp.logical_and(step == 0, core == 0)
    at_right = jnp.logical_and(step == steps - 1, core == 1)
    before = jnp.where(at_left, halo_ref[...], before_ref[...])
    after = jnp.where(at_right, halo_ref[...], after_ref[...])
    cells = [before] + [v_ref[:, c * LANES:(c + 1) * LANES] for c in range(chunks)] + [after]
    add_gram(hi_b, lo_b, hh_ref, hl_ref)
    for half, moved, hi_ref, lo_ref in ((0, moved_a, hi_a, lo_a), (1, moved_b, hi_b, lo_b)):
        shift_all(cells, half * part, part, moved)
        for k in range(STENCILS):
            for i in range(part):
                near = slice(i * LANES, (i + 1) * LANES)
                at = slice((half * part + i) * LANES, (half * part + i + 1) * LANES)
                total = w_ref[0, k:k + 1, at] * moved[off_ref[k, 0] + BAND, :, near]
                for t in range(1, TAPS):
                    total = total + w_ref[t, k:k + 1, at] * moved[off_ref[k, t] + BAND, :, near]
                keep_wide(total, k, near, at, hi_ref, lo_ref, wide_hi, wide_lo)
        if half == 0:
            add_gram(hi_a, lo_a, hh_ref, hl_ref)

    @pl.when(step == steps - 1)
    def _():
        add_gram(hi_b, lo_b, hh_ref, hl_ref)
        finish_gram(hh_ref, hl_ref, pack_ref, scale, core, mine_ref, other_ref)


def gram_v(core, offsets, v, halo, weights, scale):
    cells = v.shape[1]
    half = cells // 2
    tile = min(1024, half)
    steps = half // tile
    ratio = tile // LANES
    last = cells // LANES - 1
    spec = pltpu.PrefetchScalarGridSpec(
        num_scalar_prefetch=2,
        grid=(steps,),
        in_specs=[
            pl.BlockSpec((RANK, tile), lambda i, c, o: (0, c[0] * steps + i)),
            pl.BlockSpec((RANK, LANES), lambda i, c, o: (0, jnp.maximum((c[0] * steps + i) * ratio - 1, 0))),
            pl.BlockSpec((RANK, LANES), lambda i, c, o: (0, jnp.minimum((c[0] * steps + i + 1) * ratio, last))),
            pl.BlockSpec((RANK, LANES), lambda i, c, o: (0, 0)),
            pl.BlockSpec((TAPS, STENCILS, tile), lambda i, c, o: (0, 0, c[0] * steps + i)),
        ],
        out_specs=[pl.BlockSpec((192, LANES), lambda i, c, o: (0, 0))] * 2 + [pl.BlockSpec((WIDE, tile), lambda i, c, o: (0, i))] * 2,
        scratch_shapes=[pltpu.VMEM((2 * BAND + 1, RANK, tile // 2), F32)] * 2 + gram_scratch(tile // 2),
    )
    return pl.pallas_call(
        functools.partial(gram_v_kernel, steps, scale),
        grid_spec=spec,
        out_shape=[jax.ShapeDtypeStruct((192, LANES), F32)] * 2 + [jax.ShapeDtypeStruct((WIDE, half), BF16)] * 2,
        compiler_params=pltpu.CompilerParams(vmem_limit_bytes=VMEM_LIMIT),
        name="gram_v",
    )(core, offsets, v, v, v, halo, weights)


def gram_u_kernel(steps, scale, core_ref, u_ref, before_ref, after_ref, left_ref, right_ref, m_ref, d_ref,
                  mine_ref, other_ref, wide_hi, wide_lo,
                  hi_a, lo_a, hi_b, lo_b, hh_ref, hl_ref, pack_ref):
    step = pl.program_id(0)
    chunks = u_ref.shape[1] // LANES
    part = chunks // 2

    @pl.when(step == 0)
    def _():
        start_gram(hi_b, lo_b, hh_ref, hl_ref)

    before = jnp.where(step == 0, left_ref[...], before_ref[...])
    after = jnp.where(step == steps - 1, right_ref[...], after_ref[...])
    cells = [before] + [u_ref[:, c * LANES:(c + 1) * LANES] for c in range(chunks)] + [after]
    add_gram(hi_b, lo_b, hh_ref, hl_ref)
    for half, hi_ref, lo_ref in ((0, hi_a, lo_a), (1, hi_b, lo_b)):
        for i in range(part):
            c = half * part + i
            near = slice(i * LANES, (i + 1) * LANES)
            at = slice(c * LANES, (c + 1) * LANES)
            up = shift_left(cells[c + 1], cells[c + 2], 1)
            down = shift_right(cells[c], cells[c + 1], 1)
            lap = up - 2.0 * cells[c + 1] + down
            for k in range(STENCILS):
                total = m_ref[k:k + 1, at] * cells[c + 1] + d_ref[k:k + 1, at] * lap
                keep_wide(total, k, near, at, hi_ref, lo_ref, wide_hi, wide_lo)
        if half == 0:
            add_gram(hi_a, lo_a, hh_ref, hl_ref)

    @pl.when(step == steps - 1)
    def _():
        add_gram(hi_b, lo_b, hh_ref, hl_ref)
        finish_gram(hh_ref, hl_ref, pack_ref, scale, core_ref[0], mine_ref, other_ref)


def gram_u(core, u, left, right, mass, diffusion, scale):
    cells = u.shape[1]
    tile = min(1024, cells)
    steps = cells // tile
    ratio = tile // LANES
    last = cells // LANES - 1
    table = pl.BlockSpec((STENCILS, tile), lambda i, *_: (0, i))
    spec = pltpu.PrefetchScalarGridSpec(
        num_scalar_prefetch=1,
        grid=(steps,),
        in_specs=[
            pl.BlockSpec((RANK, tile), lambda i, *_: (0, i)),
            pl.BlockSpec((RANK, LANES), lambda i, *_: (0, jnp.maximum(i * ratio - 1, 0))),
            pl.BlockSpec((RANK, LANES), lambda i, *_: (0, jnp.minimum((i + 1) * ratio, last))),
            pl.BlockSpec((RANK, LANES), lambda i, *_: (0, 0)),
            pl.BlockSpec((RANK, LANES), lambda i, *_: (0, 0)),
            table,
            table,
        ],
        out_specs=[pl.BlockSpec((192, LANES), lambda i, *_: (0, 0))] * 2 + [pl.BlockSpec((WIDE, tile), lambda i, *_: (0, i))] * 2,
        scratch_shapes=gram_scratch(tile // 2),
    )
    return pl.pallas_call(
        functools.partial(gram_u_kernel, steps, scale),
        grid_spec=spec,
        out_shape=[jax.ShapeDtypeStruct((192, LANES), F32)] * 2 + [jax.ShapeDtypeStruct((WIDE, cells), BF16)] * 2,
        compiler_params=pltpu.CompilerParams(vmem_limit_bytes=VMEM_LIMIT),
        name="gram_u",
    )(core, u, u, u, left, right, mass, diffusion)


def lower_inverse(square):
    size = RANK
    groups = size // 8
    rows_idx = lax.broadcasted_iota(jnp.int32, (size, size), 0)
    cols_idx = lax.broadcasted_iota(jnp.int32, (size, size), 1)
    unit = jnp.where(rows_idx == cols_idx, 1.0, 0.0).astype(F32)
    both = jnp.concatenate([square, unit], axis=1)
    work = [both[8 * q:8 * q + 8, :] for q in range(groups)]
    shape = (8, 2 * size)
    sub = lax.broadcasted_iota(jnp.int32, shape, 0)
    done = []
    for p in range(groups):
        cols = [[jnp.broadcast_to(work[q][:, 8 * p + j:8 * p + j + 1], shape) for q in range(p, groups)] for j in range(8)]
        rows = [jnp.broadcast_to(work[p][j:j + 1, :], shape) for j in range(8)]
        scaled = []
        kept = None
        for j in range(8):
            pivot = jnp.broadcast_to(cols[j][0][j:j + 1, :], shape)
            inv = 1.0 / pivot
            for k in range(j + 1, 8):
                factor = jnp.broadcast_to(cols[j][0][k:k + 1, :], shape) * inv
                for q in range(groups - p):
                    cols[k][q] = cols[k][q] - cols[j][q] * factor
                rows[k] = rows[k] - rows[j] * factor
            scaled.append(rows[j] * inv)
            unit_row = rows[j] * lax.rsqrt(pivot)
            kept = unit_row if j == 0 else jnp.where(sub == j, unit_row, kept)
        for q in range(p + 1, groups):
            for j in range(8):
                work[q] = work[q] - cols[j][q - p] * scaled[j]
        done.append(kept)
    return jnp.concatenate(done, axis=0)[:, size:]


def unpack(core, mine_ref, other_ref, full_ref):
    first = core == 0
    low = jnp.where(first, mine_ref[...], other_ref[...])
    high = jnp.where(first, other_ref[...], mine_ref[...])
    g10 = jnp.concatenate([low[128:192], high[0:64]], axis=0)
    full_ref[0:128, 0:128] = low[0:128]
    full_ref[128:256, 0:128] = g10
    full_ref[0:128, 128:256] = g10.T
    full_ref[128:256, 128:256] = high[64:192]


def put_split(ref, x):
    hi, lo = split(x)
    ref[0:RANK, :] = hi
    ref[RANK:2 * RANK, :] = lo


def chain_kernel(core_ref, gv_mine, gv_other, gu_mine, gu_other, sketch_ref, c_ref, mu_ref, mv_ref, next_ref,
                 gv_ref, gu_ref, panel_ref, block_ref):
    core = core_ref[0]
    unpack(core, gv_mine, gv_other, gv_ref)
    unpack(core, gu_mine, gu_other, gu_ref)
    block_ref[...] = jnp.zeros_like(block_ref)
    for k in range(STENCILS):
        at = slice(k * RANK, (k + 1) * RANK)
        block_ref[at, at] = c_ref[...]
        panel_ref[k] = gv_ref[:, at]
    parts = [None] * STENCILS
    for p in range(STENCILS):
        at = slice(p * RANK, (p + 1) * RANK)
        inverse = lower_inverse(panel_ref[p, at, :])
        below = full_dot(panel_ref[p, p * RANK:, :], inverse, NT)
        for q in range(p + 1, STENCILS):
            head = (q - p) * RANK
            panel_ref[q, q * RANK:, :] -= full_dot(below[head:], below[head:head + RANK], NT)
        for q in range(p, STENCILS):
            head = (q - p) * RANK
            block = below[head:head + RANK]
            if q == p:
                block = jnp.where(
                    lax.broadcasted_iota(jnp.int32, block.shape, 0) >= lane_iota(block.shape), block, 0.0)
            term = full_dot(sketch_ref[p], block, NT)
            parts[q] = term if parts[q] is None else parts[q] + term
    base = jnp.concatenate(parts, axis=1)
    w_t = full_dot(base, block_ref[...], NT)
    k_t = full_dot(w_t, gu_ref[...])
    inverse_y = lower_inverse(full_dot(w_t, k_t, NT))
    x_t = full_dot(inverse_y, full_dot(k_t, block_ref[...]))
    map_u = full_dot(inverse_y, w_t)
    inner = full_dot(x_t, full_dot(x_t, gv_ref[...]), NT)
    inverse_c = lower_inverse(inner)
    map_v = full_dot(inverse_c, x_t)
    lower = full_dot(inner, inverse_c, NT)
    keep = lax.broadcasted_iota(jnp.int32, lower.shape, 0) >= lane_iota(lower.shape)
    next_ref[...] = jnp.where(keep, lower, 0.0)
    put_split(mu_ref, map_u)
    put_split(mv_ref, map_v)


def chain(core, gv_mine, gv_other, gu_mine, gu_other, sketch_t, core_matrix):
    return pl.pallas_call(
        chain_kernel,
        in_specs=[smem()] + [vmem()] * 6,
        out_specs=[vmem()] * 3,
        out_shape=[
            jax.ShapeDtypeStruct((2 * RANK, WIDE), BF16),
            jax.ShapeDtypeStruct((2 * RANK, WIDE), BF16),
            jax.ShapeDtypeStruct((RANK, RANK), F32),
        ],
        scratch_shapes=[
            pltpu.VMEM((WIDE, WIDE), F32),
            pltpu.VMEM((WIDE, WIDE), F32),
            pltpu.VMEM((STENCILS, WIDE, RANK), F32),
            pltpu.VMEM((WIDE, WIDE), F32),
        ],
        compiler_params=pltpu.CompilerParams(vmem_limit_bytes=VMEM_LIMIT),
        name="chain",
    )(core, gv_mine, gv_other, gu_mine, gu_other, sketch_t, core_matrix)


def next_kernel(map_ref, hi_ref, lo_ref, out_ref):
    both = fast_dot(map_ref[...], hi_ref[...], NN)
    out_ref[...] = both[0:RANK] + (both[RANK:2 * RANK] + fast_dot(map_ref[0:RANK, :], lo_ref[...], NN))


def next_factor(name, maps, wide_hi, wide_lo):
    cells = wide_hi.shape[1]
    tile = min(1024, cells)
    return pl.pallas_call(
        next_kernel,
        grid=(cells // tile,),
        in_specs=[
            pl.BlockSpec((2 * RANK, WIDE), lambda i: (0, 0)),
            pl.BlockSpec((WIDE, tile), lambda i: (0, i)),
            pl.BlockSpec((WIDE, tile), lambda i: (0, i)),
        ],
        out_specs=pl.BlockSpec((RANK, tile), lambda i: (0, i)),
        out_shape=jax.ShapeDtypeStruct((RANK, cells), F32),
        compiler_params=pltpu.CompilerParams(vmem_limit_bytes=VMEM_LIMIT),
        name=name,
    )(maps, wide_hi, wide_lo)


def make_sketch_t(sketch_seed, wide, rank):
    shape = (wide // rank, rank, rank)
    rows_idx = lax.broadcasted_iota(jnp.int32, shape, 0) * rank + lax.broadcasted_iota(jnp.int32, shape, 2)
    cols_idx = lax.broadcasted_iota(jnp.int32, shape, 1)
    first = (rows_idx * 131 + cols_idx * 977 + sketch_seed[0]) % 65521
    second = first * 7919 % 65521
    upper = second // 256
    lower = second % 256
    third = (upper * upper * 15 + 512 * upper * lower + lower * lower) % 65521
    fourth = (third * 30011 + rows_idx * 17 + cols_idx) % 65521
    return ((fourth.astype(F32) + 0.5) / 65521.0 - 0.5) * 3.4641


def swap(x, axis, bit):
    return lax.ppermute(x, axis, [(i, i ^ bit) for i in range(lax.axis_size(axis))])


def local(u, v, mass_table, diffusivity_table, material_index, weights, offsets, core_matrix, sketch_seed):
    gx, pa = lax.axis_size("gx"), lax.axis_size("pa")
    at_gx = lax.axis_index("gx")
    core = (at_gx % 2).astype(jnp.int32).reshape(1)
    even = core[0] == 0
    at_pa = lax.axis_index("pa")
    edge_u = jnp.where(even, u[:, :LANES], u[:, -LANES:])
    edge_v = jnp.where(even, v[:, :LANES], v[:, -LANES:])
    pairs = []
    for g in range(gx):
        for p in range(pa):
            if g % 2 == 0:
                pairs.append((g * pa + p, (g - 1) % gx * pa + (p - 1) % pa))
            else:
                pairs.append((g * pa + p, (g + 1) % gx * pa + (p + 1) % pa))
    far = lax.ppermute(jnp.concatenate([edge_u, edge_v], axis=0), ("gx", "pa"), pairs)
    out_u = jnp.logical_or(at_gx == 0, at_gx == gx - 1)
    out_v = at_pa == jnp.where(even, 0, pa - 1)
    far_u = jnp.where(out_u, 0.0, far[:RANK])
    far_v = jnp.where(out_v, 0.0, far[RANK:])
    weights = jnp.transpose(weights, (1, 0, 2))
    gv_mine, gv_other, hi_v, lo_v = gram_v(core, offsets, v, far_v, weights, 1.0 / (v.shape[1] * pa))
    near_u = swap(jnp.where(even, u[:, -LANES:], u[:, :LANES]), "gx", 1)
    left_u = jnp.where(even, far_u, near_u)
    right_u = jnp.where(even, near_u, far_u)
    onehot = (material_index[:, None, :] == jnp.arange(mass_table.shape[1], dtype=jnp.int32)[None, :, None]).astype(F32)
    mass = jnp.sum(mass_table[:, :, None] * onehot, axis=1)
    diffusion = jnp.sum(diffusivity_table[:, :, None] * onehot, axis=1)
    gu_mine, gu_other, hi_u, lo_u = gram_u(core, u, left_u, right_u, mass, diffusion, 1.0 / (u.shape[1] * gx))

    gv = gv_mine + swap(gv_other, "gx", 1)
    bit = 1
    while bit < pa:
        gv = gv + swap(gv, "pa", bit)
        bit *= 2
    gu = gu_mine + swap(gu_other, "gx", 1)
    bit = 2
    while bit < gx:
        gu = gu + swap(gu, "gx", bit)
        bit *= 2
    gv_far = swap(gv, "gx", 1)
    gu_far = swap(gu, "gx", 1)
    sketch_t = make_sketch_t(sketch_seed, WIDE, RANK)
    map_u, map_v, core_next = chain(core, gv, gv_far, gu, gu_far, sketch_t, core_matrix)
    half = next_factor("next_v", map_v, hi_v, lo_v)
    half_far = swap(half, "gx", 1)
    u_next = next_factor("next_u", map_u, hi_u, lo_u)
    v_next = jnp.concatenate([jnp.where(even, half, half_far), jnp.where(even, half_far, half)], axis=1)
    return (u_next, v_next, core_next)


def solution(mesh):
    return jax.shard_map(
        local,
        mesh=mesh,
        in_specs=(
            P(None, "gx"),
            P(None, "pa"),
            P(),
            P(),
            P(None, "gx"),
            P(None, None, "pa"),
            P(),
            P(),
            P(),
        ),
        out_specs=(P(None, "gx"), P(None, "pa"), P()),
        check_vma=False,
    )
```

time: 112 us -> 99.1 us (0.88)
  Pallas kernels: 61.8 us -> 47.7 us
  local copies, waits for them, and re-layouts: 5.05 us -> 1.26 us
  waiting for transfers between devices: 6.89 us -> 9.91 us
  other arithmetic: 6.09 us -> 8.51 us
  starting transfers between devices: 30.3 us -> 29 us
    pallas_call x2, Pallas kernels: 27.2 us -> 12.4 us  [next_factor(): pl.pallas_call(next_kernel, grid=(cells // tile,), in_specs=[pl.BlockSpec...]
    ppermute x12 -> x13, waiting for transfers between devices: 4.58 us -> 9.91 us  [swap(): lax.ppermute(x, axis, [(i, i ^ bit) for i in range(lax.axis_size(axis))])]
    unnamed x23 -> x16, local copies, waits for them, and re-layouts: 4.27 us -> 1.26 us
    ppermute x3 -> x1, starting transfers between devices: 6.92 us -> 4.12 us  [local(): lax.ppermute(jnp.concatenate([edge_u, edge_v], axis=0), ('gx', 'pa'), pairs)]
    ppermute x3 -> x1, waiting for transfers between devices: 2.3 us -> 0.01 us  [local(): lax.ppermute(jnp.concatenate([edge_u, edge_v], axis=0), ('gx', 'pa'), pairs)]
    concatenate x0 -> x2, other arithmetic: none -> 1.48 us  [the longest x1 1.47 us: local(): jnp.concatenate([jnp.where(even, half, half_far), jnp.where(even, half_fa...]
    ppermute x12 -> x13, starting transfers between devices: 23.4 us -> 24.9 us  [swap(): lax.ppermute(x, axis, [(i, i ^ bit) for i in range(lax.axis_size(axis))])]
    select_n x2 -> x4, other arithmetic: 1.42 us -> 2.37 us  [the longest x1 0.78 us: local(): edge_v = jnp.where(even, v[:, :LANES], v[:, -LANES:])]
  transfers between devices with their start and end apart: 15 -> 14, of which waited for: 5 -> 5; matrix products, arithmetic and copies ran while one was open for 6% -> 4% of each run, Pallas kernels for 8% -> 19%
where the time goes in v1:
time: 99.1 us; the launch traced here: 97.9 us
  Pallas kernels  47.7 us (48%)
  starting transfers between devices  29 us (29%)
  waiting for transfers between devices  9.91 us (10%)
  other arithmetic  8.51 us (9%)
  between operations  1.47 us (1%)
  local copies, waits for them, and re-layouts  1.26 us (1%)
    ppermute x13, starting transfers between devices, swap(): lax.ppermute(x, axis, [(i, i ^ bit) for i in range(lax.axis_size(axis))])  24.9 us
    pallas_call x1, Pallas kernels, chain(): pl.pallas_call(chain_kernel, in_specs=[smem()] + [vmem()] * 6, out_specs=...  16.6 us
    pallas_call x2, Pallas kernels, next_factor(): pl.pallas_call(next_kernel, grid=(cells // tile,), in_specs=[pl.BlockSpec...  12.4 us
    pallas_call x1, Pallas kernels, gram_u(): pl.pallas_call(functools.partial(gram_u_kernel, steps, scale), grid_spec=...  10.3 us
    ppermute x13, waiting for transfers between devices, swap(): lax.ppermute(x, axis, [(i, i ^ bit) for i in range(lax.axis_size(axis))])  9.91 us
    pallas_call x1, Pallas kernels, gram_v(): pl.pallas_call(functools.partial(gram_v_kernel, steps, scale), grid_spec=...  8.43 us
    ppermute x1, starting transfers between devices, local(): lax.ppermute(jnp.concatenate([edge_u, edge_v], axis=0), ('gx', 'pa'), pairs)  4.12 us
  transfers between devices with their start and end apart: 14, of which 5 were waited for; matrix products, arithmetic and copies ran while one was open for 4% of the time, Pallas kernels for 19%

profile of v1, /device:TPU:1, one launch (start us, length us, event | category | flops | bytes accessed | tf_op | source)
XLA Modules:
  0.0 97.9 jit_solution(10775735004115654105)
XLA Ops:
  0.6 0.8 slice_select_fusion.2
  1.4 0.8 slice_select_fusion.3
  2.2 4.1 %collective-permute-start = (f32[128,128]{1,0:T(8,128)S(1)}, f32[128,128]{1,0:T(8,128)S(1)}, u32[]{:S(2)}, u32[]{:S(2)}) collective-permute-start(f32[128,128]{1,0:T(8,128)S(1)} %pad_maximum_fusion.1), channel_id=1, source_target_pairs={{0,255},{1,224},{2,225},{3,226},{4,227},{5,228},{6,229},{7,230},{8... | collective-permute-start | bytes 196616 | tf_op jit(solution)/shard_map/ppermute | solution.py:406
  6.3 7.4 %collective-permute-start.8 = (f32[64,128]{1,0:T(8,128)S(1)}, f32[64,128]{1,0:T(8,128)S(1)}, u32[]{:S(2)}, u32[]{:S(2)}) collective-permute-start(f32[64,128]{1,0:T(8,128)S(1)} %get-tuple-element.29), channel_id=1, source_target_pairs={{0,32},{32,0},{64,96},{96,64},{128,160},{160,128},{192,224},{224,1... | collective-permute-start | bytes 98312 | tf_op jit(solution)/shard_map/ppermute | solution.py:388
  13.7 0.9 collective-permute-done.8
  14.6 0.0 collective-permute-done
  14.6 0.6 fusion.18
  15.2 0.0 copy-start.3
  15.2 0.0 copy-start.6
  15.2 0.0 copy-start.7
  15.2 8.4 %gram_v.1 = (f32[192,128]{1,0:T(8,128)}, f32[192,128]{1,0:T(8,128)}, bf16[256,4096]{1,0:T(8,128)(2,1)}, bf16[256,4096]{1,0:T(8,128)(2,1)}) custom-call(s32[1]{0:T(128)} %bitcast.core_ref, s32[4,3]{1,0:T(4,128)} %off_ref.1, f32[64,8192]{1,0:T(8,128)} %after_ref.2, f32[64,8192]{1,0:T(8,128)} %after_ref.2, f32[64,8192]{1,0:T(8,128)} %after_ref.2, ...), custom_call_target="tpu_custom_call" | custom-call | tf_op jit(solution)/shard_map/gram_v/pallas_call | solution.py:162
  23.7 1.1 %collective-permute-start.1 = (f32[192,128]{1,0:T(8,128)}, f32[192,128]{1,0:T(8,128)S(1)}, u32[]{:S(2)}, u32[]{:S(2)}) collective-permute-start(f32[192,128]{1,0:T(8,128)} %get-tuple-element.15), channel_id=1, source_target_pairs={{0,32},{32,0},{64,96},{96,64},{128,160},{160,128},{192,224},{224,1... | collective-permute-start | bytes 294920 | tf_op jit(solution)/shard_map/ppermute | solution.py:388
  24.8 1.2 %collective-permute-done.1 = f32[192,128]{1,0:T(8,128)S(1)} collective-permute-done((f32[192,128]{1,0:T(8,128)}, f32[192,128]{1,0:T(8,128)S(1)}, u32[]{:S(2)}, u32[]{:S(2)}) %collective-permute-start.1) | collective-permute-done | bytes 98336 | tf_op jit(solution)/shard_map/ppermute | solution.py:388
  26.0 0.9 add.85
  26.9 0.1 collective-permute-start.2
  27.0 4.0 %collective-permute-done.2 = f32[192,128]{1,0:T(8,128)S(1)} collective-permute-done((f32[192,128]{1,0:T(8,128)S(1)}, f32[192,128]{1,0:T(8,128)S(1)}, u32[]{:S(2)}, u32[]{:S(2)}) %collective-permute-start.2) | collective-permute-done | bytes 98336 | tf_op jit(solution)/shard_map/ppermute | solution.py:388
  31.0 0.1 collective-permute-start.3
  31.1 0.0 copy-done.3
  31.1 0.0 copy-done.6
  31.1 0.0 copy-done.7
  31.1 1.6 %select_reduce_fusion = (f32[4,8192]{1,0:T(4,128)}, f32[4,8192]{1,0:T(4,128)}) fusion(f32[4,16]{1,0:T(4,128)S(1)} %copy-done.6, s32[4,8192]{1,0:T(4,128)S(1)} %copy-done.3, f32[4,16]{1,0:T(4,128)S(1)} %copy-done.7), kind=kLoop, calls=%fused_computation.1 | loop fusion | flops 2555904 | bytes 393728 | tf_op jit(solution)/shard_map/reduce_sum | solution.py:418
  32.7 10.3 %gram_u.1 = (f32[192,128]{1,0:T(8,128)}, f32[192,128]{1,0:T(8,128)}, bf16[256,8192]{1,0:T(8,128)(2,1)}, bf16[256,8192]{1,0:T(8,128)(2,1)}) custom-call(s32[1]{0:T(128)} %bitcast.core_ref, f32[64,8192]{1,0:T(8,128)} %after_ref.3, f32[64,8192]{1,0:T(8,128)} %after_ref.3, f32[64,8192]{1,0:T(8,128)} %after_ref.3, f32[64,128]{1,0:T(8,128)} %get-tuple-element.32.left_ref, ...), custom_call_target="tpu_custom_call" | custom-call | tf_op jit(solution)/shard_map/gram_u/pallas_call | solution.py:228
  43.0 1.2 %collective-permute-start.9 = (f32[192,128]{1,0:T(8,128)}, f32[192,128]{1,0:T(8,128)S(1)}, u32[]{:S(2)}, u32[]{:S(2)}) collective-permute-start(f32[192,128]{1,0:T(8,128)} %get-tuple-element.17), channel_id=1, source_target_pairs={{0,32},{32,0},{64,96},{96,64},{128,160},{160,128},{192,224},{224,1... | collective-permute-start | bytes 294920 | tf_op jit(solution)/shard_map/ppermute | solution.py:388
  44.2 0.0 collective-permute-done.3
  44.2 2.3 %collective-permute-start.4 = (f32[192,128]{1,0:T(8,128)S(1)}, f32[192,128]{1,0:T(8,128)S(1)}, u32[]{:S(2)}, u32[]{:S(2)}) collective-permute-start(f32[192,128]{1,0:T(8,128)S(1)} %add.87), channel_id=1, source_target_pairs={{0,4},{1,5},{2,6},{3,7},{4,0},{5,1},{6,2},{7,3},{8,12},{9,13},{10,... | collective-permute-start | bytes 294920 | tf_op jit(solution)/shard_map/ppermute | solution.py:388
  47.2 0.0 collective-permute-done.9
  47.2 0.9 add.91
  48.1 1.2 %collective-permute-start.10 = (f32[192,128]{1,0:T(8,128)S(1)}, f32[192,128]{1,0:T(8,128)S(1)}, u32[]{:S(2)}, u32[]{:S(2)}) collective-permute-start(f32[192,128]{1,0:T(8,128)S(1)} %add.91), channel_id=1, source_target_pairs={{0,64},{32,96},{64,0},{96,32},{128,192},{160,224},{192,128},{224,1... | collective-permute-start | bytes 294920 | tf_op jit(solution)/shard_map/ppermute | solution.py:388
  49.3 3.2 %collective-permute-done.4 = f32[192,128]{1,0:T(8,128)S(1)} collective-permute-done((f32[192,128]{1,0:T(8,128)S(1)}, f32[192,128]{1,0:T(8,128)S(1)}, u32[]{:S(2)}, u32[]{:S(2)}) %collective-permute-start.4) | collective-permute-done | bytes 98336 | tf_op jit(solution)/shard_map/ppermute | solution.py:388
  52.5 0.1 collective-permute-start.5
  52.7 0.0 collective-permute-done.10
  52.7 3.4 %collective-permute-start.11 = (f32[192,128]{1,0:T(8,128)S(1)}, f32[192,128]{1,0:T(8,128)S(1)}, u32[]{:S(2)}, u32[]{:S(2)}) collective-permute-start(f32[192,128]{1,0:T(8,128)S(1)} %add.92), channel_id=1, source_target_pairs={{0,128},{32,160},{64,192},{96,224},{128,0},{160,32},{192,64},{224,... | collective-permute-start | bytes 294920 | tf_op jit(solution)/shard_map/ppermute | solution.py:388
  56.1 0.0 collective-permute-done.5
  56.1 2.8 %collective-permute-start.6 = (f32[192,128]{1,0:T(8,128)S(1)}, f32[192,128]{1,0:T(8,128)S(1)}, u32[]{:S(2)}, u32[]{:S(2)}) collective-permute-start(f32[192,128]{1,0:T(8,128)S(1)} %add.89), channel_id=1, source_target_pairs={{0,16},{1,17},{2,18},{3,19},{4,20},{5,21},{6,22},{7,23},{8,24},{9,... | collective-permute-start | bytes 294920 | tf_op jit(solution)/shard_map/ppermute | solution.py:388
  59.0 0.0 collective-permute-done.11
  59.0 0.0 copy-start.1
  59.0 1.5 %collective-permute-start.12 = (f32[192,128]{1,0:T(8,128)S(1)}, f32[192,128]{1,0:T(8,128)S(1)}, u32[]{:S(2)}, u32[]{:S(2)}) collective-permute-start(f32[192,128]{1,0:T(8,128)S(1)} %add.93.gu_mine), channel_id=1, source_target_pairs={{0,32},{32,0},{64,96},{96,64},{128,160},{160,128},{192,224},{224,1... | collective-permute-start | bytes 294920 | tf_op jit(solution)/shard_map/ppermute | solution.py:388
  60.5 0.7 collective-permute-done.6
  61.2 0.0 copy-start.2
  61.2 3.5 %collective-permute-start.7 = (f32[192,128]{1,0:T(8,128)S(1)}, f32[192,128]{1,0:T(8,128)S(1)}, u32[]{:S(2)}, u32[]{:S(2)}) collective-permute-start(f32[192,128]{1,0:T(8,128)S(1)} %add.90.gv_mine), channel_id=1, source_target_pairs={{0,32},{32,0},{64,96},{96,64},{128,160},{160,128},{192,224},{224,1... | collective-permute-start | bytes 294920 | tf_op jit(solution)/shard_map/ppermute | solution.py:388
  64.7 1.2 %fusion.10.sketch_ref = f32[4,64,64]{2,1,0:T(8,128)} fusion(s32[]{:T(128)} %bitcast.3, s32[64]{0:T(128)S(1)} %iota_multiply_fusion, s32[4]{0:T(128)S(1)} %iota_multiply_fusion.1), kind=kLoop, calls=%fused_computation.25 | loop fusion | flops 1048576 | bytes 65812 | tf_op jit(solution)/shard_map/mul | solution.py:384
  65.9 0.0 collective-permute-done.12.gu_other
  65.9 0.0 copy-start.4
  65.9 0.0 collective-permute-done.7.gv_other
  65.9 0.0 copy-done.1
  65.9 0.0 copy-done.2
  65.9 0.6 copy-done.4
  66.6 0.0 copy-start.5
  66.6 0.6 copy-done.5
  67.2 16.6 %chain.1 = (bf16[128,256]{1,0:T(8,128)(2,1)}, bf16[128,256]{1,0:T(8,128)(2,1)}, f32[64,64]{1,0:T(8,128)}) custom-call(s32[1]{0:T(128)} %bitcast.core_ref, f32[192,128]{1,0:T(8,128)} %copy-done.2, f32[192,128]{1,0:T(8,128)} %copy-done.5, f32[192,128]{1,0:T(8,128)} %copy-done.1, f32[192,128]{1,0:T(8,128)} %copy-done.4, f32[4,64,64]{2,1,0:T(8,128)} %fusion.10.sketch_ref, ...), custom_call_target="tpu_custom_call" | custom-call | tf_op jit(solution)/shard_map/chain/pallas_call | solution.py:331
  83.8 4.5 %next_v.1 = f32[64,4096]{1,0:T(8,128)} custom-call(bf16[128,256]{1,0:T(8,128)(2,1)} %get-tuple-element.21.map_ref, bf16[256,4096]{1,0:T(8,128)(2,1)} %get-tuple-element.22.hi_ref, bf16[256,4096]{1,0:T(8,128)(2,1)} %get-tuple-element.23.lo_ref), custom_call_target="tpu_custom_call" | custom-call | tf_op jit(solution)/shard_map/next_v/pallas_call | solution.py:359
  88.3 0.0 collective-permute-start.13
  88.3 0.0 copy-start
  88.3 8.0 %next_u.1 = f32[64,8192]{1,0:T(8,128)} custom-call(bf16[128,256]{1,0:T(8,128)(2,1)} %get-tuple-element.18.map_ref, bf16[256,8192]{1,0:T(8,128)(2,1)} %get-tuple-element.19.hi_ref, bf16[256,8192]{1,0:T(8,128)(2,1)} %get-tuple-element.20.lo_ref), custom_call_target="tpu_custom_call" | custom-call | tf_op jit(solution)/shard_map/next_u/pallas_call | solution.py:359
  96.2 0.0 collective-permute-done.13
  96.3 0.0 copy-done
  96.3 0.2 broadcast_select_fusion.1
  96.4 1.5 %pad_maximum_fusion = f32[64,8192]{1,0:T(8,128)} fusion(f32[64,4096]{1,0:T(8,128)S(1)} %get-tuple-element.28, f32[64,4096]{1,0:T(8,128)S(1)} %get-tuple-element.27), kind=kLoop, calls=%fused_computation | loop fusion | flops 524288 | bytes 4194304 | tf_op jit(solution)/shard_map/concatenate | solution.py:438
  (10 shorter events, 0.1 us)
Async XLA Ops:
  2.2 12.4 %collective-permute-start = (f32[128,128]{1,0:T(8,128)S(1)}, f32[128,128]{1,0:T(8,128)S(1)}, u32[]{:S(2)}, u32[]{:S(2)}) collective-permute-start(f32[128,128]{1,0:T(8,128)S(1)} %pad_maximum_fusion.1), channel_id=1, source_target_pairs={{0,255},{1,224},{2,225},{3,226},{4,227},{5,228},{6,229},{7,230},{8... | collective-permute-start | bytes 196616 | tf_op jit(solution)/shard_map/ppermute | solution.py:406
  6.3 8.3 %collective-permute-start.8 = (f32[64,128]{1,0:T(8,128)S(1)}, f32[64,128]{1,0:T(8,128)S(1)}, u32[]{:S(2)}, u32[]{:S(2)}) collective-permute-start(f32[64,128]{1,0:T(8,128)S(1)} %get-tuple-element.29), channel_id=1, source_target_pairs={{0,32},{32,0},{64,96},{96,64},{128,160},{160,128},{192,224},{224,1... | collective-permute-start | bytes 98312 | tf_op jit(solution)/shard_map/ppermute | solution.py:388
  15.2 15.8 %copy-start.3 = (s32[4,8192]{1,0:T(4,128)S(1)}, s32[4,8192]{1,0:T(4,128)}, u32[]{:S(2)}) copy-start(s32[4,8192]{1,0:T(4,128)} %param.13) | copy-start | bytes 393220
  15.2 15.9 %copy-start.6 = (f32[4,16]{1,0:T(4,128)S(1)}, f32[4,16]{1,0:T(4,128)}, u32[]{:S(2)}) copy-start(f32[4,16]{1,0:T(4,128)} %param.12) | copy-start | bytes 772
  15.2 15.9 %copy-start.7 = (f32[4,16]{1,0:T(4,128)S(1)}, f32[4,16]{1,0:T(4,128)}, u32[]{:S(2)}) copy-start(f32[4,16]{1,0:T(4,128)} %param.11) | copy-start | bytes 772
  23.7 2.3 %collective-permute-start.1 = (f32[192,128]{1,0:T(8,128)}, f32[192,128]{1,0:T(8,128)S(1)}, u32[]{:S(2)}, u32[]{:S(2)}) collective-permute-start(f32[192,128]{1,0:T(8,128)} %get-tuple-element.15), channel_id=1, source_target_pairs={{0,32},{32,0},{64,96},{96,64},{128,160},{160,128},{192,224},{224,1... | collective-permute-start | bytes 294920 | tf_op jit(solution)/shard_map/ppermute | solution.py:388
  26.9 4.1 %collective-permute-start.2 = (f32[192,128]{1,0:T(8,128)S(1)}, f32[192,128]{1,0:T(8,128)S(1)}, u32[]{:S(2)}, u32[]{:S(2)}) collective-permute-start(f32[192,128]{1,0:T(8,128)S(1)} %add.85), channel_id=1, source_target_pairs={{0,1},{1,0},{2,3},{3,2},{4,5},{5,4},{6,7},{7,6},{8,9},{9,8},{10,11... | collective-permute-start | bytes 294920 | tf_op jit(solution)/shard_map/ppermute | solution.py:388
  31.0 13.2 %collective-permute-start.3 = (f32[192,128]{1,0:T(8,128)S(1)}, f32[192,128]{1,0:T(8,128)S(1)}, u32[]{:S(2)}, u32[]{:S(2)}) collective-permute-start(f32[192,128]{1,0:T(8,128)S(1)} %add.86), channel_id=1, source_target_pairs={{0,2},{1,3},{2,0},{3,1},{4,6},{5,7},{6,4},{7,5},{8,10},{9,11},{10,... | collective-permute-start | bytes 294920 | tf_op jit(solution)/shard_map/ppermute | solution.py:388
  43.0 4.2 %collective-permute-start.9 = (f32[192,128]{1,0:T(8,128)}, f32[192,128]{1,0:T(8,128)S(1)}, u32[]{:S(2)}, u32[]{:S(2)}) collective-permute-start(f32[192,128]{1,0:T(8,128)} %get-tuple-element.17), channel_id=1, source_target_pairs={{0,32},{32,0},{64,96},{96,64},{128,160},{160,128},{192,224},{224,1... | collective-permute-start | bytes 294920 | tf_op jit(solution)/shard_map/ppermute | solution.py:388
  44.2 8.3 %collective-permute-start.4 = (f32[192,128]{1,0:T(8,128)S(1)}, f32[192,128]{1,0:T(8,128)S(1)}, u32[]{:S(2)}, u32[]{:S(2)}) collective-permute-start(f32[192,128]{1,0:T(8,128)S(1)} %add.87), channel_id=1, source_target_pairs={{0,4},{1,5},{2,6},{3,7},{4,0},{5,1},{6,2},{7,3},{8,12},{9,13},{10,... | collective-permute-start | bytes 294920 | tf_op jit(solution)/shard_map/ppermute | solution.py:388
  48.1 4.5 %collective-permute-start.10 = (f32[192,128]{1,0:T(8,128)S(1)}, f32[192,128]{1,0:T(8,128)S(1)}, u32[]{:S(2)}, u32[]{:S(2)}) collective-permute-start(f32[192,128]{1,0:T(8,128)S(1)} %add.91), channel_id=1, source_target_pairs={{0,64},{32,96},{64,0},{96,32},{128,192},{160,224},{192,128},{224,1... | collective-permute-start | bytes 294920 | tf_op jit(solution)/shard_map/ppermute | solution.py:388
  52.5 3.6 %collective-permute-start.5 = (f32[192,128]{1,0:T(8,128)S(1)}, f32[192,128]{1,0:T(8,128)S(1)}, u32[]{:S(2)}, u32[]{:S(2)}) collective-permute-start(f32[192,128]{1,0:T(8,128)S(1)} %add.88), channel_id=1, source_target_pairs={{0,8},{1,9},{2,10},{3,11},{4,12},{5,13},{6,14},{7,15},{8,0},{9,1},... | collective-permute-start | bytes 294920 | tf_op jit(solution)/shard_map/ppermute | solution.py:388
  52.7 6.3 %collective-permute-start.11 = (f32[192,128]{1,0:T(8,128)S(1)}, f32[192,128]{1,0:T(8,128)S(1)}, u32[]{:S(2)}, u32[]{:S(2)}) collective-permute-start(f32[192,128]{1,0:T(8,128)S(1)} %add.92), channel_id=1, source_target_pairs={{0,128},{32,160},{64,192},{96,224},{128,0},{160,32},{192,64},{224,... | collective-permute-start | bytes 294920 | tf_op jit(solution)/shard_map/ppermute | solution.py:388
  56.1 5.1 %collective-permute-start.6 = (f32[192,128]{1,0:T(8,128)S(1)}, f32[192,128]{1,0:T(8,128)S(1)}, u32[]{:S(2)}, u32[]{:S(2)}) collective-permute-start(f32[192,128]{1,0:T(8,128)S(1)} %add.89), channel_id=1, source_target_pairs={{0,16},{1,17},{2,18},{3,19},{4,20},{5,21},{6,22},{7,23},{8,24},{9,... | collective-permute-start | bytes 294920 | tf_op jit(solution)/shard_map/ppermute | solution.py:388
  59.0 6.9 %copy-start.1 = (f32[192,128]{1,0:T(8,128)}, f32[192,128]{1,0:T(8,128)S(1)}, u32[]{:S(2)}) copy-start(f32[192,128]{1,0:T(8,128)S(1)} %add.93.gu_mine) | copy-start | bytes 294916
  59.0 6.9 %collective-permute-start.12 = (f32[192,128]{1,0:T(8,128)S(1)}, f32[192,128]{1,0:T(8,128)S(1)}, u32[]{:S(2)}, u32[]{:S(2)}) collective-permute-start(f32[192,128]{1,0:T(8,128)S(1)} %add.93.gu_mine), channel_id=1, source_target_pairs={{0,32},{32,0},{64,96},{96,64},{128,160},{160,128},{192,224},{224,1... | collective-permute-start | bytes 294920 | tf_op jit(solution)/shard_map/ppermute | solution.py:388
  61.2 4.7 %copy-start.2 = (f32[192,128]{1,0:T(8,128)}, f32[192,128]{1,0:T(8,128)S(1)}, u32[]{:S(2)}) copy-start(f32[192,128]{1,0:T(8,128)S(1)} %add.90.gv_mine) | copy-start | bytes 294916
  61.2 4.7 %collective-permute-start.7 = (f32[192,128]{1,0:T(8,128)S(1)}, f32[192,128]{1,0:T(8,128)S(1)}, u32[]{:S(2)}, u32[]{:S(2)}) collective-permute-start(f32[192,128]{1,0:T(8,128)S(1)} %add.90.gv_mine), channel_id=1, source_target_pairs={{0,32},{32,0},{64,96},{96,64},{128,160},{160,128},{192,224},{224,1... | collective-permute-start | bytes 294920 | tf_op jit(solution)/shard_map/ppermute | solution.py:388
  65.9 0.6 copy-start.4
  66.6 0.6 copy-start.5
  88.3 8.0 %collective-permute-start.13 = (f32[64,4096]{1,0:T(8,128)}, f32[64,4096]{1,0:T(8,128)S(1)}, u32[]{:S(2)}, u32[]{:S(2)}) collective-permute-start(f32[64,4096]{1,0:T(8,128)} %next_v.1), channel_id=1, source_target_pairs={{0,32},{32,0},{64,96},{96,64},{128,160},{160,128},{192,224},{224,1... | collective-permute-start | bytes 3145736 | tf_op jit(solution)/shard_map/ppermute | solution.py:388
  88.3 8.0 %copy-start = (f32[64,4096]{1,0:T(8,128)S(1)}, f32[64,4096]{1,0:T(8,128)}, u32[]{:S(2)}) copy-start(f32[64,4096]{1,0:T(8,128)} %next_v.1) | copy-start | bytes 3145732

commit v2 on v1

--- a/solution.py
+++ b/solution.py
@@ -17,7 +17,7 @@
 BF16 = jnp.bfloat16
 NT = (((1,), (1,)), ((), ()))
 NN = (((1,), (0,)), ((), ()))
-VMEM_LIMIT = 56 * 1024 * 1024
+VMEM_LIMIT = 14 * 1024 * 1024
 
 
 def smem():
@@ -168,9 +168,10 @@
     )(core, offsets, v, v, v, halo, weights)
 
 
-def gram_u_kernel(steps, scale, core_ref, u_ref, before_ref, after_ref, left_ref, right_ref, m_ref, d_ref,
-                  mine_ref, other_ref, wide_hi, wide_lo,
-                  hi_a, lo_a, hi_b, lo_b, hh_ref, hl_ref, pack_ref):
+def gram_u_kernel(part_at, parts, steps, scale, core_ref, u_ref, before_ref, after_ref, left_ref, right_ref, m_ref, d_ref, *refs):
+    if part_at > 0:
+        had_mine, had_other, *refs = refs
+    mine_ref, other_ref, hi_a, lo_a, hi_b, lo_b, hh_ref, hl_ref, pack_ref = refs
     step = pl.program_id(0)
     chunks = u_ref.shape[1] // LANES
     part = chunks // 2
@@ -179,8 +180,11 @@
     def _():
         start_gram(hi_b, lo_b, hh_ref, hl_ref)
 
-    before = jnp.where(step == 0, left_ref[...], before_ref[...])
-    after = jnp.where(step == steps - 1, right_ref[...], after_ref[...])
+    before, after = before_ref[...], after_ref[...]
+    if part_at == 0:
+        before = jnp.where(step == 0, left_ref[...], before)
+    if part_at == parts - 1:
+        after = jnp.where(step == steps - 1, right_ref[...], after)
     cells = [before] + [u_ref[:, c * LANES:(c + 1) * LANES] for c in range(chunks)] + [after]
     add_gram(hi_b, lo_b, hh_ref, hl_ref)
     for half, hi_ref, lo_ref in ((0, hi_a, lo_a), (1, hi_b, lo_b)):
@@ -192,8 +196,10 @@
             down = shift_right(cells[c], cells[c + 1], 1)
             lap = up - 2.0 * cells[c + 1] + down
             for k in range(STENCILS):
-                total = m_ref[k:k + 1, at] * cells[c + 1] + d_ref[k:k + 1, at] * lap
-                keep_wide(total, k, near, at, hi_ref, lo_ref, wide_hi, wide_lo)
+                rows = slice(k * RANK, (k + 1) * RANK)
+                hi, lo = split(m_ref[k:k + 1, at] * cells[c + 1] + d_ref[k:k + 1, at] * lap)
+                hi_ref[rows, near] = hi
+                lo_ref[rows, near] = lo
         if half == 0:
             add_gram(hi_a, lo_a, hh_ref, hl_ref)
 
@@ -201,37 +207,42 @@
     def _():
         add_gram(hi_b, lo_b, hh_ref, hl_ref)
         finish_gram(hh_ref, hl_ref, pack_ref, scale, core_ref[0], mine_ref, other_ref)
-
-
-def gram_u(core, u, left, right, mass, diffusion, scale):
+        if part_at > 0:
+            mine_ref[...] += had_mine[...]
+            other_ref[...] += had_other[...]
+
+
+def gram_u(core, part_at, parts, u, left, right, mass, diffusion, scale, had=()):
     cells = u.shape[1]
-    tile = min(1024, cells)
-    steps = cells // tile
+    tile = min(1024, cells // parts)
+    steps = cells // parts // tile
+    first = part_at * steps
     ratio = tile // LANES
     last = cells // LANES - 1
-    table = pl.BlockSpec((STENCILS, tile), lambda i, *_: (0, i))
+    table = pl.BlockSpec((STENCILS, tile), lambda i, *_: (0, first + i))
+    packed = pl.BlockSpec((192, LANES), lambda i, *_: (0, 0))
     spec = pltpu.PrefetchScalarGridSpec(
         num_scalar_prefetch=1,
         grid=(steps,),
         in_specs=[
-            pl.BlockSpec((RANK, tile), lambda i, *_: (0, i)),
-            pl.BlockSpec((RANK, LANES), lambda i, *_: (0, jnp.maximum(i * ratio - 1, 0))),
-            pl.BlockSpec((RANK, LANES), lambda i, *_: (0, jnp.minimum((i + 1) * ratio, last))),
+            pl.BlockSpec((RANK, tile), lambda i, *_: (0, first + i)),
+            pl.BlockSpec((RANK, LANES), lambda i, *_: (0, jnp.maximum((first + i) * ratio - 1, 0))),
+            pl.BlockSpec((RANK, LANES), lambda i, *_: (0, jnp.minimum((first + i + 1) * ratio, last))),
             pl.BlockSpec((RANK, LANES), lambda i, *_: (0, 0)),
             pl.BlockSpec((RANK, LANES), lambda i, *_: (0, 0)),
             table,
             table,
-        ],
-        out_specs=[pl.BlockSpec((192, LANES), lambda i, *_: (0, 0))] * 2 + [pl.BlockSpec((WIDE, tile), lambda i, *_: (0, i))] * 2,
+        ] + [packed] * len(had),
+        out_specs=[packed] * 2,
         scratch_shapes=gram_scratch(tile // 2),
     )
     return pl.pallas_call(
-        functools.partial(gram_u_kernel, steps, scale),
+        functools.partial(gram_u_kernel, part_at, parts, steps, scale),
         grid_spec=spec,
-        out_shape=[jax.ShapeDtypeStruct((192, LANES), F32)] * 2 + [jax.ShapeDtypeStruct((WIDE, cells), BF16)] * 2,
+        out_shape=[jax.ShapeDtypeStruct((192, LANES), F32)] * 2,
         compiler_params=pltpu.CompilerParams(vmem_limit_bytes=VMEM_LIMIT),
-        name="gram_u",
-    )(core, u, u, u, left, right, mass, diffusion)
+        name="gram_u" + str(part_at),
+    )(core, u, u, u, left, right, mass, diffusion, *had)
 
 
 def lower_inverse(square):
@@ -277,6 +288,11 @@
     full_ref[128:256, 0:128] = g10
     full_ref[0:128, 128:256] = g10.T
     full_ref[128:256, 128:256] = high[64:192]
+
+
+def three(x):
+    hi, lo = split(x)
+    return jnp.concatenate([hi, hi, lo], axis=1)
 
 
 def put_split(ref, x):
@@ -323,7 +339,9 @@
     lower = full_dot(inner, inverse_c, NT)
     keep = lax.broadcasted_iota(jnp.int32, lower.shape, 0) >= lane_iota(lower.shape)
     next_ref[...] = jnp.where(keep, lower, 0.0)
-    put_split(mu_ref, map_u)
+    for k in range(STENCILS):
+        at = slice(k * RANK, (k + 1) * RANK)
+        mu_ref[at, :] = three(map_u[:, at])
     put_split(mv_ref, map_v)
 
 
@@ -333,7 +351,7 @@
         in_specs=[smem()] + [vmem()] * 6,
         out_specs=[vmem()] * 3,
         out_shape=[
-            jax.ShapeDtypeStruct((2 * RANK, WIDE), BF16),
+            jax.ShapeDtypeStruct((WIDE, 3 * RANK), BF16),
             jax.ShapeDtypeStruct((2 * RANK, WIDE), BF16),
             jax.ShapeDtypeStruct((RANK, RANK), F32),
         ],
@@ -371,6 +389,69 @@
     )(maps, wide_hi, wide_lo)
 
 
+def next_u_kernel(steps, u_ref, before_ref, after_ref, left_ref, right_ref, m_ref, d_ref, d_before, d_after, map_ref, out_ref,
+                  stack, p_ref):
+    step = pl.program_id(0)
+    chunks = u_ref.shape[1] // LANES
+    before = jnp.where(step == 0, left_ref[...], before_ref[...])
+    after = jnp.where(step == steps - 1, right_ref[...], after_ref[...])
+    cells = [before] + [u_ref[:, c * LANES:(c + 1) * LANES] for c in range(chunks)] + [after]
+    for c in range(chunks + 2):
+        at = slice(c * LANES, (c + 1) * LANES)
+        hi, lo = split(cells[c])
+        stack[0:RANK, at] = hi
+        stack[RANK:2 * RANK, at] = lo
+        stack[2 * RANK:3 * RANK, at] = hi
+    p_ref[...] = fast_dot(map_ref[...], stack[...], NN)
+    d = [d_before[...]] + [d_ref[:, c * LANES:(c + 1) * LANES] for c in range(chunks)] + [d_after[...]]
+
+    def weighted(c, table):
+        total = None
+        for k in range(STENCILS):
+            term = table[k:k + 1, :] * p_ref[k * RANK:(k + 1) * RANK, c * LANES:(c + 1) * LANES]
+            total = term if total is None else total + term
+        return total
+
+    pull = [None] + [weighted(c, shift_right(d[c - 1], d[c], 1)) for c in range(1, chunks + 2)]
+    push = [weighted(c, shift_left(d[c], d[c + 1], 1)) for c in range(chunks + 1)]
+    for c in range(1, chunks + 1):
+        at = slice((c - 1) * LANES, c * LANES)
+        near = weighted(c, m_ref[:, at] - 2.0 * d[c])
+        out_ref[:, at] = near + (shift_left(pull[c], pull[c + 1], 1) + shift_right(push[c - 1], push[c], 1))
+
+
+def next_u(u, left, right, mass, diffusion, maps):
+    cells = u.shape[1]
+    tile = min(1024, cells)
+    steps = cells // tile
+    ratio = tile // LANES
+    last = cells // LANES - 1
+    table = pl.BlockSpec((STENCILS, tile), lambda i: (0, i))
+    low = lambda i: (0, jnp.maximum(i * ratio - 1, 0))
+    high = lambda i: (0, jnp.minimum((i + 1) * ratio, last))
+    return pl.pallas_call(
+        functools.partial(next_u_kernel, steps),
+        grid=(steps,),
+        in_specs=[
+            pl.BlockSpec((RANK, tile), lambda i: (0, i)),
+            pl.BlockSpec((RANK, LANES), low),
+            pl.BlockSpec((RANK, LANES), high),
+            pl.BlockSpec((RANK, LANES), lambda i: (0, 0)),
+            pl.BlockSpec((RANK, LANES), lambda i: (0, 0)),
+            table,
+            table,
+            pl.BlockSpec((STENCILS, LANES), low),
+            pl.BlockSpec((STENCILS, LANES), high),
+            pl.BlockSpec((WIDE, 3 * RANK), lambda i: (0, 0)),
+        ],
+        out_specs=pl.BlockSpec((RANK, tile), lambda i: (0, i)),
+        out_shape=jax.ShapeDtypeStruct((RANK, cells), F32),
+        scratch_shapes=[pltpu.VMEM((3 * RANK, tile + 2 * LANES), BF16), pltpu.VMEM((WIDE, tile + 2 * LANES), F32)],
+        compiler_params=pltpu.CompilerParams(vmem_limit_bytes=VMEM_LIMIT),
+        name="next_u",
+    )(u, u, u, left, right, mass, diffusion, diffusion, diffusion, maps)
+
+
 def make_sketch_t(sketch_seed, wide, rank):
     shape = (wide // rank, rank, rank)
     rows_idx = lax.broadcasted_iota(jnp.int32, shape, 0) * rank + lax.broadcasted_iota(jnp.int32, shape, 2)
@@ -393,32 +474,32 @@
     at_gx = lax.axis_index("gx")
     core = (at_gx % 2).astype(jnp.int32).reshape(1)
     even = core[0] == 0
-    at_pa = lax.axis_index("pa")
-    edge_u = jnp.where(even, u[:, :LANES], u[:, -LANES:])
-    edge_v = jnp.where(even, v[:, :LANES], v[:, -LANES:])
     pairs = []
     for g in range(gx):
         for p in range(pa):
-            if g % 2 == 0:
-                pairs.append((g * pa + p, (g - 1) % gx * pa + (p - 1) % pa))
-            else:
-                pairs.append((g * pa + p, (g + 1) % gx * pa + (p + 1) % pa))
-    far = lax.ppermute(jnp.concatenate([edge_u, edge_v], axis=0), ("gx", "pa"), pairs)
-    out_u = jnp.logical_or(at_gx == 0, at_gx == gx - 1)
-    out_v = at_pa == jnp.where(even, 0, pa - 1)
-    far_u = jnp.where(out_u, 0.0, far[:RANK])
-    far_v = jnp.where(out_v, 0.0, far[RANK:])
+            q = p + 1 if g % 2 == 0 else p - 1
+            if 0 <= q < pa:
+                pairs.append((g * pa + p, g * pa + q))
+    edge_v = jnp.where(even, v[:, -LANES:], v[:, :LANES])
+    halo_v = lax.ppermute(edge_v, ("gx", "pa"), pairs)
+    onehot = (material_index[:, None, :] == jnp.arange(mass_table.shape[1], dtype=jnp.int32)[None, :, None]).astype(F32)
+    mass = jnp.sum(mass_table[:, :, None] * onehot, axis=1)
+    diffusion = jnp.sum(diffusivity_table[:, :, None] * onehot, axis=1)
+    sketch_t = make_sketch_t(sketch_seed, WIDE, RANK)
+    v_in, mass, diffusion, sketch_t = lax.optimization_barrier((v, mass, diffusion, sketch_t))
     weights = jnp.transpose(weights, (1, 0, 2))
-    gv_mine, gv_other, hi_v, lo_v = gram_v(core, offsets, v, far_v, weights, 1.0 / (v.shape[1] * pa))
+    gv_mine, gv_other, hi_v, lo_v = gram_v(core, offsets, v_in, halo_v, weights, 1.0 / (v.shape[1] * pa))
+    gv = gv_mine + swap(gv_other, "gx", 1)
+
+    u_pairs = [(i, i - 1 if i % 2 == 0 else i + 1) for i in range(gx)]
+    far_u = lax.ppermute(jnp.where(even, u[:, :LANES], u[:, -LANES:]), "gx", [(i, j) for i, j in u_pairs if 0 <= j < gx])
     near_u = swap(jnp.where(even, u[:, -LANES:], u[:, :LANES]), "gx", 1)
     left_u = jnp.where(even, far_u, near_u)
     right_u = jnp.where(even, near_u, far_u)
-    onehot = (material_index[:, None, :] == jnp.arange(mass_table.shape[1], dtype=jnp.int32)[None, :, None]).astype(F32)
-    mass = jnp.sum(mass_table[:, :, None] * onehot, axis=1)
-    diffusion = jnp.sum(diffusivity_table[:, :, None] * onehot, axis=1)
-    gu_mine, gu_other, hi_u, lo_u = gram_u(core, u, left_u, right_u, mass, diffusion, 1.0 / (u.shape[1] * gx))
-
-    gv = gv_mine + swap(gv_other, "gx", 1)
+    u_scale = 1.0 / (u.shape[1] * gx)
+    had = gram_u(core, 0, 2, u, left_u, right_u, mass, diffusion, u_scale)
+    gu_mine, gu_other = gram_u(core, 1, 2, u, left_u, right_u, mass, diffusion, u_scale, had)
+
     bit = 1
     while bit < pa:
         gv = gv + swap(gv, "pa", bit)
@@ -430,11 +511,10 @@
         bit *= 2
     gv_far = swap(gv, "gx", 1)
     gu_far = swap(gu, "gx", 1)
-    sketch_t = make_sketch_t(sketch_seed, WIDE, RANK)
     map_u, map_v, core_next = chain(core, gv, gv_far, gu, gu_far, sketch_t, core_matrix)
     half = next_factor("next_v", map_v, hi_v, lo_v)
     half_far = swap(half, "gx", 1)
-    u_next = next_factor("next_u", map_u, hi_u, lo_u)
+    u_next = next_u(u, left_u, right_u, mass, diffusion, map_u)
     v_next = jnp.concatenate([jnp.where(even, half, half_far), jnp.where(even, half_far, half)], axis=1)
     return (u_next, v_next, core_next)
 

time: 99.1 us -> 84.8 us (0.86)
  Pallas kernels: 47.7 us -> 35.4 us
  other arithmetic: 8.51 us -> 4.94 us
  waiting for transfers between devices: 9.91 us -> 7.2 us
  starting transfers between devices: 29 us -> 31.2 us
  local copies, waits for them, and re-layouts: 1.26 us -> 3.28 us
    pallas_call x2 -> x1, Pallas kernels: 12.4 us -> 1.6 us  [next_factor(): pl.pallas_call(next_kernel, grid=(cells // tile,), in_specs=[pl.BlockSpec...]
    ppermute x13, waiting for transfers between devices: 9.91 us -> 5.9 us  [swap(): lax.ppermute(x, axis, [(i, i ^ bit) for i in range(lax.axis_size(axis))])]
    unnamed x16 -> x10, local copies, waits for them, and re-layouts: 1.26 us -> 3.28 us
    ppermute x13, starting transfers between devices: 24.9 us -> 26.8 us  [swap(): lax.ppermute(x, axis, [(i, i ^ bit) for i in range(lax.axis_size(axis))])]
    pallas_call x1, Pallas kernels: 8.43 us -> 6.61 us  [gram_v(): pl.pallas_call(functools.partial(gram_v_kernel, steps, scale), grid_spec=...]
    pallas_call x1 -> x3, Pallas kernels: 10.3 us -> 11.7 us  [the longest x1 5.89 us: next_u(): pl.pallas_call(functools.partial(next_u_kernel, steps), grid=(steps,), in...]
    ppermute x1 -> x2, waiting for transfers between devices: 0.01 us -> 1.3 us  [the longest x1 1.3 us: local(): halo_v = lax.ppermute(edge_v, ('gx', 'pa'), pairs)]
    pallas_call x1, Pallas kernels: 16.6 us -> 15.5 us  [chain(): pl.pallas_call(chain_kernel, in_specs=[smem()] + [vmem()] * 6, out_specs=...]
  transfers between devices with their start and end apart: 14 -> 15, of which waited for: 5 -> 5; matrix products, arithmetic and copies ran while one was open for 4% -> 3% of each run, Pallas kernels for 19% -> 14%
where the time goes in v2:
time: 84.8 us; the launch traced here: 83.5 us
  Pallas kernels  35.4 us (42%)
  starting transfers between devices  31.2 us (37%)
  waiting for transfers between devices  7.2 us (8%)
  other arithmetic  4.94 us (6%)
  local copies, waits for them, and re-layouts  3.28 us (4%)
  between operations  1.45 us (2%)
    ppermute x13, starting transfers between devices, swap(): lax.ppermute(x, axis, [(i, i ^ bit) for i in range(lax.axis_size(axis))])  26.8 us
    pallas_call x1, Pallas kernels, chain(): pl.pallas_call(chain_kernel, in_specs=[smem()] + [vmem()] * 6, out_specs=...  15.5 us
    pallas_call x1, Pallas kernels, gram_v(): pl.pallas_call(functools.partial(gram_v_kernel, steps, scale), grid_spec=...  6.61 us
    ppermute x13, waiting for transfers between devices, swap(): lax.ppermute(x, axis, [(i, i ^ bit) for i in range(lax.axis_size(axis))])  5.9 us
    pallas_call x1, Pallas kernels, next_u(): pl.pallas_call(functools.partial(next_u_kernel, steps), grid=(steps,), in...  5.89 us
    pallas_call x2, Pallas kernels, gram_u(): pl.pallas_call(functools.partial(gram_u_kernel, part_at, parts, steps, sc...  5.84 us
    unnamed x10, local copies, waits for them, and re-layouts  3.28 us
    ppermute x1, starting transfers between devices, local(): lax.ppermute(jnp.where(even, u[:, :LANES], u[:, -LANES:]), 'gx', [(i, j)...  3.11 us
  transfers between devices with their start and end apart: 15, of which 5 were waited for; matrix products, arithmetic and copies ran while one was open for 3% of the time, Pallas kernels for 14%

profile of v2, /device:TPU:1, one launch (start us, length us, event | category | flops | bytes accessed | tf_op | source)
XLA Modules:
  0.0 83.5 jit_solution(15723601612339399222)
XLA Ops:
  0.6 0.8 slice_select_fusion
  1.4 1.3 %collective-permute-start.2 = (f32[64,128]{1,0:T(8,128)S(1)}, f32[64,128]{1,0:T(8,128)S(1)}, u32[]{:S(2)}, u32[]{:S(2)}) collective-permute-start(f32[64,128]{1,0:T(8,128)S(1)} %slice_select_fusion), channel_id=1, source_target_pairs={{0,1},{1,2},{2,3},{3,4},{4,5},{5,6},{6,7},{7,8},{8,9},{9,10},{10,1... | collective-permute-start | bytes 98312 | tf_op jit(solution)/shard_map/ppermute | solution.py:484
  3.4 0.5 fusion.10.sketch_ref
  3.9 1.9 %select_reduce_fusion = (f32[4,8192]{1,0:T(4,128)S(1)}, f32[4,8192]{1,0:T(4,128)S(1)}) fusion(f32[4,16]{1,0:T(4,128)} %param.12, s32[4,8192]{1,0:T(4,128)} %param.13, f32[4,16]{1,0:T(4,128)} %param.11), kind=kLoop, calls=%fused_computation.1 | loop fusion | flops 2555904 | bytes 393728 | tf_op jit(solution)/shard_map/reduce_sum | solution.py:487
  5.8 1.3 %collective-permute-done.2.halo_ref = f32[64,128]{1,0:T(8,128)S(1)} collective-permute-done((f32[64,128]{1,0:T(8,128)S(1)}, f32[64,128]{1,0:T(8,128)S(1)}, u32[]{:S(2)}, u32[]{:S(2)}) %collective-permute-start.2) | collective-permute-done | bytes 32800 | tf_op jit(solution)/shard_map/ppermute | solution.py:484
  7.1 0.0 copy-start.1
  7.1 1.6 %copy-done.1 = f32[64,8192]{1,0:T(8,128)S(1)} copy-done((f32[64,8192]{1,0:T(8,128)S(1)}, f32[64,8192]{1,0:T(8,128)}, u32[]{:S(2)}) %copy-start.1) | copy-done | bytes 2097176
  8.7 0.0 copy-start.2
  8.7 1.0 %copy-done.2 = f32[4,3,8192]{2,0,1:T(4,128)S(1)} copy-done((f32[4,3,8192]{2,0,1:T(4,128)S(1)}, f32[4,3,8192]{2,0,1:T(4,128)}, u32[]{:S(2)}) %copy-start.2) | copy-done | bytes 393240
  9.7 0.0 copy-start.4
  9.7 0.7 copy-done.4
  10.3 0.0 copy-start
  10.3 6.6 %gram_v.1 = (f32[192,128]{1,0:T(8,128)S(1)}, f32[192,128]{1,0:T(8,128)S(1)}, bf16[256,4096]{1,0:T(8,128)(2,1)S(1)}, bf16[256,4096]{1,0:T(8,128)(2,1)S(1)}) custom-call(s32[1]{0:T(128)} %bitcast.1.core_ref, s32[4,3]{1,0:T(4,128)S(1)} %copy-done.4, f32[64,8192]{1,0:T(8,128)S(1)} %copy-done.1, f32[64,8192]{1,0:T(8,128)S(1)} %copy-done.1, ...), custom_call_target="tpu_custom_call" | custom-call | tf_op jit(solution)/shard_map/gram_v/pallas_call | solution.py:162
  17.0 2.8 %collective-permute-start.3 = (f32[192,128]{1,0:T(8,128)S(1)}, f32[192,128]{1,0:T(8,128)S(1)}, u32[]{:S(2)}, u32[]{:S(2)}) collective-permute-start(f32[192,128]{1,0:T(8,128)S(1)} %get-tuple-element.22), channel_id=1, source_target_pairs={{0,32},{32,0},{64,96},{96,64},{128,160},{160,128},{192,224},{224,1... | collective-permute-start | bytes 294920 | tf_op jit(solution)/shard_map/ppermute | solution.py:469
  19.8 0.9 %collective-permute-done.3 = f32[192,128]{1,0:T(8,128)S(1)} collective-permute-done((f32[192,128]{1,0:T(8,128)S(1)}, f32[192,128]{1,0:T(8,128)S(1)}, u32[]{:S(2)}, u32[]{:S(2)}) %collective-permute-start.3) | collective-permute-done | bytes 98336 | tf_op jit(solution)/shard_map/ppermute | solution.py:469
  20.8 1.7 %collective-permute-start.4 = (f32[192,128]{1,0:T(8,128)S(1)}, f32[192,128]{1,0:T(8,128)S(1)}, u32[]{:S(2)}, u32[]{:S(2)}) collective-permute-start(f32[192,128]{1,0:T(8,128)S(1)} %add.99), channel_id=1, source_target_pairs={{0,1},{1,0},{2,3},{3,2},{4,5},{5,4},{6,7},{7,6},{8,9},{9,8},{10,11... | collective-permute-start | bytes 294920 | tf_op jit(solution)/shard_map/ppermute | solution.py:469
  22.5 0.0 copy-done
  22.5 0.7 collective-permute-start.1
  23.2 3.1 %collective-permute-start = (f32[64,128]{1,0:T(8,128)S(1)}, f32[64,128]{1,0:T(8,128)S(1)}, u32[]{:S(2)}, u32[]{:S(2)}) collective-permute-start(f32[64,128]{1,0:T(8,128)S(1)} %get-tuple-element.38), channel_id=1, source_target_pairs={{32,64},{64,32},{96,128},{128,96},{160,192},{192,160},{33,65},{65,... | collective-permute-start | bytes 98312 | tf_op jit(solution)/shard_map/ppermute | solution.py:495
  26.3 0.0 collective-permute-done.4
  26.4 4.3 %collective-permute-start.5 = (f32[192,128]{1,0:T(8,128)S(1)}, f32[192,128]{1,0:T(8,128)S(1)}, u32[]{:S(2)}, u32[]{:S(2)}) collective-permute-start(f32[192,128]{1,0:T(8,128)S(1)} %add.100), channel_id=1, source_target_pairs={{0,2},{1,3},{2,0},{3,1},{4,6},{5,7},{6,4},{7,5},{8,10},{9,11},{10,... | collective-permute-start | bytes 294920 | tf_op jit(solution)/shard_map/ppermute | solution.py:469
  30.6 0.0 collective-permute-done.1
  30.6 0.0 collective-permute-done
  30.7 2.9 %gram_u0.1 = (f32[192,128]{1,0:T(8,128)S(1)}, f32[192,128]{1,0:T(8,128)S(1)}) custom-call(s32[1]{0:T(128)} %bitcast.1.core_ref, f32[64,8192]{1,0:T(8,128)S(1)} %copy-done, f32[64,8192]{1,0:T(8,128)S(1)} %copy-done, f32[64,8192]{1,0:T(8,128)S(1)} %copy-done, f32[64,128]{1,0:T(8,128)S(1)} %get-tuple-element.40.left_ref, ...), custom_call_target="tpu_custom_call" | custom-call | tf_op jit(solution)/shard_map/gram_u0/pallas_call | solution.py:239
  33.6 0.0 copy-start.3
  33.6 2.9 %gram_u1.1 = (f32[192,128]{1,0:T(8,128)S(1)}, f32[192,128]{1,0:T(8,128)S(1)}) custom-call(s32[1]{0:T(128)} %bitcast.1.core_ref, f32[64,8192]{1,0:T(8,128)S(1)} %copy-done, f32[64,8192]{1,0:T(8,128)S(1)} %copy-done, f32[64,8192]{1,0:T(8,128)S(1)} %copy-done, f32[64,128]{1,0:T(8,128)S(1)} %get-tuple-element.40.left_ref, ...), custom_call_target="tpu_custom_call" | custom-call | tf_op jit(solution)/shard_map/gram_u1/pallas_call | solution.py:239
  36.5 0.2 collective-permute-start.10
  36.7 0.0 collective-permute-done.5
  36.8 2.9 %collective-permute-start.6 = (f32[192,128]{1,0:T(8,128)S(1)}, f32[192,128]{1,0:T(8,128)S(1)}, u32[]{:S(2)}, u32[]{:S(2)}) collective-permute-start(f32[192,128]{1,0:T(8,128)S(1)} %add.101), channel_id=1, source_target_pairs={{0,4},{1,5},{2,6},{3,7},{4,0},{5,1},{6,2},{7,3},{8,12},{9,13},{10,... | collective-permute-start | bytes 294920 | tf_op jit(solution)/shard_map/ppermute | solution.py:469
  39.7 0.0 collective-permute-done.10
  39.7 1.5 %collective-permute-start.11 = (f32[192,128]{1,0:T(8,128)S(1)}, f32[192,128]{1,0:T(8,128)S(1)}, u32[]{:S(2)}, u32[]{:S(2)}) collective-permute-start(f32[192,128]{1,0:T(8,128)S(1)} %add.105), channel_id=1, source_target_pairs={{0,64},{32,96},{64,0},{96,32},{128,192},{160,224},{192,128},{224,1... | collective-permute-start | bytes 294920 | tf_op jit(solution)/shard_map/ppermute | solution.py:469
  41.2 3.6 %collective-permute-done.6 = f32[192,128]{1,0:T(8,128)S(1)} collective-permute-done((f32[192,128]{1,0:T(8,128)S(1)}, f32[192,128]{1,0:T(8,128)S(1)}, u32[]{:S(2)}, u32[]{:S(2)}) %collective-permute-start.6) | collective-permute-done | bytes 98336 | tf_op jit(solution)/shard_map/ppermute | solution.py:469
  44.8 1.3 %collective-permute-start.7 = (f32[192,128]{1,0:T(8,128)S(1)}, f32[192,128]{1,0:T(8,128)S(1)}, u32[]{:S(2)}, u32[]{:S(2)}) collective-permute-start(f32[192,128]{1,0:T(8,128)S(1)} %add.102), channel_id=1, source_target_pairs={{0,8},{1,9},{2,10},{3,11},{4,12},{5,13},{6,14},{7,15},{8,0},{9,1},... | collective-permute-start | bytes 294920 | tf_op jit(solution)/shard_map/ppermute | solution.py:469
  46.1 0.0 collective-permute-done.11
  46.1 3.3 %collective-permute-start.12 = (f32[192,128]{1,0:T(8,128)S(1)}, f32[192,128]{1,0:T(8,128)S(1)}, u32[]{:S(2)}, u32[]{:S(2)}) collective-permute-start(f32[192,128]{1,0:T(8,128)S(1)} %add.106), channel_id=1, source_target_pairs={{0,128},{32,160},{64,192},{96,224},{128,0},{160,32},{192,64},{224,... | collective-permute-start | bytes 294920 | tf_op jit(solution)/shard_map/ppermute | solution.py:469
  49.4 0.0 collective-permute-done.7
  49.4 2.5 %collective-permute-start.8 = (f32[192,128]{1,0:T(8,128)S(1)}, f32[192,128]{1,0:T(8,128)S(1)}, u32[]{:S(2)}, u32[]{:S(2)}) collective-permute-start(f32[192,128]{1,0:T(8,128)S(1)} %add.103), channel_id=1, source_target_pairs={{0,16},{1,17},{2,18},{3,19},{4,20},{5,21},{6,22},{7,23},{8,24},{9,... | collective-permute-start | bytes 294920 | tf_op jit(solution)/shard_map/ppermute | solution.py:469
  51.8 0.0 collective-permute-done.12
  51.9 2.2 %collective-permute-start.13 = (f32[192,128]{1,0:T(8,128)S(1)}, f32[192,128]{1,0:T(8,128)S(1)}, u32[]{:S(2)}, u32[]{:S(2)}) collective-permute-start(f32[192,128]{1,0:T(8,128)S(1)} %add.107.gu_mine), channel_id=1, source_target_pairs={{0,32},{32,0},{64,96},{96,64},{128,160},{160,128},{192,224},{224,1... | collective-permute-start | bytes 294920 | tf_op jit(solution)/shard_map/ppermute | solution.py:469
  54.0 0.4 collective-permute-done.8
  54.5 3.0 %collective-permute-start.9 = (f32[192,128]{1,0:T(8,128)S(1)}, f32[192,128]{1,0:T(8,128)S(1)}, u32[]{:S(2)}, u32[]{:S(2)}) collective-permute-start(f32[192,128]{1,0:T(8,128)S(1)} %add.104.gv_mine), channel_id=1, source_target_pairs={{0,32},{32,0},{64,96},{96,64},{128,160},{160,128},{192,224},{224,1... | collective-permute-start | bytes 294920 | tf_op jit(solution)/shard_map/ppermute | solution.py:469
  57.5 0.0 collective-permute-done.13.gu_other
  57.5 0.9 %collective-permute-done.9.gv_other = f32[192,128]{1,0:T(8,128)S(1)} collective-permute-done((f32[192,128]{1,0:T(8,128)S(1)}, f32[192,128]{1,0:T(8,128)S(1)}, u32[]{:S(2)}, u32[]{:S(2)}) %collective-permute-start.9) | collective-permute-done | bytes 98336 | tf_op jit(solution)/shard_map/ppermute | solution.py:469
  58.4 0.0 copy-done.3
  58.4 15.5 %chain.1 = (bf16[256,192]{1,0:T(8,128)(2,1)S(1)}, bf16[128,256]{1,0:T(8,128)(2,1)S(1)}, f32[64,64]{1,0:T(8,128)}) custom-call(s32[1]{0:T(128)} %bitcast.1.core_ref, f32[192,128]{1,0:T(8,128)S(1)} %add.104.gv_mine, f32[192,128]{1,0:T(8,128)S(1)} %collective-permute-done.9.gv_other, f32[192,128]{1,0:T(8,128)S(1)} %add.107.gu_mine, ...), custom_call_target="tpu_custom_call" | custom-call | tf_op jit(solution)/shard_map/chain/pallas_call | solution.py:349
  73.9 1.6 %next_v.1 = f32[64,4096]{1,0:T(8,128)S(1)} custom-call(bf16[128,256]{1,0:T(8,128)(2,1)S(1)} %get-tuple-element.29.map_ref, bf16[256,4096]{1,0:T(8,128)(2,1)S(1)} %get-tuple-element.30.hi_ref, bf16[256,4096]{1,0:T(8,128)(2,1)S(1)} %get-tuple-element.31.lo_ref), custom_call_target="tpu_custom_call" | custom-call | tf_op jit(solution)/shard_map/next_v/pallas_call | solution.py:377
  75.5 0.4 collective-permute-start.14
  76.0 5.9 %next_u.1 = f32[64,8192]{1,0:T(8,128)} custom-call(f32[64,8192]{1,0:T(8,128)S(1)} %copy-done, f32[64,8192]{1,0:T(8,128)S(1)} %copy-done, f32[64,8192]{1,0:T(8,128)S(1)} %copy-done, f32[64,128]{1,0:T(8,128)S(1)} %get-tuple-element.40.left_ref, f32[64,128]{1,0:T(8,128)S(1)} %get-tuple-element.39.right_ref, f32[4,8192]{1,0:T(4,128)S(1)} %get-tuple-element.18.m_ref, ...), custom_call_target="tpu_custom_call" | custom-call | tf_op jit(solution)/shard_map/next_u/pallas_call | solution.py:432
  81.9 0.0 collective-permute-done.14
  81.9 0.2 broadcast_select_fusion.1
  82.1 1.5 %pad_maximum_fusion = f32[64,8192]{1,0:T(8,128)} fusion(f32[64,4096]{1,0:T(8,128)S(1)} %get-tuple-element.36, f32[64,4096]{1,0:T(8,128)S(1)} %get-tuple-element.35), kind=kLoop, calls=%fused_computation | loop fusion | flops 524288 | bytes 4194304 | tf_op jit(solution)/shard_map/concatenate | solution.py:518
  (13 shorter events, 0.1 us)
Async XLA Ops:
  1.4 5.6 %collective-permute-start.2 = (f32[64,128]{1,0:T(8,128)S(1)}, f32[64,128]{1,0:T(8,128)S(1)}, u32[]{:S(2)}, u32[]{:S(2)}) collective-permute-start(f32[64,128]{1,0:T(8,128)S(1)} %slice_select_fusion), channel_id=1, source_target_pairs={{0,1},{1,2},{2,3},{3,4},{4,5},{5,6},{6,7},{7,8},{8,9},{9,10},{10,1... | collective-permute-start | bytes 98312 | tf_op jit(solution)/shard_map/ppermute | solution.py:484
  7.1 1.6 %copy-start.1 = (f32[64,8192]{1,0:T(8,128)S(1)}, f32[64,8192]{1,0:T(8,128)}, u32[]{:S(2)}) copy-start(f32[64,8192]{1,0:T(8,128)} %after_ref.3) | copy-start | bytes 6291460
  8.7 1.0 %copy-start.2 = (f32[4,3,8192]{2,0,1:T(4,128)S(1)}, f32[4,3,8192]{2,0,1:T(4,128)}, u32[]{:S(2)}) copy-start(f32[4,3,8192]{2,0,1:T(4,128)} %param.14) | copy-start | bytes 1179652
  9.7 0.7 copy-start.4
  10.3 12.1 %copy-start = (f32[64,8192]{1,0:T(8,128)S(1)}, f32[64,8192]{1,0:T(8,128)}, u32[]{:S(2)}) copy-start(f32[64,8192]{1,0:T(8,128)} %after_ref.6) | copy-start | bytes 6291460
  17.0 3.8 %collective-permute-start.3 = (f32[192,128]{1,0:T(8,128)S(1)}, f32[192,128]{1,0:T(8,128)S(1)}, u32[]{:S(2)}, u32[]{:S(2)}) collective-permute-start(f32[192,128]{1,0:T(8,128)S(1)} %get-tuple-element.22), channel_id=1, source_target_pairs={{0,32},{32,0},{64,96},{96,64},{128,160},{160,128},{192,224},{224,1... | collective-permute-start | bytes 294920 | tf_op jit(solution)/shard_map/ppermute | solution.py:469
  20.8 5.6 %collective-permute-start.4 = (f32[192,128]{1,0:T(8,128)S(1)}, f32[192,128]{1,0:T(8,128)S(1)}, u32[]{:S(2)}, u32[]{:S(2)}) collective-permute-start(f32[192,128]{1,0:T(8,128)S(1)} %add.99), channel_id=1, source_target_pairs={{0,1},{1,0},{2,3},{3,2},{4,5},{5,4},{6,7},{7,6},{8,9},{9,8},{10,11... | collective-permute-start | bytes 294920 | tf_op jit(solution)/shard_map/ppermute | solution.py:469
  22.5 8.2 %collective-permute-start.1 = (f32[64,128]{1,0:T(8,128)S(1)}, f32[64,128]{1,0:T(8,128)S(1)}, u32[]{:S(2)}, u32[]{:S(2)}) collective-permute-start(f32[64,128]{1,0:T(8,128)S(1)} %get-tuple-element.37), channel_id=1, source_target_pairs={{0,32},{32,0},{64,96},{96,64},{128,160},{160,128},{192,224},{224,1... | collective-permute-start | bytes 98312 | tf_op jit(solution)/shard_map/ppermute | solution.py:469
  23.2 7.4 %collective-permute-start = (f32[64,128]{1,0:T(8,128)S(1)}, f32[64,128]{1,0:T(8,128)S(1)}, u32[]{:S(2)}, u32[]{:S(2)}) collective-permute-start(f32[64,128]{1,0:T(8,128)S(1)} %get-tuple-element.38), channel_id=1, source_target_pairs={{32,64},{64,32},{96,128},{128,96},{160,192},{192,160},{33,65},{65,... | collective-permute-start | bytes 98312 | tf_op jit(solution)/shard_map/ppermute | solution.py:495
  26.4 10.4 %collective-permute-start.5 = (f32[192,128]{1,0:T(8,128)S(1)}, f32[192,128]{1,0:T(8,128)S(1)}, u32[]{:S(2)}, u32[]{:S(2)}) collective-permute-start(f32[192,128]{1,0:T(8,128)S(1)} %add.100), channel_id=1, source_target_pairs={{0,2},{1,3},{2,0},{3,1},{4,6},{5,7},{6,4},{7,5},{8,10},{9,11},{10,... | collective-permute-start | bytes 294920 | tf_op jit(solution)/shard_map/ppermute | solution.py:469
  33.6 24.8 %copy-start.3 = (f32[64,64]{1,0:T(8,128)S(1)}, f32[64,64]{1,0:T(8,128)}, u32[]{:S(2)}) copy-start(f32[64,64]{1,0:T(8,128)} %c_ref.1) | copy-start | bytes 49156
  36.5 3.2 %collective-permute-start.10 = (f32[192,128]{1,0:T(8,128)S(1)}, f32[192,128]{1,0:T(8,128)S(1)}, u32[]{:S(2)}, u32[]{:S(2)}) collective-permute-start(f32[192,128]{1,0:T(8,128)S(1)} %get-tuple-element.26), channel_id=1, source_target_pairs={{0,32},{32,0},{64,96},{96,64},{128,160},{160,128},{192,224},{224,1... | collective-permute-start | bytes 294920 | tf_op jit(solution)/shard_map/ppermute | solution.py:469
  36.8 8.0 %collective-permute-start.6 = (f32[192,128]{1,0:T(8,128)S(1)}, f32[192,128]{1,0:T(8,128)S(1)}, u32[]{:S(2)}, u32[]{:S(2)}) collective-permute-start(f32[192,128]{1,0:T(8,128)S(1)} %add.101), channel_id=1, source_target_pairs={{0,4},{1,5},{2,6},{3,7},{4,0},{5,1},{6,2},{7,3},{8,12},{9,13},{10,... | collective-permute-start | bytes 294920 | tf_op jit(solution)/shard_map/ppermute | solution.py:469
  39.7 6.4 %collective-permute-start.11 = (f32[192,128]{1,0:T(8,128)S(1)}, f32[192,128]{1,0:T(8,128)S(1)}, u32[]{:S(2)}, u32[]{:S(2)}) collective-permute-start(f32[192,128]{1,0:T(8,128)S(1)} %add.105), channel_id=1, source_target_pairs={{0,64},{32,96},{64,0},{96,32},{128,192},{160,224},{192,128},{224,1... | collective-permute-start | bytes 294920 | tf_op jit(solution)/shard_map/ppermute | solution.py:469
  44.8 4.6 %collective-permute-start.7 = (f32[192,128]{1,0:T(8,128)S(1)}, f32[192,128]{1,0:T(8,128)S(1)}, u32[]{:S(2)}, u32[]{:S(2)}) collective-permute-start(f32[192,128]{1,0:T(8,128)S(1)} %add.102), channel_id=1, source_target_pairs={{0,8},{1,9},{2,10},{3,11},{4,12},{5,13},{6,14},{7,15},{8,0},{9,1},... | collective-permute-start | bytes 294920 | tf_op jit(solution)/shard_map/ppermute | solution.py:469
  46.1 5.7 %collective-permute-start.12 = (f32[192,128]{1,0:T(8,128)S(1)}, f32[192,128]{1,0:T(8,128)S(1)}, u32[]{:S(2)}, u32[]{:S(2)}) collective-permute-start(f32[192,128]{1,0:T(8,128)S(1)} %add.106), channel_id=1, source_target_pairs={{0,128},{32,160},{64,192},{96,224},{128,0},{160,32},{192,64},{224,... | collective-permute-start | bytes 294920 | tf_op jit(solution)/shard_map/ppermute | solution.py:469
  49.4 5.1 %collective-permute-start.8 = (f32[192,128]{1,0:T(8,128)S(1)}, f32[192,128]{1,0:T(8,128)S(1)}, u32[]{:S(2)}, u32[]{:S(2)}) collective-permute-start(f32[192,128]{1,0:T(8,128)S(1)} %add.103), channel_id=1, source_target_pairs={{0,16},{1,17},{2,18},{3,19},{4,20},{5,21},{6,22},{7,23},{8,24},{9,... | collective-permute-start | bytes 294920 | tf_op jit(solution)/shard_map/ppermute | solution.py:469
  51.9 5.6 %collective-permute-start.13 = (f32[192,128]{1,0:T(8,128)S(1)}, f32[192,128]{1,0:T(8,128)S(1)}, u32[]{:S(2)}, u32[]{:S(2)}) collective-permute-start(f32[192,128]{1,0:T(8,128)S(1)} %add.107.gu_mine), channel_id=1, source_target_pairs={{0,32},{32,0},{64,96},{96,64},{128,160},{160,128},{192,224},{224,1... | collective-permute-start | bytes 294920 | tf_op jit(solution)/shard_map/ppermute | solution.py:469
  54.5 4.0 %collective-permute-start.9 = (f32[192,128]{1,0:T(8,128)S(1)}, f32[192,128]{1,0:T(8,128)S(1)}, u32[]{:S(2)}, u32[]{:S(2)}) collective-permute-start(f32[192,128]{1,0:T(8,128)S(1)} %add.104.gv_mine), channel_id=1, source_target_pairs={{0,32},{32,0},{64,96},{96,64},{128,160},{160,128},{192,224},{224,1... | collective-permute-start | bytes 294920 | tf_op jit(solution)/shard_map/ppermute | solution.py:469
  75.5 6.3 %collective-permute-start.14 = (f32[64,4096]{1,0:T(8,128)S(1)}, f32[64,4096]{1,0:T(8,128)S(1)}, u32[]{:S(2)}, u32[]{:S(2)}) collective-permute-start(f32[64,4096]{1,0:T(8,128)S(1)} %next_v.1), channel_id=1, source_target_pairs={{0,32},{32,0},{64,96},{96,64},{128,160},{160,128},{192,224},{224,1... | collective-permute-start | bytes 3145736 | tf_op jit(solution)/shard_map/ppermute | solution.py:469

commit v3 on v2

--- a/solution.py
+++ b/solution.py
@@ -6,6 +6,7 @@
 from jax.experimental import pallas as pl
 from jax.experimental.pallas import tpu as pltpu
 from jax.sharding import PartitionSpec as P
+
 
 BAND = 4
 LANES = 128
@@ -40,6 +41,13 @@
 
 def full_dot(a, b, dims=NN):
     return lax.dot_general(a, b, dims, precision=lax.Precision.HIGHEST, preferred_element_type=F32)
+
+
+def split_dot(a, b, dims=NN):
+    a_hi, a_lo = split(a)
+    b_hi, b_lo = split(b)
+    small = fast_dot(a_hi, b_lo, dims) + fast_dot(a_lo, b_hi, dims)
+    return fast_dot(a_hi, b_hi, dims) + small
 
 
 def lane_iota(shape):
@@ -241,40 +249,52 @@
         grid_spec=spec,
         out_shape=[jax.ShapeDtypeStruct((192, LANES), F32)] * 2,
         compiler_params=pltpu.CompilerParams(vmem_limit_bytes=VMEM_LIMIT),
-        name="gram_u" + str(part_at),
     )(core, u, u, u, left, right, mass, diffusion, *had)
 
 
-def lower_inverse(square):
+def lower_inverse(square, zero):
     size = RANK
     groups = size // 8
     rows_idx = lax.broadcasted_iota(jnp.int32, (size, size), 0)
-    cols_idx = lax.broadcasted_iota(jnp.int32, (size, size), 1)
-    unit = jnp.where(rows_idx == cols_idx, 1.0, 0.0).astype(F32)
+    unit = jnp.where(rows_idx == lane_iota((size, size)), 1.0, 0.0).astype(F32)
     both = jnp.concatenate([square, unit], axis=1)
     work = [both[8 * q:8 * q + 8, :] for q in range(groups)]
     shape = (8, 2 * size)
     sub = lax.broadcasted_iota(jnp.int32, shape, 0)
+
+    def lane(x, at):
+        return jnp.broadcast_to(x[:, at:at + 1], shape)
+
+    def row(x, at):
+        return jnp.broadcast_to(x[at:at + 1, :], shape)
+
     done = []
     for p in range(groups):
-        cols = [[jnp.broadcast_to(work[q][:, 8 * p + j:8 * p + j + 1], shape) for q in range(p, groups)] for j in range(8)]
-        rows = [jnp.broadcast_to(work[p][j:j + 1, :], shape) for j in range(8)]
-        scaled = []
+        cols = [lane(work[p], 8 * p + j) + zero for j in range(8)]
+        rows = [row(work[p], j) for j in range(8)]
         kept = None
+        invs = []
         for j in range(8):
-            pivot = jnp.broadcast_to(cols[j][0][j:j + 1, :], shape)
+            pivot = row(cols[j], j)
             inv = 1.0 / pivot
-            for k in range(j + 1, 8):
-                factor = jnp.broadcast_to(cols[j][0][k:k + 1, :], shape) * inv
-                for q in range(groups - p):
-                    cols[k][q] = cols[k][q] - cols[j][q] * factor
-                rows[k] = rows[k] - rows[j] * factor
-            scaled.append(rows[j] * inv)
             unit_row = rows[j] * lax.rsqrt(pivot)
             kept = unit_row if j == 0 else jnp.where(sub == j, unit_row, kept)
+            last = p == groups - 1
+            above = cols[j] if last else jnp.where(sub == j, 0.0, cols[j])
+            for k in range(j + 1, 8):
+                cols[k] = cols[k] - above * (row(cols[j], k) * inv)
+            scaled = rows[j] * inv
+            for k in range(j + 1 if last else 0, 8):
+                if k != j:
+                    rows[k] = rows[k] - scaled * row(cols[j], k)
+            invs.append(inv)
+        if p < groups - 1:
+            rows = [r * inv for r, inv in zip(rows, invs)]
         for q in range(p + 1, groups):
-            for j in range(8):
-                work[q] = work[q] - cols[j][q - p] * scaled[j]
+            terms = [lane(work[q], 8 * p + j) * rows[j] for j in range(8)]
+            while len(terms) > 1:
+                terms = [terms[i] + terms[i + 1] for i in range(0, len(terms), 2)]
+            work[q] = work[q] - terms[0]
         done.append(kept)
     return jnp.concatenate(done, axis=0)[:, size:]
 
@@ -302,19 +322,21 @@
 
 
 def chain_kernel(core_ref, gv_mine, gv_other, gu_mine, gu_other, sketch_ref, c_ref, mu_ref, mv_ref, next_ref,
-                 gv_ref, gu_ref, panel_ref, block_ref):
+                 gv_ref, gu_ref, panel_ref):
     core = core_ref[0]
+    zero = jnp.where(core > 1, 1.0, 0.0).astype(F32)
     unpack(core, gv_mine, gv_other, gv_ref)
     unpack(core, gu_mine, gu_other, gu_ref)
-    block_ref[...] = jnp.zeros_like(block_ref)
+    blocks = [slice(k * RANK, (k + 1) * RANK) for k in range(STENCILS)]
     for k in range(STENCILS):
-        at = slice(k * RANK, (k + 1) * RANK)
-        block_ref[at, at] = c_ref[...]
-        panel_ref[k] = gv_ref[:, at]
+        panel_ref[k] = gv_ref[:, blocks[k]]
+    c = c_ref[...]
+    low = lax.broadcasted_iota(jnp.int32, (RANK, RANK), 0) >= lane_iota((RANK, RANK))
     parts = [None] * STENCILS
+    w = []
+    k_t = None
     for p in range(STENCILS):
-        at = slice(p * RANK, (p + 1) * RANK)
-        inverse = lower_inverse(panel_ref[p, at, :])
+        inverse = lower_inverse(panel_ref[p, blocks[p], :], zero)
         below = full_dot(panel_ref[p, p * RANK:, :], inverse, NT)
         for q in range(p + 1, STENCILS):
             head = (q - p) * RANK
@@ -323,26 +345,24 @@
             head = (q - p) * RANK
             block = below[head:head + RANK]
             if q == p:
-                block = jnp.where(
-                    lax.broadcasted_iota(jnp.int32, block.shape, 0) >= lane_iota(block.shape), block, 0.0)
-            term = full_dot(sketch_ref[p], block, NT)
+                block = jnp.where(low, block, 0.0)
+            term = split_dot(sketch_ref[p], block, NT)
             parts[q] = term if parts[q] is None else parts[q] + term
-    base = jnp.concatenate(parts, axis=1)
-    w_t = full_dot(base, block_ref[...], NT)
-    k_t = full_dot(w_t, gu_ref[...])
-    inverse_y = lower_inverse(full_dot(w_t, k_t, NT))
-    x_t = full_dot(inverse_y, full_dot(k_t, block_ref[...]))
-    map_u = full_dot(inverse_y, w_t)
-    inner = full_dot(x_t, full_dot(x_t, gv_ref[...]), NT)
-    inverse_c = lower_inverse(inner)
-    map_v = full_dot(inverse_c, x_t)
-    lower = full_dot(inner, inverse_c, NT)
-    keep = lax.broadcasted_iota(jnp.int32, lower.shape, 0) >= lane_iota(lower.shape)
-    next_ref[...] = jnp.where(keep, lower, 0.0)
+        w.append(split_dot(parts[p], c, NT))
+        term = full_dot(w[p], gu_ref[blocks[p], :])
+        k_t = term if k_t is None else k_t + term
+    w_t = jnp.concatenate(w, axis=1)
+    inverse_y = lower_inverse(full_dot(w_t, k_t, NT), zero)
+    back = jnp.concatenate([split_dot(k_t[:, at], c) for at in blocks], axis=1)
+    back_gram = full_dot(back, gv_ref[...])
+    x_t = full_dot(inverse_y, back)
+    inner = full_dot(x_t, full_dot(inverse_y, back_gram), NT)
+    inverse_c = lower_inverse(inner, zero)
+    map_u = split_dot(inverse_y, w_t)
     for k in range(STENCILS):
-        at = slice(k * RANK, (k + 1) * RANK)
-        mu_ref[at, :] = three(map_u[:, at])
-    put_split(mv_ref, map_v)
+        mu_ref[blocks[k], :] = three(map_u[:, blocks[k]])
+    put_split(mv_ref, split_dot(inverse_c, x_t))
+    next_ref[...] = jnp.where(low, full_dot(inner, inverse_c, NT), 0.0)
 
 
 def chain(core, gv_mine, gv_other, gu_mine, gu_other, sketch_t, core_matrix):
@@ -359,7 +379,6 @@
             pltpu.VMEM((WIDE, WIDE), F32),
             pltpu.VMEM((WIDE, WIDE), F32),
             pltpu.VMEM((STENCILS, WIDE, RANK), F32),
-            pltpu.VMEM((WIDE, WIDE), F32),
         ],
         compiler_params=pltpu.CompilerParams(vmem_limit_bytes=VMEM_LIMIT),
         name="chain",
@@ -371,7 +390,7 @@
     out_ref[...] = both[0:RANK] + (both[RANK:2 * RANK] + fast_dot(map_ref[0:RANK, :], lo_ref[...], NN))
 
 
-def next_factor(name, maps, wide_hi, wide_lo):
+def next_factor(maps, wide_hi, wide_lo):
     cells = wide_hi.shape[1]
     tile = min(1024, cells)
     return pl.pallas_call(
@@ -385,7 +404,6 @@
         out_specs=pl.BlockSpec((RANK, tile), lambda i: (0, i)),
         out_shape=jax.ShapeDtypeStruct((RANK, cells), F32),
         compiler_params=pltpu.CompilerParams(vmem_limit_bytes=VMEM_LIMIT),
-        name=name,
     )(maps, wide_hi, wide_lo)
 
 
@@ -469,7 +487,12 @@
     return lax.ppermute(x, axis, [(i, i ^ bit) for i in range(lax.axis_size(axis))])
 
 
-def local(u, v, mass_table, diffusivity_table, material_index, weights, offsets, core_matrix, sketch_seed):
+def four_way(x, axis, bit):
+    near, far, both = (swap(x, axis, b) for b in (bit, 2 * bit, 3 * bit))
+    return (x + near) + (far + both)
+
+
+def body(u, v, mass_table, diffusivity_table, material_index, weights, offsets, core_matrix, sketch_seed):
     gx, pa = lax.axis_size("gx"), lax.axis_size("pa")
     at_gx = lax.axis_index("gx")
     core = (at_gx % 2).astype(jnp.int32).reshape(1)
@@ -485,34 +508,32 @@
     onehot = (material_index[:, None, :] == jnp.arange(mass_table.shape[1], dtype=jnp.int32)[None, :, None]).astype(F32)
     mass = jnp.sum(mass_table[:, :, None] * onehot, axis=1)
     diffusion = jnp.sum(diffusivity_table[:, :, None] * onehot, axis=1)
-    sketch_t = make_sketch_t(sketch_seed, WIDE, RANK)
-    v_in, mass, diffusion, sketch_t = lax.optimization_barrier((v, mass, diffusion, sketch_t))
-    weights = jnp.transpose(weights, (1, 0, 2))
-    gv_mine, gv_other, hi_v, lo_v = gram_v(core, offsets, v_in, halo_v, weights, 1.0 / (v.shape[1] * pa))
-    gv = gv_mine + swap(gv_other, "gx", 1)
-
+    near_u = swap(jnp.where(even, u[:, -LANES:], u[:, :LANES]), "gx", 1)
     u_pairs = [(i, i - 1 if i % 2 == 0 else i + 1) for i in range(gx)]
     far_u = lax.ppermute(jnp.where(even, u[:, :LANES], u[:, -LANES:]), "gx", [(i, j) for i, j in u_pairs if 0 <= j < gx])
-    near_u = swap(jnp.where(even, u[:, -LANES:], u[:, :LANES]), "gx", 1)
+    core_v, mass, diffusion = lax.optimization_barrier((core, mass, diffusion))
+    weights = pltpu.with_memory_space_constraint(jnp.transpose(weights, (1, 0, 2)), pltpu.HBM)
+    v_in = pltpu.with_memory_space_constraint(v, pltpu.HBM)
+    gv_mine, gv_other, hi_v, lo_v = gram_v(core_v, pltpu.with_memory_space_constraint(offsets, pltpu.HBM), v_in, halo_v, weights, 1.0 / (v.shape[1] * pa))
+    gv = gv_mine + swap(gv_other, "gx", 1)
+
     left_u = jnp.where(even, far_u, near_u)
     right_u = jnp.where(even, near_u, far_u)
     u_scale = 1.0 / (u.shape[1] * gx)
     had = gram_u(core, 0, 2, u, left_u, right_u, mass, diffusion, u_scale)
     gu_mine, gu_other = gram_u(core, 1, 2, u, left_u, right_u, mass, diffusion, u_scale, had)
+    sketch_t = make_sketch_t(sketch_seed, WIDE, RANK)
 
     bit = 1
-    while bit < pa:
+    while bit * 4 < pa:
         gv = gv + swap(gv, "pa", bit)
         bit *= 2
-    gu = gu_mine + swap(gu_other, "gx", 1)
-    bit = 2
-    while bit < gx:
-        gu = gu + swap(gu, "gx", bit)
-        bit *= 2
+    gu = four_way(gu_mine + swap(gu_other, "gx", 1), "gx", 2)
+    gv = four_way(gv, "pa", bit)
     gv_far = swap(gv, "gx", 1)
     gu_far = swap(gu, "gx", 1)
     map_u, map_v, core_next = chain(core, gv, gv_far, gu, gu_far, sketch_t, core_matrix)
-    half = next_factor("next_v", map_v, hi_v, lo_v)
+    half = next_factor(map_v, hi_v, lo_v)
     half_far = swap(half, "gx", 1)
     u_next = next_u(u, left_u, right_u, mass, diffusion, map_u)
     v_next = jnp.concatenate([jnp.where(even, half, half_far), jnp.where(even, half_far, half)], axis=1)
@@ -521,7 +542,7 @@
 
 def solution(mesh):
     return jax.shard_map(
-        local,
+        body,
         mesh=mesh,
         in_specs=(
             P(None, "gx"),

time: 84.8 us -> 87 us (1.026); the launches traced: 83.5 us -> 86.7 us
  starting transfers between devices: 31.2 us -> 34.6 us
  local copies, waits for them, and re-layouts: 3.28 us -> 0.01 us
  waiting for transfers between devices: 7.2 us -> 9.27 us
  Pallas kernels: 35.4 us -> 36.5 us
    unnamed x10 -> x4, local copies, waits for them, and re-layouts: 3.28 us -> 0.01 us
    ppermute x13 -> x15, starting transfers between devices: 26.8 us -> 29.7 us  [swap(): lax.ppermute(x, axis, [(i, i ^ bit) for i in range(lax.axis_size(axis))])]
    ppermute x2, waiting for transfers between devices: 1.3 us -> 2.5 us  [the longest x1 2.5 us: body(): halo_v = lax.ppermute(edge_v, ('gx', 'pa'), pairs)]
    pallas_call x1, Pallas kernels: 6.61 us -> 7.65 us  [gram_v(): pl.pallas_call(functools.partial(gram_v_kernel, steps, scale), grid_spec=...]
    ppermute x13 -> x15, waiting for transfers between devices: 5.9 us -> 6.77 us  [swap(): lax.ppermute(x, axis, [(i, i ^ bit) for i in range(lax.axis_size(axis))])]
  transfers between devices with their start and end apart: 15 -> 17, of which waited for: 5 -> 5; matrix products, arithmetic and copies ran while one was open for 3% -> 3% of each run, Pallas kernels for 14% -> 13%
where the time goes in v3:
time: 87 us; the launch traced here: 86.7 us
  Pallas kernels  36.5 us (42%)
  starting transfers between devices  34.6 us (40%)
  waiting for transfers between devices  9.27 us (11%)
  other arithmetic  4.9 us (6%)
  between operations  1.45 us (2%)
    ppermute x15, starting transfers between devices, swap(): lax.ppermute(x, axis, [(i, i ^ bit) for i in range(lax.axis_size(axis))])  29.7 us
    pallas_call x1, Pallas kernels, chain(): pl.pallas_call(chain_kernel, in_specs=[smem()] + [vmem()] * 6, out_specs=...  15.6 us
    pallas_call x1, Pallas kernels, gram_v(): pl.pallas_call(functools.partial(gram_v_kernel, steps, scale), grid_spec=...  7.65 us
    ppermute x15, waiting for transfers between devices, swap(): lax.ppermute(x, axis, [(i, i ^ bit) for i in range(lax.axis_size(axis))])  6.77 us
    pallas_call x1, Pallas kernels, next_u(): pl.pallas_call(functools.partial(next_u_kernel, steps), grid=(steps,), in...  5.85 us
    pallas_call x2, Pallas kernels, gram_u(): pl.pallas_call(functools.partial(gram_u_kernel, part_at, parts, steps, sc...  5.77 us
    ppermute x1, starting transfers between devices, body(): lax.ppermute(jnp.where(even, u[:, :LANES], u[:, -LANES:]), 'gx', [(i, j)...  3.56 us
    ppermute x1, waiting for transfers between devices, body(): halo_v = lax.ppermute(edge_v, ('gx', 'pa'), pairs)  2.5 us
  transfers between devices with their start and end apart: 17, of which 5 were waited for; matrix products, arithmetic and copies ran while one was open for 3% of the time, Pallas kernels for 13%

profile of v3, /device:TPU:1, one launch (start us, length us, event | category | flops | bytes accessed | tf_op | source)
XLA Modules:
  0.0 86.7 jit_solution(8211168398749014297)
XLA Ops:
  0.6 0.8 slice_select_fusion
  1.4 1.3 %collective-permute-start.2 = (f32[64,128]{1,0:T(8,128)S(1)}, f32[64,128]{1,0:T(8,128)S(1)}, u32[]{:S(2)}, u32[]{:S(2)}) collective-permute-start(f32[64,128]{1,0:T(8,128)S(1)} %slice_select_fusion), channel_id=1, source_target_pairs={{0,1},{1,2},{2,3},{3,4},{4,5},{5,6},{6,7},{7,8},{8,9},{9,10},{10,1... | collective-permute-start | bytes 98312 | tf_op jit(solution)/shard_map/ppermute | solution.py:507
  2.7 1.9 %select_reduce_fusion = (f32[4,8192]{1,0:T(4,128)S(1)}, f32[4,8192]{1,0:T(4,128)S(1)}) fusion(f32[4,16]{1,0:T(4,128)} %param.12, s32[4,8192]{1,0:T(4,128)} %param.13, f32[4,16]{1,0:T(4,128)} %param.11), kind=kLoop, calls=%fused_computation.1 | loop fusion | flops 2555904 | bytes 393728 | tf_op jit(solution)/shard_map/reduce_sum | solution.py:510
  4.6 2.5 %collective-permute-done.2.halo_ref = f32[64,128]{1,0:T(8,128)S(1)} collective-permute-done((f32[64,128]{1,0:T(8,128)S(1)}, f32[64,128]{1,0:T(8,128)S(1)}, u32[]{:S(2)}, u32[]{:S(2)}) %collective-permute-start.2) | collective-permute-done | bytes 32800 | tf_op jit(solution)/shard_map/ppermute | solution.py:507
  7.1 0.0 copy-start
  7.1 7.7 %gram_v.1 = (f32[192,128]{1,0:T(8,128)S(1)}, f32[192,128]{1,0:T(8,128)S(1)}, bf16[256,4096]{1,0:T(8,128)(2,1)S(1)}, bf16[256,4096]{1,0:T(8,128)(2,1)S(1)}) custom-call(s32[1]{0:T(128)} %bitcast.core_ref, s32[4,3]{1,0:T(4,128)} %off_ref.1, f32[64,8192]{1,0:T(8,128)} %after_ref.4, f32[64,8192]{1,0:T(8,128)} %after_ref.4, f32[64,8192]{1,0:T(8,128)} %after_ref.4, ...), custom_call_target="tpu_custom_call" | custom-call | tf_op jit(solution)/shard_map/gram_v/pallas_call | solution.py:170
  14.7 1.7 %collective-permute-start.3 = (f32[192,128]{1,0:T(8,128)S(1)}, f32[192,128]{1,0:T(8,128)S(1)}, u32[]{:S(2)}, u32[]{:S(2)}) collective-permute-start(f32[192,128]{1,0:T(8,128)S(1)} %get-tuple-element.21), channel_id=1, source_target_pairs={{0,32},{32,0},{64,96},{96,64},{128,160},{160,128},{192,224},{224,1... | collective-permute-start | bytes 294920 | tf_op jit(solution)/shard_map/ppermute | solution.py:487
  16.4 0.0 copy-done
  16.4 0.1 collective-permute-start.1
  16.6 3.6 %collective-permute-start = (f32[64,128]{1,0:T(8,128)S(1)}, f32[64,128]{1,0:T(8,128)S(1)}, u32[]{:S(2)}, u32[]{:S(2)}) collective-permute-start(f32[64,128]{1,0:T(8,128)S(1)} %get-tuple-element.36), channel_id=1, source_target_pairs={{32,64},{64,32},{96,128},{128,96},{160,192},{192,160},{33,65},{65,... | collective-permute-start | bytes 98312 | tf_op jit(solution)/shard_map/ppermute | solution.py:513
  20.8 0.0 collective-permute-done.3
  20.8 1.8 %collective-permute-start.4 = (f32[192,128]{1,0:T(8,128)S(1)}, f32[192,128]{1,0:T(8,128)S(1)}, u32[]{:S(2)}, u32[]{:S(2)}) collective-permute-start(f32[192,128]{1,0:T(8,128)S(1)} %add.91), channel_id=1, source_target_pairs={{0,1},{1,0},{2,3},{3,2},{4,5},{5,4},{6,7},{7,6},{8,9},{9,8},{10,11... | collective-permute-start | bytes 294920 | tf_op jit(solution)/shard_map/ppermute | solution.py:487
  22.6 0.0 collective-permute-done.1
  22.6 0.0 collective-permute-done
  22.6 2.9 %shard_map.112 = (f32[192,128]{1,0:T(8,128)S(1)}, f32[192,128]{1,0:T(8,128)S(1)}) custom-call(s32[1]{0:T(128)} %bitcast.core_ref, f32[64,8192]{1,0:T(8,128)S(1)} %copy-done, f32[64,8192]{1,0:T(8,128)S(1)} %copy-done, f32[64,8192]{1,0:T(8,128)S(1)} %copy-done, f32[64,128]{1,0:T(8,128)S(1)} %get-tuple-element.38.left_ref, ...), custom_call_target="tpu_custom_call" | custom-call | tf_op jit(solution)/shard_map/pallas_call | solution.py:247
  25.5 2.9 %shard_map.113 = (f32[192,128]{1,0:T(8,128)S(1)}, f32[192,128]{1,0:T(8,128)S(1)}) custom-call(s32[1]{0:T(128)} %bitcast.core_ref, f32[64,8192]{1,0:T(8,128)S(1)} %copy-done, f32[64,8192]{1,0:T(8,128)S(1)} %copy-done, f32[64,8192]{1,0:T(8,128)S(1)} %copy-done, f32[64,128]{1,0:T(8,128)S(1)} %get-tuple-element.38.left_ref, ...), custom_call_target="tpu_custom_call" | custom-call | tf_op jit(solution)/shard_map/pallas_call | solution.py:247
  28.4 0.0 copy-start.1
  28.4 0.1 collective-permute-start.11
  28.5 0.0 collective-permute-done.4
  28.6 4.2 %collective-permute-start.5 = (f32[192,128]{1,0:T(8,128)S(1)}, f32[192,128]{1,0:T(8,128)S(1)}, u32[]{:S(2)}, u32[]{:S(2)}) collective-permute-start(f32[192,128]{1,0:T(8,128)S(1)} %add.92), channel_id=1, source_target_pairs={{0,2},{1,3},{2,0},{3,1},{4,6},{5,7},{6,4},{7,5},{8,10},{9,11},{10,... | collective-permute-start | bytes 294920 | tf_op jit(solution)/shard_map/ppermute | solution.py:487
  32.8 0.0 collective-permute-done.11
  32.8 2.3 %collective-permute-start.14 = (f32[192,128]{1,0:T(8,128)S(1)}, f32[192,128]{1,0:T(8,128)S(1)}, u32[]{:S(2)}, u32[]{:S(2)}) collective-permute-start(f32[192,128]{1,0:T(8,128)S(1)} %add.98), channel_id=1, source_target_pairs={{0,192},{32,224},{64,128},{96,160},{128,64},{160,96},{192,0},{224,... | collective-permute-start | bytes 294920 | tf_op jit(solution)/shard_map/ppermute | solution.py:487
  35.1 0.9 %collective-permute-start.13 = (f32[192,128]{1,0:T(8,128)S(1)}, f32[192,128]{1,0:T(8,128)S(1)}, u32[]{:S(2)}, u32[]{:S(2)}) collective-permute-start(f32[192,128]{1,0:T(8,128)S(1)} %add.98), channel_id=1, source_target_pairs={{0,128},{32,160},{64,192},{96,224},{128,0},{160,32},{192,64},{224,... | collective-permute-start | bytes 294920 | tf_op jit(solution)/shard_map/ppermute | solution.py:487
  36.0 0.2 collective-permute-start.12
  36.1 1.4 %collective-permute-done.5 = f32[192,128]{1,0:T(8,128)S(1)} collective-permute-done((f32[192,128]{1,0:T(8,128)S(1)}, f32[192,128]{1,0:T(8,128)S(1)}, u32[]{:S(2)}, u32[]{:S(2)}) %collective-permute-start.5) | collective-permute-done | bytes 98336 | tf_op jit(solution)/shard_map/ppermute | solution.py:487
  37.6 6.6 %collective-permute-start.6 = (f32[192,128]{1,0:T(8,128)S(1)}, f32[192,128]{1,0:T(8,128)S(1)}, u32[]{:S(2)}, u32[]{:S(2)}) collective-permute-start(f32[192,128]{1,0:T(8,128)S(1)} %add.93), channel_id=1, source_target_pairs={{0,4},{1,5},{2,6},{3,7},{4,0},{5,1},{6,2},{7,3},{8,12},{9,13},{10,... | collective-permute-start | bytes 294920 | tf_op jit(solution)/shard_map/ppermute | solution.py:487
  44.1 2.7 %collective-permute-done.6 = f32[192,128]{1,0:T(8,128)S(1)} collective-permute-done((f32[192,128]{1,0:T(8,128)S(1)}, f32[192,128]{1,0:T(8,128)S(1)}, u32[]{:S(2)}, u32[]{:S(2)}) %collective-permute-start.6) | collective-permute-done | bytes 98336 | tf_op jit(solution)/shard_map/ppermute | solution.py:487
  46.8 5.7 %collective-permute-start.9 = (f32[192,128]{1,0:T(8,128)S(1)}, f32[192,128]{1,0:T(8,128)S(1)}, u32[]{:S(2)}, u32[]{:S(2)}) collective-permute-start(f32[192,128]{1,0:T(8,128)S(1)} %add.94), channel_id=1, source_target_pairs={{0,24},{1,25},{2,26},{3,27},{4,28},{5,29},{6,30},{7,31},{8,16},{9,... | collective-permute-start | bytes 294920 | tf_op jit(solution)/shard_map/ppermute | solution.py:487
  52.6 0.0 collective-permute-start.8
  52.6 0.0 collective-permute-done.14
  52.6 0.7 collective-permute-start.7
  53.2 0.0 collective-permute-done.13
  53.2 0.0 collective-permute-done.12
  53.3 2.0 %collective-permute-start.15 = (f32[192,128]{1,0:T(8,128)S(1)}, f32[192,128]{1,0:T(8,128)S(1)}, u32[]{:S(2)}, u32[]{:S(2)}) collective-permute-start(f32[192,128]{1,0:T(8,128)S(1)} %add_add_fusion.gu_mine), channel_id=1, source_target_pairs={{0,32},{32,0},{64,96},{96,64},{128,160},{160,128},{192,224},{224,1... | collective-permute-start | bytes 294920 | tf_op jit(solution)/shard_map/ppermute | solution.py:487
  55.3 0.0 collective-permute-done.9
  55.3 2.2 %collective-permute-done.8 = f32[192,128]{1,0:T(8,128)S(1)} collective-permute-done((f32[192,128]{1,0:T(8,128)S(1)}, f32[192,128]{1,0:T(8,128)S(1)}, u32[]{:S(2)}, u32[]{:S(2)}) %collective-permute-start.8) | collective-permute-done | bytes 98336 | tf_op jit(solution)/shard_map/ppermute | solution.py:487
  57.5 0.0 collective-permute-done.7
  57.6 3.1 %collective-permute-start.10 = (f32[192,128]{1,0:T(8,128)S(1)}, f32[192,128]{1,0:T(8,128)S(1)}, u32[]{:S(2)}, u32[]{:S(2)}) collective-permute-start(f32[192,128]{1,0:T(8,128)S(1)} %add_add_fusion.1.gv_mine), channel_id=1, source_target_pairs={{0,32},{32,0},{64,96},{96,64},{128,160},{160,128},{192,224},{224,1... | collective-permute-start | bytes 294920 | tf_op jit(solution)/shard_map/ppermute | solution.py:487
  60.6 0.5 fusion.10.sketch_ref
  61.2 0.0 collective-permute-done.15.gu_other
  61.2 0.4 collective-permute-done.10.gv_other
  61.6 0.0 copy-done.1
  61.6 15.6 %chain.1 = (bf16[256,192]{1,0:T(8,128)(2,1)S(1)}, bf16[128,256]{1,0:T(8,128)(2,1)S(1)}, f32[64,64]{1,0:T(8,128)}) custom-call(s32[1]{0:T(128)} %bitcast.core_ref, f32[192,128]{1,0:T(8,128)S(1)} %add_add_fusion.1.gv_mine, f32[192,128]{1,0:T(8,128)S(1)} %collective-permute-done.10.gv_other, f32[192,128]{1,0:T(8,128)S(1)} %add_add_fusion.gu_mine, ...), custom_call_target="tpu_custom_call" | custom-call | tf_op jit(solution)/shard_map/chain/pallas_call | solution.py:369
  77.2 1.6 %shard_map.114 = f32[64,4096]{1,0:T(8,128)S(1)} custom-call(bf16[128,256]{1,0:T(8,128)(2,1)S(1)} %get-tuple-element.27.map_ref, bf16[256,4096]{1,0:T(8,128)(2,1)S(1)} %get-tuple-element.28.hi_ref, bf16[256,4096]{1,0:T(8,128)(2,1)S(1)} %get-tuple-element.29.lo_ref), custom_call_target="tpu_custom_call" | custom-call | tf_op jit(solution)/shard_map/pallas_call | solution.py:396
  78.8 0.4 collective-permute-start.16
  79.3 5.9 %next_u.1 = f32[64,8192]{1,0:T(8,128)} custom-call(f32[64,8192]{1,0:T(8,128)S(1)} %copy-done, f32[64,8192]{1,0:T(8,128)S(1)} %copy-done, f32[64,8192]{1,0:T(8,128)S(1)} %copy-done, f32[64,128]{1,0:T(8,128)S(1)} %get-tuple-element.38.left_ref, f32[64,128]{1,0:T(8,128)S(1)} %get-tuple-element.37.right_ref, f32[4,8192]{1,0:T(4,128)S(1)} %get-tuple-element.17.m_ref, ...), custom_call_target="tpu_custom_call" | custom-call | tf_op jit(solution)/shard_map/next_u/pallas_call | solution.py:450
  85.1 0.0 collective-permute-done.16
  85.1 0.1 broadcast_select_fusion.1
  85.3 1.5 %pad_maximum_fusion = f32[64,8192]{1,0:T(8,128)} fusion(f32[64,4096]{1,0:T(8,128)S(1)} %get-tuple-element.34, f32[64,4096]{1,0:T(8,128)S(1)} %get-tuple-element.33), kind=kLoop, calls=%fused_computation | loop fusion | flops 524288 | bytes 4194304 | tf_op jit(solution)/shard_map/concatenate | solution.py:539
  (11 shorter events, 0.1 us)
Async XLA Ops:
  1.4 5.6 %collective-permute-start.2 = (f32[64,128]{1,0:T(8,128)S(1)}, f32[64,128]{1,0:T(8,128)S(1)}, u32[]{:S(2)}, u32[]{:S(2)}) collective-permute-start(f32[64,128]{1,0:T(8,128)S(1)} %slice_select_fusion), channel_id=1, source_target_pairs={{0,1},{1,2},{2,3},{3,4},{4,5},{5,6},{6,7},{7,8},{8,9},{9,10},{10,1... | collective-permute-start | bytes 98312 | tf_op jit(solution)/shard_map/ppermute | solution.py:507
  7.1 9.4 %copy-start = (f32[64,8192]{1,0:T(8,128)S(1)}, f32[64,8192]{1,0:T(8,128)}, u32[]{:S(2)}) copy-start(f32[64,8192]{1,0:T(8,128)} %after_ref.7) | copy-start | bytes 6291460
  14.7 6.0 %collective-permute-start.3 = (f32[192,128]{1,0:T(8,128)S(1)}, f32[192,128]{1,0:T(8,128)S(1)}, u32[]{:S(2)}, u32[]{:S(2)}) collective-permute-start(f32[192,128]{1,0:T(8,128)S(1)} %get-tuple-element.21), channel_id=1, source_target_pairs={{0,32},{32,0},{64,96},{96,64},{128,160},{160,128},{192,224},{224,1... | collective-permute-start | bytes 294920 | tf_op jit(solution)/shard_map/ppermute | solution.py:487
  16.4 6.2 %collective-permute-start.1 = (f32[64,128]{1,0:T(8,128)S(1)}, f32[64,128]{1,0:T(8,128)S(1)}, u32[]{:S(2)}, u32[]{:S(2)}) collective-permute-start(f32[64,128]{1,0:T(8,128)S(1)} %get-tuple-element.35), channel_id=1, source_target_pairs={{0,32},{32,0},{64,96},{96,64},{128,160},{160,128},{192,224},{224,1... | collective-permute-start | bytes 98312 | tf_op jit(solution)/shard_map/ppermute | solution.py:487
  16.6 6.1 %collective-permute-start = (f32[64,128]{1,0:T(8,128)S(1)}, f32[64,128]{1,0:T(8,128)S(1)}, u32[]{:S(2)}, u32[]{:S(2)}) collective-permute-start(f32[64,128]{1,0:T(8,128)S(1)} %get-tuple-element.36), channel_id=1, source_target_pairs={{32,64},{64,32},{96,128},{128,96},{160,192},{192,160},{33,65},{65,... | collective-permute-start | bytes 98312 | tf_op jit(solution)/shard_map/ppermute | solution.py:513
  20.8 7.7 %collective-permute-start.4 = (f32[192,128]{1,0:T(8,128)S(1)}, f32[192,128]{1,0:T(8,128)S(1)}, u32[]{:S(2)}, u32[]{:S(2)}) collective-permute-start(f32[192,128]{1,0:T(8,128)S(1)} %add.91), channel_id=1, source_target_pairs={{0,1},{1,0},{2,3},{3,2},{4,5},{5,4},{6,7},{7,6},{8,9},{9,8},{10,11... | collective-permute-start | bytes 294920 | tf_op jit(solution)/shard_map/ppermute | solution.py:487
  28.4 33.1 %copy-start.1 = (f32[64,64]{1,0:T(8,128)S(1)}, f32[64,64]{1,0:T(8,128)}, u32[]{:S(2)}) copy-start(f32[64,64]{1,0:T(8,128)} %c_ref.1) | copy-start | bytes 49156
  28.4 4.3 %collective-permute-start.11 = (f32[192,128]{1,0:T(8,128)S(1)}, f32[192,128]{1,0:T(8,128)S(1)}, u32[]{:S(2)}, u32[]{:S(2)}) collective-permute-start(f32[192,128]{1,0:T(8,128)S(1)} %get-tuple-element.25), channel_id=1, source_target_pairs={{0,32},{32,0},{64,96},{96,64},{128,160},{160,128},{192,224},{224,1... | collective-permute-start | bytes 294920 | tf_op jit(solution)/shard_map/ppermute | solution.py:487
  28.6 9.0 %collective-permute-start.5 = (f32[192,128]{1,0:T(8,128)S(1)}, f32[192,128]{1,0:T(8,128)S(1)}, u32[]{:S(2)}, u32[]{:S(2)}) collective-permute-start(f32[192,128]{1,0:T(8,128)S(1)} %add.92), channel_id=1, source_target_pairs={{0,2},{1,3},{2,0},{3,1},{4,6},{5,7},{6,4},{7,5},{8,10},{9,11},{10,... | collective-permute-start | bytes 294920 | tf_op jit(solution)/shard_map/ppermute | solution.py:487
  32.8 19.8 %collective-permute-start.14 = (f32[192,128]{1,0:T(8,128)S(1)}, f32[192,128]{1,0:T(8,128)S(1)}, u32[]{:S(2)}, u32[]{:S(2)}) collective-permute-start(f32[192,128]{1,0:T(8,128)S(1)} %add.98), channel_id=1, source_target_pairs={{0,192},{32,224},{64,128},{96,160},{128,64},{160,96},{192,0},{224,... | collective-permute-start | bytes 294920 | tf_op jit(solution)/shard_map/ppermute | solution.py:487
  35.1 18.2 %collective-permute-start.13 = (f32[192,128]{1,0:T(8,128)S(1)}, f32[192,128]{1,0:T(8,128)S(1)}, u32[]{:S(2)}, u32[]{:S(2)}) collective-permute-start(f32[192,128]{1,0:T(8,128)S(1)} %add.98), channel_id=1, source_target_pairs={{0,128},{32,160},{64,192},{96,224},{128,0},{160,32},{192,64},{224,... | collective-permute-start | bytes 294920 | tf_op jit(solution)/shard_map/ppermute | solution.py:487
  36.0 17.3 %collective-permute-start.12 = (f32[192,128]{1,0:T(8,128)S(1)}, f32[192,128]{1,0:T(8,128)S(1)}, u32[]{:S(2)}, u32[]{:S(2)}) collective-permute-start(f32[192,128]{1,0:T(8,128)S(1)} %add.98), channel_id=1, source_target_pairs={{0,64},{32,96},{64,0},{96,32},{128,192},{160,224},{192,128},{224,1... | collective-permute-start | bytes 294920 | tf_op jit(solution)/shard_map/ppermute | solution.py:487
  37.6 9.2 %collective-permute-start.6 = (f32[192,128]{1,0:T(8,128)S(1)}, f32[192,128]{1,0:T(8,128)S(1)}, u32[]{:S(2)}, u32[]{:S(2)}) collective-permute-start(f32[192,128]{1,0:T(8,128)S(1)} %add.93), channel_id=1, source_target_pairs={{0,4},{1,5},{2,6},{3,7},{4,0},{5,1},{6,2},{7,3},{8,12},{9,13},{10,... | collective-permute-start | bytes 294920 | tf_op jit(solution)/shard_map/ppermute | solution.py:487
  46.8 8.5 %collective-permute-start.9 = (f32[192,128]{1,0:T(8,128)S(1)}, f32[192,128]{1,0:T(8,128)S(1)}, u32[]{:S(2)}, u32[]{:S(2)}) collective-permute-start(f32[192,128]{1,0:T(8,128)S(1)} %add.94), channel_id=1, source_target_pairs={{0,24},{1,25},{2,26},{3,27},{4,28},{5,29},{6,30},{7,31},{8,16},{9,... | collective-permute-start | bytes 294920 | tf_op jit(solution)/shard_map/ppermute | solution.py:487
  52.6 5.0 %collective-permute-start.8 = (f32[192,128]{1,0:T(8,128)S(1)}, f32[192,128]{1,0:T(8,128)S(1)}, u32[]{:S(2)}, u32[]{:S(2)}) collective-permute-start(f32[192,128]{1,0:T(8,128)S(1)} %add.94), channel_id=1, source_target_pairs={{0,16},{1,17},{2,18},{3,19},{4,20},{5,21},{6,22},{7,23},{8,24},{9,... | collective-permute-start | bytes 294920 | tf_op jit(solution)/shard_map/ppermute | solution.py:487
  52.6 5.0 %collective-permute-start.7 = (f32[192,128]{1,0:T(8,128)S(1)}, f32[192,128]{1,0:T(8,128)S(1)}, u32[]{:S(2)}, u32[]{:S(2)}) collective-permute-start(f32[192,128]{1,0:T(8,128)S(1)} %add.94), channel_id=1, source_target_pairs={{0,8},{1,9},{2,10},{3,11},{4,12},{5,13},{6,14},{7,15},{8,0},{9,1},... | collective-permute-start | bytes 294920 | tf_op jit(solution)/shard_map/ppermute | solution.py:487
  53.3 7.9 %collective-permute-start.15 = (f32[192,128]{1,0:T(8,128)S(1)}, f32[192,128]{1,0:T(8,128)S(1)}, u32[]{:S(2)}, u32[]{:S(2)}) collective-permute-start(f32[192,128]{1,0:T(8,128)S(1)} %add_add_fusion.gu_mine), channel_id=1, source_target_pairs={{0,32},{32,0},{64,96},{96,64},{128,160},{160,128},{192,224},{224,1... | collective-permute-start | bytes 294920 | tf_op jit(solution)/shard_map/ppermute | solution.py:487
  57.6 4.0 %collective-permute-start.10 = (f32[192,128]{1,0:T(8,128)S(1)}, f32[192,128]{1,0:T(8,128)S(1)}, u32[]{:S(2)}, u32[]{:S(2)}) collective-permute-start(f32[192,128]{1,0:T(8,128)S(1)} %add_add_fusion.1.gv_mine), channel_id=1, source_target_pairs={{0,32},{32,0},{64,96},{96,64},{128,160},{160,128},{192,224},{224,1... | collective-permute-start | bytes 294920 | tf_op jit(solution)/shard_map/ppermute | solution.py:487
  78.8 6.3 %collective-permute-start.16 = (f32[64,4096]{1,0:T(8,128)S(1)}, f32[64,4096]{1,0:T(8,128)S(1)}, u32[]{:S(2)}, u32[]{:S(2)}) collective-permute-start(f32[64,4096]{1,0:T(8,128)S(1)} %shard_map.114), channel_id=1, source_target_pairs={{0,32},{32,0},{64,96},{96,64},{128,160},{160,128},{192,224},{224,1... | collective-permute-start | bytes 3145736 | tf_op jit(solution)/shard_map/ppermute | solution.py:487

commit v4 on v3

--- a/solution.py
+++ b/solution.py
@@ -18,7 +18,7 @@
 BF16 = jnp.bfloat16
 NT = (((1,), (1,)), ((), ()))
 NN = (((1,), (0,)), ((), ()))
-VMEM_LIMIT = 14 * 1024 * 1024
+VMEM_LIMIT = 16 * 1024 * 1024
 
 
 def smem():
@@ -150,7 +150,7 @@
 def gram_v(core, offsets, v, halo, weights, scale):
     cells = v.shape[1]
     half = cells // 2
-    tile = min(1024, half)
+    tile = min(2048, half)
     steps = half // tile
     ratio = tile // LANES
     last = cells // LANES - 1
@@ -392,7 +392,7 @@
 
 def next_factor(maps, wide_hi, wide_lo):
     cells = wide_hi.shape[1]
-    tile = min(1024, cells)
+    tile = min(2048, cells)
     return pl.pallas_call(
         next_kernel,
         grid=(cells // tile,),
@@ -440,7 +440,7 @@
 
 def next_u(u, left, right, mass, diffusion, maps):
     cells = u.shape[1]
-    tile = min(1024, cells)
+    tile = min(2048, cells)
     steps = cells // tile
     ratio = tile // LANES
     last = cells // LANES - 1

time: 87 us -> 85.8 us (0.986)
  Pallas kernels: 36.5 us -> 35.5 us
where the time goes in v4:
time: 85.8 us; the launch traced here: 85.5 us
  Pallas kernels  35.5 us (41%)
  starting transfers between devices  34.4 us (40%)
  waiting for transfers between devices  9.28 us (11%)
  other arithmetic  4.93 us (6%)
  between operations  1.46 us (2%)
    ppermute x15, starting transfers between devices, swap(): lax.ppermute(x, axis, [(i, i ^ bit) for i in range(lax.axis_size(axis))])  29.5 us
    pallas_call x1, Pallas kernels, chain(): pl.pallas_call(chain_kernel, in_specs=[smem()] + [vmem()] * 6, out_specs=...  15.6 us
    pallas_call x1, Pallas kernels, gram_v(): pl.pallas_call(functools.partial(gram_v_kernel, steps, scale), grid_spec=...  7.73 us
    ppermute x15, waiting for transfers between devices, swap(): lax.ppermute(x, axis, [(i, i ^ bit) for i in range(lax.axis_size(axis))])  6.77 us
    pallas_call x2, Pallas kernels, gram_u(): pl.pallas_call(functools.partial(gram_u_kernel, part_at, parts, steps, sc...  5.77 us
    pallas_call x1, Pallas kernels, next_u(): pl.pallas_call(functools.partial(next_u_kernel, steps), grid=(steps,), in...  5.04 us
    ppermute x1, starting transfers between devices, body(): lax.ppermute(jnp.where(even, u[:, :LANES], u[:, -LANES:]), 'gx', [(i, j)...  3.57 us
    ppermute x1, waiting for transfers between devices, body(): halo_v = lax.ppermute(edge_v, ('gx', 'pa'), pairs)  2.5 us
  transfers between devices with their start and end apart: 17, of which 5 were waited for; matrix products, arithmetic and copies ran while one was open for 3% of the time, Pallas kernels for 13%

profile of v4, /device:TPU:1, one launch (start us, length us, event | category | flops | bytes accessed | tf_op | source)
XLA Modules:
  0.0 85.5 jit_solution(7372890590588358068)
XLA Ops:
  0.6 0.8 slice_select_fusion
  1.4 1.3 %collective-permute-start.2 = (f32[64,128]{1,0:T(8,128)S(1)}, f32[64,128]{1,0:T(8,128)S(1)}, u32[]{:S(2)}, u32[]{:S(2)}) collective-permute-start(f32[64,128]{1,0:T(8,128)S(1)} %slice_select_fusion), channel_id=1, source_target_pairs={{0,1},{1,2},{2,3},{3,4},{4,5},{5,6},{6,7},{7,8},{8,9},{9,10},{10,1... | collective-permute-start | bytes 98312 | tf_op jit(solution)/shard_map/ppermute | solution.py:507
  2.7 1.9 %select_reduce_fusion = (f32[4,8192]{1,0:T(4,128)S(1)}, f32[4,8192]{1,0:T(4,128)S(1)}) fusion(f32[4,16]{1,0:T(4,128)} %param.12, s32[4,8192]{1,0:T(4,128)} %param.13, f32[4,16]{1,0:T(4,128)} %param.11), kind=kLoop, calls=%fused_computation.1 | loop fusion | flops 2555904 | bytes 393728 | tf_op jit(solution)/shard_map/reduce_sum | solution.py:510
  4.6 2.5 %collective-permute-done.2.halo_ref = f32[64,128]{1,0:T(8,128)S(1)} collective-permute-done((f32[64,128]{1,0:T(8,128)S(1)}, f32[64,128]{1,0:T(8,128)S(1)}, u32[]{:S(2)}, u32[]{:S(2)}) %collective-permute-start.2) | collective-permute-done | bytes 32800 | tf_op jit(solution)/shard_map/ppermute | solution.py:507
  7.1 0.0 copy-start
  7.1 7.7 %gram_v.1 = (f32[192,128]{1,0:T(8,128)S(1)}, f32[192,128]{1,0:T(8,128)S(1)}, bf16[256,4096]{1,0:T(8,128)(2,1)S(1)}, bf16[256,4096]{1,0:T(8,128)(2,1)S(1)}) custom-call(s32[1]{0:T(128)} %bitcast.core_ref, s32[4,3]{1,0:T(4,128)} %off_ref.1, f32[64,8192]{1,0:T(8,128)} %after_ref.4, f32[64,8192]{1,0:T(8,128)} %after_ref.4, f32[64,8192]{1,0:T(8,128)} %after_ref.4, ...), custom_call_target="tpu_custom_call" | custom-call | tf_op jit(solution)/shard_map/gram_v/pallas_call | solution.py:170
  14.8 1.7 %collective-permute-start.3 = (f32[192,128]{1,0:T(8,128)S(1)}, f32[192,128]{1,0:T(8,128)S(1)}, u32[]{:S(2)}, u32[]{:S(2)}) collective-permute-start(f32[192,128]{1,0:T(8,128)S(1)} %get-tuple-element.21), channel_id=1, source_target_pairs={{0,32},{32,0},{64,96},{96,64},{128,160},{160,128},{192,224},{224,1... | collective-permute-start | bytes 294920 | tf_op jit(solution)/shard_map/ppermute | solution.py:487
  16.5 0.0 copy-done
  16.5 0.1 collective-permute-start.1
  16.6 3.6 %collective-permute-start = (f32[64,128]{1,0:T(8,128)S(1)}, f32[64,128]{1,0:T(8,128)S(1)}, u32[]{:S(2)}, u32[]{:S(2)}) collective-permute-start(f32[64,128]{1,0:T(8,128)S(1)} %get-tuple-element.36), channel_id=1, source_target_pairs={{32,64},{64,32},{96,128},{128,96},{160,192},{192,160},{33,65},{65,... | collective-permute-start | bytes 98312 | tf_op jit(solution)/shard_map/ppermute | solution.py:513
  20.8 0.0 collective-permute-done.3
  20.9 1.8 %collective-permute-start.4 = (f32[192,128]{1,0:T(8,128)S(1)}, f32[192,128]{1,0:T(8,128)S(1)}, u32[]{:S(2)}, u32[]{:S(2)}) collective-permute-start(f32[192,128]{1,0:T(8,128)S(1)} %add.91), channel_id=1, source_target_pairs={{0,1},{1,0},{2,3},{3,2},{4,5},{5,4},{6,7},{7,6},{8,9},{9,8},{10,11... | collective-permute-start | bytes 294920 | tf_op jit(solution)/shard_map/ppermute | solution.py:487
  22.7 0.0 collective-permute-done.1
  22.7 0.0 collective-permute-done
  22.7 2.9 %shard_map.112 = (f32[192,128]{1,0:T(8,128)S(1)}, f32[192,128]{1,0:T(8,128)S(1)}) custom-call(s32[1]{0:T(128)} %bitcast.core_ref, f32[64,8192]{1,0:T(8,128)S(1)} %copy-done, f32[64,8192]{1,0:T(8,128)S(1)} %copy-done, f32[64,8192]{1,0:T(8,128)S(1)} %copy-done, f32[64,128]{1,0:T(8,128)S(1)} %get-tuple-element.38.left_ref, ...), custom_call_target="tpu_custom_call" | custom-call | tf_op jit(solution)/shard_map/pallas_call | solution.py:247
  25.6 2.9 %shard_map.113 = (f32[192,128]{1,0:T(8,128)S(1)}, f32[192,128]{1,0:T(8,128)S(1)}) custom-call(s32[1]{0:T(128)} %bitcast.core_ref, f32[64,8192]{1,0:T(8,128)S(1)} %copy-done, f32[64,8192]{1,0:T(8,128)S(1)} %copy-done, f32[64,8192]{1,0:T(8,128)S(1)} %copy-done, f32[64,128]{1,0:T(8,128)S(1)} %get-tuple-element.38.left_ref, ...), custom_call_target="tpu_custom_call" | custom-call | tf_op jit(solution)/shard_map/pallas_call | solution.py:247
  28.5 0.0 copy-start.1
  28.5 0.1 collective-permute-start.11
  28.6 0.0 collective-permute-done.4
  28.6 4.2 %collective-permute-start.5 = (f32[192,128]{1,0:T(8,128)S(1)}, f32[192,128]{1,0:T(8,128)S(1)}, u32[]{:S(2)}, u32[]{:S(2)}) collective-permute-start(f32[192,128]{1,0:T(8,128)S(1)} %add.92), channel_id=1, source_target_pairs={{0,2},{1,3},{2,0},{3,1},{4,6},{5,7},{6,4},{7,5},{8,10},{9,11},{10,... | collective-permute-start | bytes 294920 | tf_op jit(solution)/shard_map/ppermute | solution.py:487
  32.8 0.0 collective-permute-done.11
  32.8 2.3 %collective-permute-start.14 = (f32[192,128]{1,0:T(8,128)S(1)}, f32[192,128]{1,0:T(8,128)S(1)}, u32[]{:S(2)}, u32[]{:S(2)}) collective-permute-start(f32[192,128]{1,0:T(8,128)S(1)} %add.98), channel_id=1, source_target_pairs={{0,192},{32,224},{64,128},{96,160},{128,64},{160,96},{192,0},{224,... | collective-permute-start | bytes 294920 | tf_op jit(solution)/shard_map/ppermute | solution.py:487
  35.1 0.9 %collective-permute-start.13 = (f32[192,128]{1,0:T(8,128)S(1)}, f32[192,128]{1,0:T(8,128)S(1)}, u32[]{:S(2)}, u32[]{:S(2)}) collective-permute-start(f32[192,128]{1,0:T(8,128)S(1)} %add.98), channel_id=1, source_target_pairs={{0,128},{32,160},{64,192},{96,224},{128,0},{160,32},{192,64},{224,... | collective-permute-start | bytes 294920 | tf_op jit(solution)/shard_map/ppermute | solution.py:487
  36.0 0.2 collective-permute-start.12
  36.2 1.4 %collective-permute-done.5 = f32[192,128]{1,0:T(8,128)S(1)} collective-permute-done((f32[192,128]{1,0:T(8,128)S(1)}, f32[192,128]{1,0:T(8,128)S(1)}, u32[]{:S(2)}, u32[]{:S(2)}) %collective-permute-start.5) | collective-permute-done | bytes 98336 | tf_op jit(solution)/shard_map/ppermute | solution.py:487
  37.6 6.5 %collective-permute-start.6 = (f32[192,128]{1,0:T(8,128)S(1)}, f32[192,128]{1,0:T(8,128)S(1)}, u32[]{:S(2)}, u32[]{:S(2)}) collective-permute-start(f32[192,128]{1,0:T(8,128)S(1)} %add.93), channel_id=1, source_target_pairs={{0,4},{1,5},{2,6},{3,7},{4,0},{5,1},{6,2},{7,3},{8,12},{9,13},{10,... | collective-permute-start | bytes 294920 | tf_op jit(solution)/shard_map/ppermute | solution.py:487
  44.2 2.7 %collective-permute-done.6 = f32[192,128]{1,0:T(8,128)S(1)} collective-permute-done((f32[192,128]{1,0:T(8,128)S(1)}, f32[192,128]{1,0:T(8,128)S(1)}, u32[]{:S(2)}, u32[]{:S(2)}) %collective-permute-start.6) | collective-permute-done | bytes 98336 | tf_op jit(solution)/shard_map/ppermute | solution.py:487
  46.9 5.7 %collective-permute-start.9 = (f32[192,128]{1,0:T(8,128)S(1)}, f32[192,128]{1,0:T(8,128)S(1)}, u32[]{:S(2)}, u32[]{:S(2)}) collective-permute-start(f32[192,128]{1,0:T(8,128)S(1)} %add.94), channel_id=1, source_target_pairs={{0,24},{1,25},{2,26},{3,27},{4,28},{5,29},{6,30},{7,31},{8,16},{9,... | collective-permute-start | bytes 294920 | tf_op jit(solution)/shard_map/ppermute | solution.py:487
  52.6 0.0 collective-permute-start.8
  52.6 0.0 collective-permute-done.14
  52.6 0.7 collective-permute-start.7
  53.3 0.0 collective-permute-done.13
  53.3 0.0 collective-permute-done.12
  53.3 2.0 %collective-permute-start.15 = (f32[192,128]{1,0:T(8,128)S(1)}, f32[192,128]{1,0:T(8,128)S(1)}, u32[]{:S(2)}, u32[]{:S(2)}) collective-permute-start(f32[192,128]{1,0:T(8,128)S(1)} %add_add_fusion.gu_mine), channel_id=1, source_target_pairs={{0,32},{32,0},{64,96},{96,64},{128,160},{160,128},{192,224},{224,1... | collective-permute-start | bytes 294920 | tf_op jit(solution)/shard_map/ppermute | solution.py:487
  55.3 0.0 collective-permute-done.9
  55.4 2.2 %collective-permute-done.8 = f32[192,128]{1,0:T(8,128)S(1)} collective-permute-done((f32[192,128]{1,0:T(8,128)S(1)}, f32[192,128]{1,0:T(8,128)S(1)}, u32[]{:S(2)}, u32[]{:S(2)}) %collective-permute-start.8) | collective-permute-done | bytes 98336 | tf_op jit(solution)/shard_map/ppermute | solution.py:487
  57.6 0.0 collective-permute-done.7
  57.6 2.9 %collective-permute-start.10 = (f32[192,128]{1,0:T(8,128)S(1)}, f32[192,128]{1,0:T(8,128)S(1)}, u32[]{:S(2)}, u32[]{:S(2)}) collective-permute-start(f32[192,128]{1,0:T(8,128)S(1)} %add_add_fusion.1.gv_mine), channel_id=1, source_target_pairs={{0,32},{32,0},{64,96},{96,64},{128,160},{160,128},{192,224},{224,1... | collective-permute-start | bytes 294920 | tf_op jit(solution)/shard_map/ppermute | solution.py:487
  60.5 0.5 fusion.10.sketch_ref
  61.0 0.0 collective-permute-done.15.gu_other
  61.0 0.4 collective-permute-done.10.gv_other
  61.4 0.0 copy-done.1
  61.4 15.6 %chain.1 = (bf16[256,192]{1,0:T(8,128)(2,1)S(1)}, bf16[128,256]{1,0:T(8,128)(2,1)S(1)}, f32[64,64]{1,0:T(8,128)}) custom-call(s32[1]{0:T(128)} %bitcast.core_ref, f32[192,128]{1,0:T(8,128)S(1)} %add_add_fusion.1.gv_mine, f32[192,128]{1,0:T(8,128)S(1)} %collective-permute-done.10.gv_other, f32[192,128]{1,0:T(8,128)S(1)} %add_add_fusion.gu_mine, ...), custom_call_target="tpu_custom_call" | custom-call | tf_op jit(solution)/shard_map/chain/pallas_call | solution.py:369
  77.1 1.3 %shard_map.114 = f32[64,4096]{1,0:T(8,128)S(1)} custom-call(bf16[128,256]{1,0:T(8,128)(2,1)S(1)} %get-tuple-element.27.map_ref, bf16[256,4096]{1,0:T(8,128)(2,1)S(1)} %get-tuple-element.28.hi_ref, bf16[256,4096]{1,0:T(8,128)(2,1)S(1)} %get-tuple-element.29.lo_ref), custom_call_target="tpu_custom_call" | custom-call | tf_op jit(solution)/shard_map/pallas_call | solution.py:396
  78.4 0.5 collective-permute-start.16
  78.8 5.0 %next_u.1 = f32[64,8192]{1,0:T(8,128)} custom-call(f32[64,8192]{1,0:T(8,128)S(1)} %copy-done, f32[64,8192]{1,0:T(8,128)S(1)} %copy-done, f32[64,8192]{1,0:T(8,128)S(1)} %copy-done, f32[64,128]{1,0:T(8,128)S(1)} %get-tuple-element.38.left_ref, f32[64,128]{1,0:T(8,128)S(1)} %get-tuple-element.37.right_ref, f32[4,8192]{1,0:T(4,128)S(1)} %get-tuple-element.17.m_ref, ...), custom_call_target="tpu_custom_call" | custom-call | tf_op jit(solution)/shard_map/next_u/pallas_call | solution.py:450
  83.9 0.0 collective-permute-done.16
  83.9 0.2 broadcast_select_fusion.1
  84.1 1.5 %pad_maximum_fusion = f32[64,8192]{1,0:T(8,128)} fusion(f32[64,4096]{1,0:T(8,128)S(1)} %get-tuple-element.34, f32[64,4096]{1,0:T(8,128)S(1)} %get-tuple-element.33), kind=kLoop, calls=%fused_computation | loop fusion | flops 524288 | bytes 4194304 | tf_op jit(solution)/shard_map/concatenate | solution.py:539
  (11 shorter events, 0.1 us)
Async XLA Ops:
  1.4 5.6 %collective-permute-start.2 = (f32[64,128]{1,0:T(8,128)S(1)}, f32[64,128]{1,0:T(8,128)S(1)}, u32[]{:S(2)}, u32[]{:S(2)}) collective-permute-start(f32[64,128]{1,0:T(8,128)S(1)} %slice_select_fusion), channel_id=1, source_target_pairs={{0,1},{1,2},{2,3},{3,4},{4,5},{5,6},{6,7},{7,8},{8,9},{9,10},{10,1... | collective-permute-start | bytes 98312 | tf_op jit(solution)/shard_map/ppermute | solution.py:507
  7.1 9.4 %copy-start = (f32[64,8192]{1,0:T(8,128)S(1)}, f32[64,8192]{1,0:T(8,128)}, u32[]{:S(2)}) copy-start(f32[64,8192]{1,0:T(8,128)} %after_ref.7) | copy-start | bytes 6291460
  14.8 6.0 %collective-permute-start.3 = (f32[192,128]{1,0:T(8,128)S(1)}, f32[192,128]{1,0:T(8,128)S(1)}, u32[]{:S(2)}, u32[]{:S(2)}) collective-permute-start(f32[192,128]{1,0:T(8,128)S(1)} %get-tuple-element.21), channel_id=1, source_target_pairs={{0,32},{32,0},{64,96},{96,64},{128,160},{160,128},{192,224},{224,1... | collective-permute-start | bytes 294920 | tf_op jit(solution)/shard_map/ppermute | solution.py:487
  16.5 6.2 %collective-permute-start.1 = (f32[64,128]{1,0:T(8,128)S(1)}, f32[64,128]{1,0:T(8,128)S(1)}, u32[]{:S(2)}, u32[]{:S(2)}) collective-permute-start(f32[64,128]{1,0:T(8,128)S(1)} %get-tuple-element.35), channel_id=1, source_target_pairs={{0,32},{32,0},{64,96},{96,64},{128,160},{160,128},{192,224},{224,1... | collective-permute-start | bytes 98312 | tf_op jit(solution)/shard_map/ppermute | solution.py:487
  16.6 6.1 %collective-permute-start = (f32[64,128]{1,0:T(8,128)S(1)}, f32[64,128]{1,0:T(8,128)S(1)}, u32[]{:S(2)}, u32[]{:S(2)}) collective-permute-start(f32[64,128]{1,0:T(8,128)S(1)} %get-tuple-element.36), channel_id=1, source_target_pairs={{32,64},{64,32},{96,128},{128,96},{160,192},{192,160},{33,65},{65,... | collective-permute-start | bytes 98312 | tf_op jit(solution)/shard_map/ppermute | solution.py:513
  20.9 7.7 %collective-permute-start.4 = (f32[192,128]{1,0:T(8,128)S(1)}, f32[192,128]{1,0:T(8,128)S(1)}, u32[]{:S(2)}, u32[]{:S(2)}) collective-permute-start(f32[192,128]{1,0:T(8,128)S(1)} %add.91), channel_id=1, source_target_pairs={{0,1},{1,0},{2,3},{3,2},{4,5},{5,4},{6,7},{7,6},{8,9},{9,8},{10,11... | collective-permute-start | bytes 294920 | tf_op jit(solution)/shard_map/ppermute | solution.py:487
  28.5 33.0 %copy-start.1 = (f32[64,64]{1,0:T(8,128)S(1)}, f32[64,64]{1,0:T(8,128)}, u32[]{:S(2)}) copy-start(f32[64,64]{1,0:T(8,128)} %c_ref.1) | copy-start | bytes 49156
  28.5 4.3 %collective-permute-start.11 = (f32[192,128]{1,0:T(8,128)S(1)}, f32[192,128]{1,0:T(8,128)S(1)}, u32[]{:S(2)}, u32[]{:S(2)}) collective-permute-start(f32[192,128]{1,0:T(8,128)S(1)} %get-tuple-element.25), channel_id=1, source_target_pairs={{0,32},{32,0},{64,96},{96,64},{128,160},{160,128},{192,224},{224,1... | collective-permute-start | bytes 294920 | tf_op jit(solution)/shard_map/ppermute | solution.py:487
  28.6 9.0 %collective-permute-start.5 = (f32[192,128]{1,0:T(8,128)S(1)}, f32[192,128]{1,0:T(8,128)S(1)}, u32[]{:S(2)}, u32[]{:S(2)}) collective-permute-start(f32[192,128]{1,0:T(8,128)S(1)} %add.92), channel_id=1, source_target_pairs={{0,2},{1,3},{2,0},{3,1},{4,6},{5,7},{6,4},{7,5},{8,10},{9,11},{10,... | collective-permute-start | bytes 294920 | tf_op jit(solution)/shard_map/ppermute | solution.py:487
  32.8 19.8 %collective-permute-start.14 = (f32[192,128]{1,0:T(8,128)S(1)}, f32[192,128]{1,0:T(8,128)S(1)}, u32[]{:S(2)}, u32[]{:S(2)}) collective-permute-start(f32[192,128]{1,0:T(8,128)S(1)} %add.98), channel_id=1, source_target_pairs={{0,192},{32,224},{64,128},{96,160},{128,64},{160,96},{192,0},{224,... | collective-permute-start | bytes 294920 | tf_op jit(solution)/shard_map/ppermute | solution.py:487
  35.1 18.2 %collective-permute-start.13 = (f32[192,128]{1,0:T(8,128)S(1)}, f32[192,128]{1,0:T(8,128)S(1)}, u32[]{:S(2)}, u32[]{:S(2)}) collective-permute-start(f32[192,128]{1,0:T(8,128)S(1)} %add.98), channel_id=1, source_target_pairs={{0,128},{32,160},{64,192},{96,224},{128,0},{160,32},{192,64},{224,... | collective-permute-start | bytes 294920 | tf_op jit(solution)/shard_map/ppermute | solution.py:487
  36.0 17.3 %collective-permute-start.12 = (f32[192,128]{1,0:T(8,128)S(1)}, f32[192,128]{1,0:T(8,128)S(1)}, u32[]{:S(2)}, u32[]{:S(2)}) collective-permute-start(f32[192,128]{1,0:T(8,128)S(1)} %add.98), channel_id=1, source_target_pairs={{0,64},{32,96},{64,0},{96,32},{128,192},{160,224},{192,128},{224,1... | collective-permute-start | bytes 294920 | tf_op jit(solution)/shard_map/ppermute | solution.py:487
  37.6 9.2 %collective-permute-start.6 = (f32[192,128]{1,0:T(8,128)S(1)}, f32[192,128]{1,0:T(8,128)S(1)}, u32[]{:S(2)}, u32[]{:S(2)}) collective-permute-start(f32[192,128]{1,0:T(8,128)S(1)} %add.93), channel_id=1, source_target_pairs={{0,4},{1,5},{2,6},{3,7},{4,0},{5,1},{6,2},{7,3},{8,12},{9,13},{10,... | collective-permute-start | bytes 294920 | tf_op jit(solution)/shard_map/ppermute | solution.py:487
  46.9 8.5 %collective-permute-start.9 = (f32[192,128]{1,0:T(8,128)S(1)}, f32[192,128]{1,0:T(8,128)S(1)}, u32[]{:S(2)}, u32[]{:S(2)}) collective-permute-start(f32[192,128]{1,0:T(8,128)S(1)} %add.94), channel_id=1, source_target_pairs={{0,24},{1,25},{2,26},{3,27},{4,28},{5,29},{6,30},{7,31},{8,16},{9,... | collective-permute-start | bytes 294920 | tf_op jit(solution)/shard_map/ppermute | solution.py:487
  52.6 5.0 %collective-permute-start.8 = (f32[192,128]{1,0:T(8,128)S(1)}, f32[192,128]{1,0:T(8,128)S(1)}, u32[]{:S(2)}, u32[]{:S(2)}) collective-permute-start(f32[192,128]{1,0:T(8,128)S(1)} %add.94), channel_id=1, source_target_pairs={{0,16},{1,17},{2,18},{3,19},{4,20},{5,21},{6,22},{7,23},{8,24},{9,... | collective-permute-start | bytes 294920 | tf_op jit(solution)/shard_map/ppermute | solution.py:487
  52.6 5.0 %collective-permute-start.7 = (f32[192,128]{1,0:T(8,128)S(1)}, f32[192,128]{1,0:T(8,128)S(1)}, u32[]{:S(2)}, u32[]{:S(2)}) collective-permute-start(f32[192,128]{1,0:T(8,128)S(1)} %add.94), channel_id=1, source_target_pairs={{0,8},{1,9},{2,10},{3,11},{4,12},{5,13},{6,14},{7,15},{8,0},{9,1},... | collective-permute-start | bytes 294920 | tf_op jit(solution)/shard_map/ppermute | solution.py:487
  53.3 7.7 %collective-permute-start.15 = (f32[192,128]{1,0:T(8,128)S(1)}, f32[192,128]{1,0:T(8,128)S(1)}, u32[]{:S(2)}, u32[]{:S(2)}) collective-permute-start(f32[192,128]{1,0:T(8,128)S(1)} %add_add_fusion.gu_mine), channel_id=1, source_target_pairs={{0,32},{32,0},{64,96},{96,64},{128,160},{160,128},{192,224},{224,1... | collective-permute-start | bytes 294920 | tf_op jit(solution)/shard_map/ppermute | solution.py:487
  57.6 3.8 %collective-permute-start.10 = (f32[192,128]{1,0:T(8,128)S(1)}, f32[192,128]{1,0:T(8,128)S(1)}, u32[]{:S(2)}, u32[]{:S(2)}) collective-permute-start(f32[192,128]{1,0:T(8,128)S(1)} %add_add_fusion.1.gv_mine), channel_id=1, source_target_pairs={{0,32},{32,0},{64,96},{96,64},{128,160},{160,128},{192,224},{224,1... | collective-permute-start | bytes 294920 | tf_op jit(solution)/shard_map/ppermute | solution.py:487
  78.4 5.5 %collective-permute-start.16 = (f32[64,4096]{1,0:T(8,128)S(1)}, f32[64,4096]{1,0:T(8,128)S(1)}, u32[]{:S(2)}, u32[]{:S(2)}) collective-permute-start(f32[64,4096]{1,0:T(8,128)S(1)} %shard_map.114), channel_id=1, source_target_pairs={{0,32},{32,0},{64,96},{96,64},{128,160},{160,128},{192,224},{224,1... | collective-permute-start | bytes 3145736 | tf_op jit(solution)/shard_map/ppermute | solution.py:487
